TPU v7x, 256 devices: a whole 4x4x8 slice. The times are simulated.
256 devices in a mesh: gx: 64 (over y, z, core), gy: 4 (over x).
Axes of the slice: x: 4, y: 4, z: 8, core: 2. Of those that a mesh axis runs over, the one named last changes fastest.
Arguments:
- members_state: float32 [3, 64, 512, 512], P(None, None, 'gx', 'gy'), may hold values from -6 to 6
- depth_level: int32 [512, 512], P('gx', 'gy'), may hold values from 1 to 8
- land_mask: int32 [512, 512], P('gx', 'gy'), may hold values 0 or 1
- obs_cells: int32 [64, 4, 256], P('gx', 'gy'), may hold values from 0 to 1023
- obs_values: float32 [64, 4, 256], P('gx', 'gy'), may hold values from -6 to 6
- obs_error: float32 [64, 4, 256], P('gx', 'gy'), may hold values from 2 to 8
Outputs:
- analysis: float32 [3, 64, 512, 512], P(None, None, 'gx', 'gy')
Inputs may be any that keep to these rules, and one draw needn't show every extreme that they name: Each value of obs_cells is the row-major index of a cell within the 8 x 128 block held by the device at the same position along gx and gy.
All inputs are finite; a program needn't handle non-finite values. No bound on the sum of `land_mask` on one device may be relied on, other than what follows from the above.
Results may differ from a plain program's by a relative error of at most 0.00005.
Values sent between devices are 32-bit elements; how exact they have to be, the bound alone decides.
No kernel may reach another device: no remote copies, remote signals or barrier semaphores. Data moves between devices by JAX's collectives and lax.ppermute only.
A program may use at most 64 MiB of HBM per device.

v0:
```python
import jax
import jax.numpy as jnp
from jax import lax
from jax.sharding import PartitionSpec as P


def extended(block, sides, width):
    for axis, dim in sides:
        count = lax.axis_size(axis)
        forward = [(i, i + 1) for i in range(count - 1)]
        backward = [(target, source) for source, target in forward]
        low = lax.ppermute(
            lax.slice_in_dim(block, block.shape[dim] - width, None, axis=dim), axis, forward
        )
        high = lax.ppermute(lax.slice_in_dim(block, 0, width, axis=dim), axis, backward)
        block = jnp.concatenate([low, block, high], axis=dim)
    return block


def height_tendency(padded, geo):
    h = padded[0]
    u = padded[1]
    v = padded[2]
    depth = geo[0]
    mask = geo[1][1:-1, 1:-1]
    east = depth * u
    north = depth * v

    def along_x(a):
        return (a[:, 2:, 1:-1] - a[:, :-2, 1:-1]) * 0.5

    def along_y(a):
        return (a[:, 1:-1, 2:] - a[:, 1:-1, :-2]) * 0.5

    def laplace(a):
        return (
            a[:, 2:, 1:-1]
            + a[:, :-2, 1:-1]
            + a[:, 1:-1, 2:]
            + a[:, 1:-1, :-2]
            - 4.0 * a[:, 1:-1, 1:-1]
        )

    def inner(a):
        return a[:, 1:-1, 1:-1]

    dh = -along_x(east) - along_y(north) + 0.05 * laplace(h)
    du = -along_x(h) + 0.2 * inner(v) + 0.05 * laplace(u)
    dv = -along_y(h) - 0.2 * inner(u) + 0.05 * laplace(v)
    return jnp.stack([dh, du, dv]) * mask


def tri_solve(lower, rhs, flipped):
    return lax.linalg.triangular_solve(lower, rhs, left_side=True, lower=True, transpose_a=flipped)


def padded_section(field):
    return extended(field, (("gx", 2), ("gy", 3)), 1)


def local(members_state, depth_level, land_mask, obs_cells, obs_values, obs_error):
    maskf = land_mask.astype(jnp.float32)
    geo = jnp.stack([0.25 * depth_level.astype(jnp.float32) * maskf, maskf])
    geo_wide = extended(geo, (("gx", 1), ("gy", 2)), 3)
    first_offset = members_state * maskf
    single_geometry = geo_wide[:, 2:-2, 2:-2]
    s1 = first_offset + 0.3 * height_tendency(padded_section(first_offset), single_geometry)
    variance_estimate2 = 0.75 * first_offset + 0.25 * (
        s1 + 0.3 * height_tendency(padded_section(s1), single_geometry)
    )
    prior_model_vector = 1.0 / 3.0 * first_offset + 2.0 / 3.0 * (
        variance_estimate2
        + 0.3 * height_tendency(padded_section(variance_estimate2), single_geometry)
    )
    sample_average = jnp.mean(prior_model_vector, axis=1, keepdims=True)
    sample_deviations = prior_model_vector - sample_average
    sample_number = prior_model_vector.shape[1]
    free_elevation_field = prior_model_vector[0].reshape(sample_number, -1)
    measured_data = jnp.take(free_elevation_field, obs_cells.reshape(-1), axis=1)
    obs_mean = jnp.mean(measured_data, axis=0, keepdims=True)
    error = obs_error.reshape(-1)
    scaled = (measured_data - obs_mean) / (error * jnp.sqrt(jnp.float32(sample_number - 1)))
    innovation = (obs_values.reshape(-1) - obs_mean[0]) / error
    gram_part = jnp.dot(scaled, scaled.T, precision=lax.Precision.HIGHEST)
    proj_part = jnp.dot(scaled, innovation, precision=lax.Precision.HIGHEST)
    eye = jnp.eye(sample_number, dtype=jnp.float32)
    gram, projection = lax.psum((gram_part, proj_part), ("gx", "gy"))
    lower = jnp.linalg.cholesky(eye + gram)
    half = tri_solve(lower, projection[:, None], False)
    weights = tri_solve(lower, half, True)[:, 0]
    inverse = tri_solve(lower, eye, False)
    transform = weights[:, None] / jnp.sqrt(jnp.float32(sample_number - 1)) + inverse.T
    mixed = jnp.einsum(
        "km,fkxy->fmxy", transform, sample_deviations, precision=lax.Precision.HIGHEST
    )
    return sample_average + mixed


def solution(mesh):
    placed = (
        P(None, None, "gx", "gy"),
        P("gx", "gy"),
        P("gx", "gy"),
        P("gx", "gy", None),
        P("gx", "gy", None),
        P("gx", "gy", None),
    )
    return jax.shard_map(
        local, mesh=mesh, in_specs=placed, out_specs=P(None, None, "gx", "gy"), check_vma=False
    )
```

profile of v0, /device:TPU:24, one launch (start us, length us, event | category | flops | bytes accessed | tf_op | source)
XLA Modules:
  0.0 179.3 jit_solution(6452280479091019301)
XLA Ops:
  1.4 7.4 %collective-permute-start.1 = (f32[2,3,128]{2,1,0:T(4,128)S(1)}, f32[2,3,128]{2,1,0:T(4,128)S(1)}, u32[]{:S(2)}, u32[]{:S(2)}) collective-permute-start(f32[2,3,128]{2,1,0:T(4,128)S(1)} %get-tuple-element.47), channel_id=1, source_target_pairs={{4,0},{8,4},{12,8},{16,12},{20,16},{24,20},{28,24},{32,28},{36,32}... | collective-permute-start | bytes 9224 | tf_op jit(solution)/shard_map/ppermute | solution.py:15
  8.8 1.9 %collective-permute-start = (f32[2,3,128]{2,1,0:T(4,128)S(1)}, f32[2,3,128]{2,1,0:T(4,128)S(1)}, u32[]{:S(2)}, u32[]{:S(2)}) collective-permute-start(f32[2,3,128]{2,1,0:T(4,128)S(1)} %get-tuple-element.46), channel_id=1, source_target_pairs={{0,4},{4,8},{8,12},{12,16},{16,20},{20,24},{24,28},{28,32},{32,36}... | collective-permute-start | bytes 9224 | tf_op jit(solution)/shard_map/ppermute | solution.py:12
  10.7 1.6 copy.15
  12.6 3.2 %collective-permute-done = f32[2,3,128]{2,1,0:T(4,128)S(1)} collective-permute-done((f32[2,3,128]{2,1,0:T(4,128)S(1)}, f32[2,3,128]{2,1,0:T(4,128)S(1)}, u32[]{:S(2)}, u32[]{:S(2)}) %collective-permute-start) | collective-permute-done | bytes 3104 | tf_op jit(solution)/shard_map/ppermute | solution.py:12
  15.9 1.3 collective-permute-start.3
  17.2 4.5 %collective-permute-start.2 = (f32[2,14,3]{2,1,0:T(8,128)S(1)}, f32[2,14,3]{2,1,0:T(8,128)S(1)}, u32[]{:S(2)}, u32[]{:S(2)}) collective-permute-start(f32[2,14,3]{2,1,0:T(8,128)S(1)} %get-tuple-element.44), channel_id=1, source_target_pairs={{0,1},{1,2},{2,3},{4,5},{5,6},{6,7},{8,9},{9,10},{10,11},{12,13},{... | collective-permute-start | bytes 1016 | tf_op jit(solution)/shard_map/ppermute | solution.py:12
  21.8 2.0 %collective-permute-start.5 = (f32[3,64,1,128]{1,3,2,0:T(8,128)S(1)}, f32[3,64,1,128]{1,3,2,0:T(8,128)S(1)}, u32[]{:S(2)}, u32[]{:S(2)}) collective-permute-start(f32[3,64,1,128]{1,3,2,0:T(8,128)S(1)} %get-tuple-element.41), channel_id=1, source_target_pairs={{4,0},{8,4},{12,8},{16,12},{20,16},{24,20},{28,24},{32,28},{36,32}... | collective-permute-start | bytes 294920 | tf_op jit(solution)/shard_map/ppermute | solution.py:15
  23.8 2.3 %collective-permute-start.4 = (f32[3,64,1,128]{1,3,2,0:T(8,128)S(1)}, f32[3,64,1,128]{1,3,2,0:T(8,128)S(1)}, u32[]{:S(2)}, u32[]{:S(2)}) collective-permute-start(f32[3,64,1,128]{1,3,2,0:T(8,128)S(1)} %get-tuple-element.40), channel_id=1, source_target_pairs={{0,4},{4,8},{8,12},{12,16},{16,20},{20,24},{24,28},{28,32},{32,36}... | collective-permute-start | bytes 294920 | tf_op jit(solution)/shard_map/ppermute | solution.py:12
  26.9 5.9 %collective-permute-done.4 = f32[3,64,1,128]{1,3,2,0:T(8,128)S(1)} collective-permute-done((f32[3,64,1,128]{1,3,2,0:T(8,128)S(1)}, f32[3,64,1,128]{1,3,2,0:T(8,128)S(1)}, u32[]{:S(2)}, u32[]{:S(2)}) %collective-permute-start.4) | collective-permute-done | bytes 98336 | tf_op jit(solution)/shard_map/ppermute | solution.py:12
  32.9 1.3 collective-permute-start.7
  34.2 4.5 %collective-permute-start.6 = (f32[3,64,10,1]{1,3,2,0:T(1,128)S(1)}, f32[3,64,10,1]{1,3,2,0:T(1,128)S(1)}, u32[]{:S(2)}, u32[]{:S(2)}) collective-permute-start(f32[3,64,10,1]{1,3,2,0:T(1,128)S(1)} %get-tuple-element.34), channel_id=1, source_target_pairs={{0,1},{1,2},{2,3},{4,5},{5,6},{6,7},{8,9},{9,10},{10,11},{12,13},{... | collective-permute-start | bytes 23048 | tf_op jit(solution)/shard_map/ppermute | solution.py:12
  38.9 1.3 collective-permute-done.6
  42.2 1.9 %collective-permute-start.9 = (f32[3,64,1,128]{1,3,2,0:T(8,128)S(1)}, f32[3,64,1,128]{1,3,2,0:T(8,128)S(1)}, u32[]{:S(2)}, u32[]{:S(2)}) collective-permute-start(f32[3,64,1,128]{1,3,2,0:T(8,128)S(1)} %get-tuple-element.39), channel_id=1, source_target_pairs={{4,0},{8,4},{12,8},{16,12},{20,16},{24,20},{28,24},{32,28},{36,32}... | collective-permute-start | bytes 294920 | tf_op jit(solution)/shard_map/ppermute | solution.py:15
  44.2 2.4 %collective-permute-start.8 = (f32[3,64,1,128]{1,3,2,0:T(8,128)S(1)}, f32[3,64,1,128]{1,3,2,0:T(8,128)S(1)}, u32[]{:S(2)}, u32[]{:S(2)}) collective-permute-start(f32[3,64,1,128]{1,3,2,0:T(8,128)S(1)} %get-tuple-element.38), channel_id=1, source_target_pairs={{0,4},{4,8},{8,12},{12,16},{16,20},{20,24},{24,28},{28,32},{32,36}... | collective-permute-start | bytes 294920 | tf_op jit(solution)/shard_map/ppermute | solution.py:12
  46.6 0.8 collective-permute-done.9
  47.3 5.9 %collective-permute-done.8 = f32[3,64,1,128]{1,3,2,0:T(8,128)S(1)} collective-permute-done((f32[3,64,1,128]{1,3,2,0:T(8,128)S(1)}, f32[3,64,1,128]{1,3,2,0:T(8,128)S(1)}, u32[]{:S(2)}, u32[]{:S(2)}) %collective-permute-start.8) | collective-permute-done | bytes 98336 | tf_op jit(solution)/shard_map/ppermute | solution.py:12
  53.3 1.3 collective-permute-start.11
  54.6 4.8 %collective-permute-start.10 = (f32[3,64,10,1]{1,3,2,0:T(1,128)S(1)}, f32[3,64,10,1]{1,3,2,0:T(1,128)S(1)}, u32[]{:S(2)}, u32[]{:S(2)}) collective-permute-start(f32[3,64,10,1]{1,3,2,0:T(1,128)S(1)} %get-tuple-element.32), channel_id=1, source_target_pairs={{0,1},{1,2},{2,3},{4,5},{5,6},{6,7},{8,9},{9,10},{10,11},{12,13},{... | collective-permute-start | bytes 23048 | tf_op jit(solution)/shard_map/ppermute | solution.py:12
  59.5 1.4 collective-permute-done.10
  62.5 0.8 fusion.5
  63.3 1.9 %collective-permute-start.13 = (f32[3,64,1,128]{1,3,2,0:T(8,128)S(1)}, f32[3,64,1,128]{1,3,2,0:T(8,128)S(1)}, u32[]{:S(2)}, u32[]{:S(2)}) collective-permute-start(f32[3,64,1,128]{1,3,2,0:T(8,128)S(1)} %get-tuple-element.37), channel_id=1, source_target_pairs={{4,0},{8,4},{12,8},{16,12},{20,16},{24,20},{28,24},{32,28},{36,32}... | collective-permute-start | bytes 294920 | tf_op jit(solution)/shard_map/ppermute | solution.py:15
  65.3 2.4 %collective-permute-start.12 = (f32[3,64,1,128]{1,3,2,0:T(8,128)S(1)}, f32[3,64,1,128]{1,3,2,0:T(8,128)S(1)}, u32[]{:S(2)}, u32[]{:S(2)}) collective-permute-start(f32[3,64,1,128]{1,3,2,0:T(8,128)S(1)} %get-tuple-element.36), channel_id=1, source_target_pairs={{0,4},{4,8},{8,12},{12,16},{16,20},{20,24},{24,28},{28,32},{32,36}... | collective-permute-start | bytes 294920 | tf_op jit(solution)/shard_map/ppermute | solution.py:12
  68.4 5.9 %collective-permute-done.12 = f32[3,64,1,128]{1,3,2,0:T(8,128)S(1)} collective-permute-done((f32[3,64,1,128]{1,3,2,0:T(8,128)S(1)}, f32[3,64,1,128]{1,3,2,0:T(8,128)S(1)}, u32[]{:S(2)}, u32[]{:S(2)}) %collective-permute-start.12) | collective-permute-done | bytes 98336 | tf_op jit(solution)/shard_map/ppermute | solution.py:12
  74.4 1.3 collective-permute-start.15
  75.7 4.8 %collective-permute-start.14 = (f32[3,64,10,1]{1,3,2,0:T(1,128)S(1)}, f32[3,64,10,1]{1,3,2,0:T(1,128)S(1)}, u32[]{:S(2)}, u32[]{:S(2)}) collective-permute-start(f32[3,64,10,1]{1,3,2,0:T(1,128)S(1)} %get-tuple-element.30), channel_id=1, source_target_pairs={{0,1},{1,2},{2,3},{4,5},{5,6},{6,7},{8,9},{9,10},{10,11},{12,13},{... | collective-permute-start | bytes 23048 | tf_op jit(solution)/shard_map/ppermute | solution.py:12
  80.5 1.4 collective-permute-done.14
  83.6 1.7 fusion.77
  87.0 76.1 %all-reduce = (f32[64,64]{1,0:T(8,128)S(1)}, f32[64]{0:T(128)S(1)}) all-reduce(f32[64,64]{1,0:T(8,128)S(1)} %fusion.83, f32[64]{0:T(128)S(1)} %convolution_bitcast_fusion.2), channel_id=1, replica_groups=mesh['gx'=64,'gy'=4] {'gx','gy'}, use_global_device_ids=true, to_apply=%region_2.3 | all-reduce | flops 4160 | bytes 33280 | tf_op jit(solution)/shard_map/psum | solution.py:87
  163.2 5.8 %cholesky.18 = f32[64,64]{1,0:T(8,128)S(1)} custom-call(f32[64,64]{1,0:T(8,128)S(1)} %fusion.74), custom_call_target="Cholesky" | custom-call | tf_op jit(solution)/shard_map/jit(cholesky)/cholesky | solution.py:88
  170.4 4.9 %custom-call.10 = f32[1,64,64]{1,2,0:T(8,128)S(1)} custom-call(f32[1,64,64]{2,1,0:T(8,128)S(1)} %fusion.70), custom_call_target="InvertDiagBlocksLowerTriangular" | custom-call | tf_op jit(solution)/shard_map/triangular_solve | solution.py:54
  175.9 2.1 %fusion.15 = f32[3,64,8,128]{3,1,2,0:T(8,128)S(1)} fusion(f32[64,64,1,1]{1,0,3,2:T(8,128)S(1)} %fusion.18, f32[3,64,8,128]{1,3,2,0:T(8,128)S(1)} %get-tuple-element.8, f32[3,8,128]{2,1,0:T(8,128)S(1)} %broadcast_multiply_fusion.7), kind=kOutput, calls=%fused_computation.20 | convolution fusion | flops 151388160 | bytes 1601536 | tf_op jit(solution)/shard_map/km,fkxy->fmxy/dot_general | solution.py:93
  178.0 1.3 copy.19
  (65 shorter events, 12.5 us)
Async XLA Ops:
  1.4 11.2 %collective-permute-start.1 = (f32[2,3,128]{2,1,0:T(4,128)S(1)}, f32[2,3,128]{2,1,0:T(4,128)S(1)}, u32[]{:S(2)}, u32[]{:S(2)}) collective-permute-start(f32[2,3,128]{2,1,0:T(4,128)S(1)} %get-tuple-element.47), channel_id=1, source_target_pairs={{4,0},{8,4},{12,8},{16,12},{20,16},{24,20},{28,24},{32,28},{36,32}... | collective-permute-start | bytes 9224 | tf_op jit(solution)/shard_map/ppermute | solution.py:15
  8.8 7.0 %collective-permute-start = (f32[2,3,128]{2,1,0:T(4,128)S(1)}, f32[2,3,128]{2,1,0:T(4,128)S(1)}, u32[]{:S(2)}, u32[]{:S(2)}) collective-permute-start(f32[2,3,128]{2,1,0:T(4,128)S(1)} %get-tuple-element.46), channel_id=1, source_target_pairs={{0,4},{4,8},{8,12},{12,16},{16,20},{20,24},{24,28},{28,32},{32,36}... | collective-permute-start | bytes 9224 | tf_op jit(solution)/shard_map/ppermute | solution.py:12
  15.9 10.2 %collective-permute-start.3 = (f32[2,14,3]{2,1,0:T(8,128)S(1)}, f32[2,14,3]{2,1,0:T(8,128)S(1)}, u32[]{:S(2)}, u32[]{:S(2)}) collective-permute-start(f32[2,14,3]{2,1,0:T(8,128)S(1)} %get-tuple-element.45), channel_id=1, source_target_pairs={{1,0},{2,1},{3,2},{5,4},{6,5},{7,6},{9,8},{10,9},{11,10},{13,12},{... | collective-permute-start | bytes 1016 | tf_op jit(solution)/shard_map/ppermute | solution.py:15
  17.2 8.9 %collective-permute-start.2 = (f32[2,14,3]{2,1,0:T(8,128)S(1)}, f32[2,14,3]{2,1,0:T(8,128)S(1)}, u32[]{:S(2)}, u32[]{:S(2)}) collective-permute-start(f32[2,14,3]{2,1,0:T(8,128)S(1)} %get-tuple-element.44), channel_id=1, source_target_pairs={{0,1},{1,2},{2,3},{4,5},{5,6},{6,7},{8,9},{9,10},{10,11},{12,13},{... | collective-permute-start | bytes 1016 | tf_op jit(solution)/shard_map/ppermute | solution.py:12
  21.8 5.2 %collective-permute-start.5 = (f32[3,64,1,128]{1,3,2,0:T(8,128)S(1)}, f32[3,64,1,128]{1,3,2,0:T(8,128)S(1)}, u32[]{:S(2)}, u32[]{:S(2)}) collective-permute-start(f32[3,64,1,128]{1,3,2,0:T(8,128)S(1)} %get-tuple-element.41), channel_id=1, source_target_pairs={{4,0},{8,4},{12,8},{16,12},{20,16},{24,20},{28,24},{32,28},{36,32}... | collective-permute-start | bytes 294920 | tf_op jit(solution)/shard_map/ppermute | solution.py:15
  23.8 9.1 %collective-permute-start.4 = (f32[3,64,1,128]{1,3,2,0:T(8,128)S(1)}, f32[3,64,1,128]{1,3,2,0:T(8,128)S(1)}, u32[]{:S(2)}, u32[]{:S(2)}) collective-permute-start(f32[3,64,1,128]{1,3,2,0:T(8,128)S(1)} %get-tuple-element.40), channel_id=1, source_target_pairs={{0,4},{4,8},{8,12},{12,16},{16,20},{20,24},{24,28},{28,32},{32,36}... | collective-permute-start | bytes 294920 | tf_op jit(solution)/shard_map/ppermute | solution.py:12
  32.9 6.0 %collective-permute-start.7 = (f32[3,64,10,1]{1,3,2,0:T(1,128)S(1)}, f32[3,64,10,1]{1,3,2,0:T(1,128)S(1)}, u32[]{:S(2)}, u32[]{:S(2)}) collective-permute-start(f32[3,64,10,1]{1,3,2,0:T(1,128)S(1)} %get-tuple-element.35), channel_id=1, source_target_pairs={{1,0},{2,1},{3,2},{5,4},{6,5},{7,6},{9,8},{10,9},{11,10},{13,12},{... | collective-permute-start | bytes 23048 | tf_op jit(solution)/shard_map/ppermute | solution.py:15
  34.2 6.0 %collective-permute-start.6 = (f32[3,64,10,1]{1,3,2,0:T(1,128)S(1)}, f32[3,64,10,1]{1,3,2,0:T(1,128)S(1)}, u32[]{:S(2)}, u32[]{:S(2)}) collective-permute-start(f32[3,64,10,1]{1,3,2,0:T(1,128)S(1)} %get-tuple-element.34), channel_id=1, source_target_pairs={{0,1},{1,2},{2,3},{4,5},{5,6},{6,7},{8,9},{9,10},{10,11},{12,13},{... | collective-permute-start | bytes 23048 | tf_op jit(solution)/shard_map/ppermute | solution.py:12
  42.2 17.2 %copy-start = (s32[1,1,256]{2,1,0:T(1,128)S(1)}, s32[1,1,256]{2,1,0:T(1,128)}, u32[]{:S(2)}) copy-start(s32[1,1,256]{2,1,0:T(1,128)} %param.9) | copy-start | bytes 3076
  42.2 5.1 %collective-permute-start.9 = (f32[3,64,1,128]{1,3,2,0:T(8,128)S(1)}, f32[3,64,1,128]{1,3,2,0:T(8,128)S(1)}, u32[]{:S(2)}, u32[]{:S(2)}) collective-permute-start(f32[3,64,1,128]{1,3,2,0:T(8,128)S(1)} %get-tuple-element.39), channel_id=1, source_target_pairs={{4,0},{8,4},{12,8},{16,12},{20,16},{24,20},{28,24},{32,28},{36,32}... | collective-permute-start | bytes 294920 | tf_op jit(solution)/shard_map/ppermute | solution.py:15
  44.2 9.1 %collective-permute-start.8 = (f32[3,64,1,128]{1,3,2,0:T(8,128)S(1)}, f32[3,64,1,128]{1,3,2,0:T(8,128)S(1)}, u32[]{:S(2)}, u32[]{:S(2)}) collective-permute-start(f32[3,64,1,128]{1,3,2,0:T(8,128)S(1)} %get-tuple-element.38), channel_id=1, source_target_pairs={{0,4},{4,8},{8,12},{12,16},{16,20},{20,24},{24,28},{28,32},{32,36}... | collective-permute-start | bytes 294920 | tf_op jit(solution)/shard_map/ppermute | solution.py:12
  53.3 6.2 %collective-permute-start.11 = (f32[3,64,10,1]{1,3,2,0:T(1,128)S(1)}, f32[3,64,10,1]{1,3,2,0:T(1,128)S(1)}, u32[]{:S(2)}, u32[]{:S(2)}) collective-permute-start(f32[3,64,10,1]{1,3,2,0:T(1,128)S(1)} %get-tuple-element.33), channel_id=1, source_target_pairs={{1,0},{2,1},{3,2},{5,4},{6,5},{7,6},{9,8},{10,9},{11,10},{13,12},{... | collective-permute-start | bytes 23048 | tf_op jit(solution)/shard_map/ppermute | solution.py:15
  54.6 6.3 %collective-permute-start.10 = (f32[3,64,10,1]{1,3,2,0:T(1,128)S(1)}, f32[3,64,10,1]{1,3,2,0:T(1,128)S(1)}, u32[]{:S(2)}, u32[]{:S(2)}) collective-permute-start(f32[3,64,10,1]{1,3,2,0:T(1,128)S(1)} %get-tuple-element.32), channel_id=1, source_target_pairs={{0,1},{1,2},{2,3},{4,5},{5,6},{6,7},{8,9},{9,10},{10,11},{12,13},{... | collective-permute-start | bytes 23048 | tf_op jit(solution)/shard_map/ppermute | solution.py:12
  63.3 5.1 %collective-permute-start.13 = (f32[3,64,1,128]{1,3,2,0:T(8,128)S(1)}, f32[3,64,1,128]{1,3,2,0:T(8,128)S(1)}, u32[]{:S(2)}, u32[]{:S(2)}) collective-permute-start(f32[3,64,1,128]{1,3,2,0:T(8,128)S(1)} %get-tuple-element.37), channel_id=1, source_target_pairs={{4,0},{8,4},{12,8},{16,12},{20,16},{24,20},{28,24},{32,28},{36,32}... | collective-permute-start | bytes 294920 | tf_op jit(solution)/shard_map/ppermute | solution.py:15
  65.3 9.1 %collective-permute-start.12 = (f32[3,64,1,128]{1,3,2,0:T(8,128)S(1)}, f32[3,64,1,128]{1,3,2,0:T(8,128)S(1)}, u32[]{:S(2)}, u32[]{:S(2)}) collective-permute-start(f32[3,64,1,128]{1,3,2,0:T(8,128)S(1)} %get-tuple-element.36), channel_id=1, source_target_pairs={{0,4},{4,8},{8,12},{12,16},{16,20},{20,24},{24,28},{28,32},{32,36}... | collective-permute-start | bytes 294920 | tf_op jit(solution)/shard_map/ppermute | solution.py:12
  74.4 6.2 %collective-permute-start.15 = (f32[3,64,10,1]{1,3,2,0:T(1,128)S(1)}, f32[3,64,10,1]{1,3,2,0:T(1,128)S(1)}, u32[]{:S(2)}, u32[]{:S(2)}) collective-permute-start(f32[3,64,10,1]{1,3,2,0:T(1,128)S(1)} %get-tuple-element.31), channel_id=1, source_target_pairs={{1,0},{2,1},{3,2},{5,4},{6,5},{7,6},{9,8},{10,9},{11,10},{13,12},{... | collective-permute-start | bytes 23048 | tf_op jit(solution)/shard_map/ppermute | solution.py:15
  75.7 6.3 %collective-permute-start.14 = (f32[3,64,10,1]{1,3,2,0:T(1,128)S(1)}, f32[3,64,10,1]{1,3,2,0:T(1,128)S(1)}, u32[]{:S(2)}, u32[]{:S(2)}) collective-permute-start(f32[3,64,10,1]{1,3,2,0:T(1,128)S(1)} %get-tuple-element.30), channel_id=1, source_target_pairs={{0,1},{1,2},{2,3},{4,5},{5,6},{6,7},{8,9},{9,10},{10,11},{12,13},{... | collective-permute-start | bytes 23048 | tf_op jit(solution)/shard_map/ppermute | solution.py:12
  85.3 1.0 copy-start.1
  85.3 1.0 copy-start.2
where the time goes:
time: 181 us; the launch traced here: 179 us
  blocking collectives  76.1 us (42%)
  starting transfers between devices  46.2 us (26%)
  waiting for transfers between devices  27.3 us (15%)
  other arithmetic  21.6 us (12%)
  local copies, waits for them, and re-layouts  4.53 us (3%)
  matrix products  3.22 us (2%)
    psum x1, blocking collectives, local(): gram, projection = lax.psum((gram_part, proj_part), ('gx', 'gy'))  76.1 us
    ppermute x8, starting transfers between devices, extended(): lax.ppermute(lax.slice_in_dim(block, block.shape[dim] - width, None, axis...  27.8 us
    ppermute x8, waiting for transfers between devices, extended(): lax.ppermute(lax.slice_in_dim(block, block.shape[dim] - width, None, axis...  25.1 us
    ppermute x8, starting transfers between devices, extended(): lax.ppermute(lax.slice_in_dim(block, 0, width, axis=dim), axis, backward)  18.4 us
    another operation x3, other arithmetic, local(): lower = jnp.linalg.cholesky(eye + gram)  6.52 us
    another operation x2, other arithmetic, tri_solve(): lax.linalg.triangular_solve(lower, rhs, left_side=True, lower=True, trans...  5.55 us
  transfers between devices with their start and end apart: 16, of which 10 were waited for; matrix products, arithmetic and copies ran while one was open for 1% of the time, Pallas kernels for 0%

commit v1 on v0

--- a/solution.py
+++ b/solution.py
@@ -54,6 +54,14 @@
     return lax.linalg.triangular_solve(lower, rhs, left_side=True, lower=True, transpose_a=flipped)
 
 
+def summed(part):
+    for axis, flips in (("gx", (1,)), ("gy", (1, 3)), ("gx", (16, 48, 2, 4, 12))):
+        count = lax.axis_size(axis)
+        for flip in flips:
+            part = part + lax.ppermute(part, axis, [(i, i ^ flip) for i in range(count)])
+    return part
+
+
 def padded_section(field):
     return extended(field, (("gx", 2), ("gy", 3)), 1)
 
@@ -84,7 +92,8 @@
     gram_part = jnp.dot(scaled, scaled.T, precision=lax.Precision.HIGHEST)
     proj_part = jnp.dot(scaled, innovation, precision=lax.Precision.HIGHEST)
     eye = jnp.eye(sample_number, dtype=jnp.float32)
-    gram, projection = lax.psum((gram_part, proj_part), ("gx", "gy"))
+    both = summed(jnp.concatenate([gram_part, proj_part[:, None]], axis=1))
+    gram, projection = both[:, :sample_number], both[:, sample_number]
     lower = jnp.linalg.cholesky(eye + gram)
     half = tri_solve(lower, projection[:, None], False)
     weights = tri_solve(lower, half, True)[:, 0]

time: 181 us -> 141 us (0.78)
  blocking collectives: 76.1 us -> 0 us
  waiting for transfers between devices: 27.3 us -> 55.7 us
  starting transfers between devices: 46.2 us -> 53.6 us
    psum x1 -> x0, blocking collectives: 76.1 us -> none  [local(): gram, projection = lax.psum((gram_part, proj_part), ('gx', 'gy'))]
    ppermute x0 -> x8, waiting for transfers between devices: none -> 28.5 us  [summed(): lax.ppermute(part, axis, [(i, i ^ flip) for i in range(count)])]
    ppermute x0 -> x8, starting transfers between devices: none -> 7.44 us  [summed(): lax.ppermute(part, axis, [(i, i ^ flip) for i in range(count)])]
  transfers between devices with their start and end apart: 16 -> 24, of which waited for: 10 -> 18; matrix products, arithmetic and copies ran while one was open for 1% -> 2% of each run, Pallas kernels for 0% -> 0%
where the time goes in v1:
time: 141 us; the launch traced here: 140 us
  waiting for transfers between devices  55.7 us (40%)
  starting transfers between devices  53.6 us (38%)
  other arithmetic  21.6 us (15%)
  local copies, waits for them, and re-layouts  4.7 us (3%)
  matrix products  3.83 us (3%)
    ppermute x8, waiting for transfers between devices, summed(): lax.ppermute(part, axis, [(i, i ^ flip) for i in range(count)])  28.5 us
    ppermute x8, starting transfers between devices, extended(): lax.ppermute(lax.slice_in_dim(block, block.shape[dim] - width, None, axis...  27.8 us
    ppermute x8, waiting for transfers between devices, extended(): lax.ppermute(lax.slice_in_dim(block, block.shape[dim] - width, None, axis...  25.1 us
    ppermute x8, starting transfers between devices, extended(): lax.ppermute(lax.slice_in_dim(block, 0, width, axis=dim), axis, backward)  18.4 us
    ppermute x8, starting transfers between devices, summed(): lax.ppermute(part, axis, [(i, i ^ flip) for i in range(count)])  7.44 us
    another operation x3, other arithmetic, local(): lower = jnp.linalg.cholesky(eye + gram)  6.52 us
    another operation x2, other arithmetic, tri_solve(): lax.linalg.triangular_solve(lower, rhs, left_side=True, lower=True, trans...  5.55 us
    another operation x6, other arithmetic, height_tendency(): return jnp.stack([dh, du, dv]) * mask  2.94 us
  transfers between devices with their start and end apart: 24, of which 18 were waited for; matrix products, arithmetic and copies ran while one was open for 2% of the time, Pallas kernels for 0%

profile of v1, /device:TPU:24, one launch (start us, length us, event | category | flops | bytes accessed | tf_op | source)
XLA Modules:
  0.0 140.1 jit_solution(17589224268390294629)
XLA Ops:
  1.4 7.4 %collective-permute-start.1 = (f32[2,3,128]{2,1,0:T(4,128)S(1)}, f32[2,3,128]{2,1,0:T(4,128)S(1)}, u32[]{:S(2)}, u32[]{:S(2)}) collective-permute-start(f32[2,3,128]{2,1,0:T(4,128)S(1)} %get-tuple-element.45), channel_id=1, source_target_pairs={{4,0},{8,4},{12,8},{16,12},{20,16},{24,20},{28,24},{32,28},{36,32}... | collective-permute-start | bytes 9224 | tf_op jit(solution)/shard_map/ppermute | solution.py:15
  8.8 1.9 %collective-permute-start = (f32[2,3,128]{2,1,0:T(4,128)S(1)}, f32[2,3,128]{2,1,0:T(4,128)S(1)}, u32[]{:S(2)}, u32[]{:S(2)}) collective-permute-start(f32[2,3,128]{2,1,0:T(4,128)S(1)} %get-tuple-element.44), channel_id=1, source_target_pairs={{0,4},{4,8},{8,12},{12,16},{16,20},{20,24},{24,28},{28,32},{32,36}... | collective-permute-start | bytes 9224 | tf_op jit(solution)/shard_map/ppermute | solution.py:12
  10.7 1.6 %copy.17 = f32[3,64,8,128]{1,3,2,0:T(8,128)S(1)} copy(f32[3,64,8,128]{3,2,1,0:T(8,128)} %param.6) | data formatting | bytes 1572864 | tf_op args[0]
  12.6 3.2 %collective-permute-done = f32[2,3,128]{2,1,0:T(4,128)S(1)} collective-permute-done((f32[2,3,128]{2,1,0:T(4,128)S(1)}, f32[2,3,128]{2,1,0:T(4,128)S(1)}, u32[]{:S(2)}, u32[]{:S(2)}) %collective-permute-start) | collective-permute-done | bytes 3104 | tf_op jit(solution)/shard_map/ppermute | solution.py:12
  17.2 4.5 %collective-permute-start.2 = (f32[2,14,3]{2,1,0:T(8,128)S(1)}, f32[2,14,3]{2,1,0:T(8,128)S(1)}, u32[]{:S(2)}, u32[]{:S(2)}) collective-permute-start(f32[2,14,3]{2,1,0:T(8,128)S(1)} %get-tuple-element.42), channel_id=1, source_target_pairs={{0,1},{1,2},{2,3},{4,5},{5,6},{6,7},{8,9},{9,10},{10,11},{12,13},{... | collective-permute-start | bytes 1016 | tf_op jit(solution)/shard_map/ppermute | solution.py:12
  21.8 2.0 %collective-permute-start.5 = (f32[3,64,1,128]{1,3,2,0:T(8,128)S(1)}, f32[3,64,1,128]{1,3,2,0:T(8,128)S(1)}, u32[]{:S(2)}, u32[]{:S(2)}) collective-permute-start(f32[3,64,1,128]{1,3,2,0:T(8,128)S(1)} %get-tuple-element.39), channel_id=1, source_target_pairs={{4,0},{8,4},{12,8},{16,12},{20,16},{24,20},{28,24},{32,28},{36,32}... | collective-permute-start | bytes 294920 | tf_op jit(solution)/shard_map/ppermute | solution.py:15
  23.8 2.3 %collective-permute-start.4 = (f32[3,64,1,128]{1,3,2,0:T(8,128)S(1)}, f32[3,64,1,128]{1,3,2,0:T(8,128)S(1)}, u32[]{:S(2)}, u32[]{:S(2)}) collective-permute-start(f32[3,64,1,128]{1,3,2,0:T(8,128)S(1)} %get-tuple-element.38), channel_id=1, source_target_pairs={{0,4},{4,8},{8,12},{12,16},{16,20},{20,24},{24,28},{28,32},{32,36}... | collective-permute-start | bytes 294920 | tf_op jit(solution)/shard_map/ppermute | solution.py:12
  26.9 5.9 %collective-permute-done.4 = f32[3,64,1,128]{1,3,2,0:T(8,128)S(1)} collective-permute-done((f32[3,64,1,128]{1,3,2,0:T(8,128)S(1)}, f32[3,64,1,128]{1,3,2,0:T(8,128)S(1)}, u32[]{:S(2)}, u32[]{:S(2)}) %collective-permute-start.4) | collective-permute-done | bytes 98336 | tf_op jit(solution)/shard_map/ppermute | solution.py:12
  34.2 4.5 %collective-permute-start.6 = (f32[3,64,10,1]{1,3,2,0:T(1,128)S(1)}, f32[3,64,10,1]{1,3,2,0:T(1,128)S(1)}, u32[]{:S(2)}, u32[]{:S(2)}) collective-permute-start(f32[3,64,10,1]{1,3,2,0:T(1,128)S(1)} %get-tuple-element.32), channel_id=1, source_target_pairs={{0,1},{1,2},{2,3},{4,5},{5,6},{6,7},{8,9},{9,10},{10,11},{12,13},{... | collective-permute-start | bytes 23048 | tf_op jit(solution)/shard_map/ppermute | solution.py:12
  42.2 1.9 %collective-permute-start.9 = (f32[3,64,1,128]{1,3,2,0:T(8,128)S(1)}, f32[3,64,1,128]{1,3,2,0:T(8,128)S(1)}, u32[]{:S(2)}, u32[]{:S(2)}) collective-permute-start(f32[3,64,1,128]{1,3,2,0:T(8,128)S(1)} %get-tuple-element.37), channel_id=1, source_target_pairs={{4,0},{8,4},{12,8},{16,12},{20,16},{24,20},{28,24},{32,28},{36,32}... | collective-permute-start | bytes 294920 | tf_op jit(solution)/shard_map/ppermute | solution.py:15
  44.2 2.4 %collective-permute-start.8 = (f32[3,64,1,128]{1,3,2,0:T(8,128)S(1)}, f32[3,64,1,128]{1,3,2,0:T(8,128)S(1)}, u32[]{:S(2)}, u32[]{:S(2)}) collective-permute-start(f32[3,64,1,128]{1,3,2,0:T(8,128)S(1)} %get-tuple-element.36), channel_id=1, source_target_pairs={{0,4},{4,8},{8,12},{12,16},{16,20},{20,24},{24,28},{28,32},{32,36}... | collective-permute-start | bytes 294920 | tf_op jit(solution)/shard_map/ppermute | solution.py:12
  47.3 5.9 %collective-permute-done.8 = f32[3,64,1,128]{1,3,2,0:T(8,128)S(1)} collective-permute-done((f32[3,64,1,128]{1,3,2,0:T(8,128)S(1)}, f32[3,64,1,128]{1,3,2,0:T(8,128)S(1)}, u32[]{:S(2)}, u32[]{:S(2)}) %collective-permute-start.8) | collective-permute-done | bytes 98336 | tf_op jit(solution)/shard_map/ppermute | solution.py:12
  54.6 4.8 %collective-permute-start.10 = (f32[3,64,10,1]{1,3,2,0:T(1,128)S(1)}, f32[3,64,10,1]{1,3,2,0:T(1,128)S(1)}, u32[]{:S(2)}, u32[]{:S(2)}) collective-permute-start(f32[3,64,10,1]{1,3,2,0:T(1,128)S(1)} %get-tuple-element.30), channel_id=1, source_target_pairs={{0,1},{1,2},{2,3},{4,5},{5,6},{6,7},{8,9},{9,10},{10,11},{12,13},{... | collective-permute-start | bytes 23048 | tf_op jit(solution)/shard_map/ppermute | solution.py:12
  59.5 1.4 collective-permute-done.10
  63.3 1.9 %collective-permute-start.13 = (f32[3,64,1,128]{1,3,2,0:T(8,128)S(1)}, f32[3,64,1,128]{1,3,2,0:T(8,128)S(1)}, u32[]{:S(2)}, u32[]{:S(2)}) collective-permute-start(f32[3,64,1,128]{1,3,2,0:T(8,128)S(1)} %get-tuple-element.35), channel_id=1, source_target_pairs={{4,0},{8,4},{12,8},{16,12},{20,16},{24,20},{28,24},{32,28},{36,32}... | collective-permute-start | bytes 294920 | tf_op jit(solution)/shard_map/ppermute | solution.py:15
  65.3 2.4 %collective-permute-start.12 = (f32[3,64,1,128]{1,3,2,0:T(8,128)S(1)}, f32[3,64,1,128]{1,3,2,0:T(8,128)S(1)}, u32[]{:S(2)}, u32[]{:S(2)}) collective-permute-start(f32[3,64,1,128]{1,3,2,0:T(8,128)S(1)} %get-tuple-element.34), channel_id=1, source_target_pairs={{0,4},{4,8},{8,12},{12,16},{16,20},{20,24},{24,28},{28,32},{32,36}... | collective-permute-start | bytes 294920 | tf_op jit(solution)/shard_map/ppermute | solution.py:12
  68.4 5.9 %collective-permute-done.12 = f32[3,64,1,128]{1,3,2,0:T(8,128)S(1)} collective-permute-done((f32[3,64,1,128]{1,3,2,0:T(8,128)S(1)}, f32[3,64,1,128]{1,3,2,0:T(8,128)S(1)}, u32[]{:S(2)}, u32[]{:S(2)}) %collective-permute-start.12) | collective-permute-done | bytes 98336 | tf_op jit(solution)/shard_map/ppermute | solution.py:12
  75.7 4.8 %collective-permute-start.14 = (f32[3,64,10,1]{1,3,2,0:T(1,128)S(1)}, f32[3,64,10,1]{1,3,2,0:T(1,128)S(1)}, u32[]{:S(2)}, u32[]{:S(2)}) collective-permute-start(f32[3,64,10,1]{1,3,2,0:T(1,128)S(1)} %get-tuple-element.28), channel_id=1, source_target_pairs={{0,1},{1,2},{2,3},{4,5},{5,6},{6,7},{8,9},{9,10},{10,11},{12,13},{... | collective-permute-start | bytes 23048 | tf_op jit(solution)/shard_map/ppermute | solution.py:12
  80.5 1.4 collective-permute-done.14
  83.6 1.7 %fusion.78 = (f32[3,8,128]{2,1,0:T(8,128)S(1)}, f32[3,64,8,128]{1,3,2,0:T(8,128)S(1)}) fusion(f32[8,128]{1,0:T(8,128)S(1)} %slice.427, f32[1,64,8,128]{1,3,2,0:T(8,128)S(1)} %get-tuple-element.14, f32[1,64,8,128]{1,3,2,0:T(8,128)S(1)} %get-tuple-element.13, f32[1,64,8,128]{1,3,2,0:T(8,128)S(1)} %fusion.32, f32[1,64,8,128]{1,3,2,0:T(8,128)S(1)} %get-tuple-element.19, ...), kind=kLoop, calls=%fused_computation.165 | loop fusion | flops 4518912 | bytes 3952640 | tf_op jit(solution)/shard_map/reduce_sum | solution.py:83
  88.9 2.3 %collective-permute-start.17 = (f32[64,65]{1,0:T(8,128)S(1)}, f32[64,65]{1,0:T(8,128)S(1)}, u32[]{:S(2)}, u32[]{:S(2)}) collective-permute-start(f32[64,65]{1,0:T(8,128)S(1)} %fusion.87), channel_id=1, source_target_pairs={{0,1},{1,0},{2,3},{3,2},{4,5},{5,4},{6,7},{7,6},{8,9},{9,8},{10,11... | collective-permute-start | bytes 49928 | tf_op jit(solution)/shard_map/ppermute | solution.py:61
  91.2 1.9 %collective-permute-done.17 = f32[64,65]{1,0:T(8,128)S(1)} collective-permute-done((f32[64,65]{1,0:T(8,128)S(1)}, f32[64,65]{1,0:T(8,128)S(1)}, u32[]{:S(2)}, u32[]{:S(2)}) %collective-permute-start.17) | collective-permute-done | bytes 16672 | tf_op jit(solution)/shard_map/ppermute | solution.py:61
  93.1 4.6 %collective-permute-start.18 = (f32[64,65]{1,0:T(8,128)S(1)}, f32[64,65]{1,0:T(8,128)S(1)}, u32[]{:S(2)}, u32[]{:S(2)}) collective-permute-start(f32[64,65]{1,0:T(8,128)S(1)} %add.267), channel_id=1, source_target_pairs={{0,3},{1,2},{2,1},{3,0},{4,7},{5,6},{6,5},{7,4},{8,11},{9,10},{10,... | collective-permute-start | bytes 49928 | tf_op jit(solution)/shard_map/ppermute | solution.py:61
  97.7 1.9 %collective-permute-done.18 = f32[64,65]{1,0:T(8,128)S(1)} collective-permute-done((f32[64,65]{1,0:T(8,128)S(1)}, f32[64,65]{1,0:T(8,128)S(1)}, u32[]{:S(2)}, u32[]{:S(2)}) %collective-permute-start.18) | collective-permute-done | bytes 16672 | tf_op jit(solution)/shard_map/ppermute | solution.py:61
  100.1 3.5 %collective-permute-done.19 = f32[64,65]{1,0:T(8,128)S(1)} collective-permute-done((f32[64,65]{1,0:T(8,128)S(1)}, f32[64,65]{1,0:T(8,128)S(1)}, u32[]{:S(2)}, u32[]{:S(2)}) %collective-permute-start.19) | collective-permute-done | bytes 16672 | tf_op jit(solution)/shard_map/ppermute | solution.py:61
  103.5 5.1 %collective-permute-done.20 = f32[64,65]{1,0:T(8,128)S(1)} collective-permute-done((f32[64,65]{1,0:T(8,128)S(1)}, f32[64,65]{1,0:T(8,128)S(1)}, u32[]{:S(2)}, u32[]{:S(2)}) %collective-permute-start.20) | collective-permute-done | bytes 16672 | tf_op jit(solution)/shard_map/ppermute | solution.py:61
  108.7 4.1 %collective-permute-done.21 = f32[64,65]{1,0:T(8,128)S(1)} collective-permute-done((f32[64,65]{1,0:T(8,128)S(1)}, f32[64,65]{1,0:T(8,128)S(1)}, u32[]{:S(2)}, u32[]{:S(2)}) %collective-permute-start.21) | collective-permute-done | bytes 16672 | tf_op jit(solution)/shard_map/ppermute | solution.py:61
  112.8 4.8 %collective-permute-done.22 = f32[64,65]{1,0:T(8,128)S(1)} collective-permute-done((f32[64,65]{1,0:T(8,128)S(1)}, f32[64,65]{1,0:T(8,128)S(1)}, u32[]{:S(2)}, u32[]{:S(2)}) %collective-permute-start.22) | collective-permute-done | bytes 16672 | tf_op jit(solution)/shard_map/ppermute | solution.py:61
  117.6 6.0 %collective-permute-done.23 = f32[64,65]{1,0:T(8,128)S(1)} collective-permute-done((f32[64,65]{1,0:T(8,128)S(1)}, f32[64,65]{1,0:T(8,128)S(1)}, u32[]{:S(2)}, u32[]{:S(2)}) %collective-permute-start.23) | collective-permute-done | bytes 16672 | tf_op jit(solution)/shard_map/ppermute | solution.py:61
  124.0 5.8 %cholesky.18 = f32[64,64]{1,0:T(8,128)S(1)} custom-call(f32[64,64]{1,0:T(8,128)S(1)} %fusion.74), custom_call_target="Cholesky" | custom-call | tf_op jit(solution)/shard_map/jit(cholesky)/cholesky | solution.py:97
  131.1 4.9 %custom-call.10 = f32[1,64,64]{1,2,0:T(8,128)S(1)} custom-call(f32[1,64,64]{2,1,0:T(8,128)S(1)} %fusion.70), custom_call_target="InvertDiagBlocksLowerTriangular" | custom-call | tf_op jit(solution)/shard_map/triangular_solve | solution.py:54
  136.6 2.1 %fusion.15 = f32[3,64,8,128]{3,1,2,0:T(8,128)S(1)} fusion(f32[64,64,1,1]{1,0,3,2:T(8,128)S(1)} %fusion.18, f32[3,64,8,128]{1,3,2,0:T(8,128)S(1)} %get-tuple-element.6, f32[3,8,128]{2,1,0:T(8,128)S(1)} %broadcast_multiply_fusion.7), kind=kOutput, calls=%fused_computation.20 | convolution fusion | flops 151388160 | bytes 1601536 | tf_op jit(solution)/shard_map/km,fkxy->fmxy/dot_general | solution.py:102
  (89 shorter events, 24.3 us)
Async XLA Ops:
  1.4 11.2 %collective-permute-start.1 = (f32[2,3,128]{2,1,0:T(4,128)S(1)}, f32[2,3,128]{2,1,0:T(4,128)S(1)}, u32[]{:S(2)}, u32[]{:S(2)}) collective-permute-start(f32[2,3,128]{2,1,0:T(4,128)S(1)} %get-tuple-element.45), channel_id=1, source_target_pairs={{4,0},{8,4},{12,8},{16,12},{20,16},{24,20},{28,24},{32,28},{36,32}... | collective-permute-start | bytes 9224 | tf_op jit(solution)/shard_map/ppermute | solution.py:15
  8.8 7.0 %collective-permute-start = (f32[2,3,128]{2,1,0:T(4,128)S(1)}, f32[2,3,128]{2,1,0:T(4,128)S(1)}, u32[]{:S(2)}, u32[]{:S(2)}) collective-permute-start(f32[2,3,128]{2,1,0:T(4,128)S(1)} %get-tuple-element.44), channel_id=1, source_target_pairs={{0,4},{4,8},{8,12},{12,16},{16,20},{20,24},{24,28},{28,32},{32,36}... | collective-permute-start | bytes 9224 | tf_op jit(solution)/shard_map/ppermute | solution.py:12
  15.9 10.2 %collective-permute-start.3 = (f32[2,14,3]{2,1,0:T(8,128)S(1)}, f32[2,14,3]{2,1,0:T(8,128)S(1)}, u32[]{:S(2)}, u32[]{:S(2)}) collective-permute-start(f32[2,14,3]{2,1,0:T(8,128)S(1)} %get-tuple-element.43), channel_id=1, source_target_pairs={{1,0},{2,1},{3,2},{5,4},{6,5},{7,6},{9,8},{10,9},{11,10},{13,12},{... | collective-permute-start | bytes 1016 | tf_op jit(solution)/shard_map/ppermute | solution.py:15
  17.2 8.9 %collective-permute-start.2 = (f32[2,14,3]{2,1,0:T(8,128)S(1)}, f32[2,14,3]{2,1,0:T(8,128)S(1)}, u32[]{:S(2)}, u32[]{:S(2)}) collective-permute-start(f32[2,14,3]{2,1,0:T(8,128)S(1)} %get-tuple-element.42), channel_id=1, source_target_pairs={{0,1},{1,2},{2,3},{4,5},{5,6},{6,7},{8,9},{9,10},{10,11},{12,13},{... | collective-permute-start | bytes 1016 | tf_op jit(solution)/shard_map/ppermute | solution.py:12
  21.8 5.2 %collective-permute-start.5 = (f32[3,64,1,128]{1,3,2,0:T(8,128)S(1)}, f32[3,64,1,128]{1,3,2,0:T(8,128)S(1)}, u32[]{:S(2)}, u32[]{:S(2)}) collective-permute-start(f32[3,64,1,128]{1,3,2,0:T(8,128)S(1)} %get-tuple-element.39), channel_id=1, source_target_pairs={{4,0},{8,4},{12,8},{16,12},{20,16},{24,20},{28,24},{32,28},{36,32}... | collective-permute-start | bytes 294920 | tf_op jit(solution)/shard_map/ppermute | solution.py:15
  23.8 9.1 %collective-permute-start.4 = (f32[3,64,1,128]{1,3,2,0:T(8,128)S(1)}, f32[3,64,1,128]{1,3,2,0:T(8,128)S(1)}, u32[]{:S(2)}, u32[]{:S(2)}) collective-permute-start(f32[3,64,1,128]{1,3,2,0:T(8,128)S(1)} %get-tuple-element.38), channel_id=1, source_target_pairs={{0,4},{4,8},{8,12},{12,16},{16,20},{20,24},{24,28},{28,32},{32,36}... | collective-permute-start | bytes 294920 | tf_op jit(solution)/shard_map/ppermute | solution.py:12
  32.9 6.0 %collective-permute-start.7 = (f32[3,64,10,1]{1,3,2,0:T(1,128)S(1)}, f32[3,64,10,1]{1,3,2,0:T(1,128)S(1)}, u32[]{:S(2)}, u32[]{:S(2)}) collective-permute-start(f32[3,64,10,1]{1,3,2,0:T(1,128)S(1)} %get-tuple-element.33), channel_id=1, source_target_pairs={{1,0},{2,1},{3,2},{5,4},{6,5},{7,6},{9,8},{10,9},{11,10},{13,12},{... | collective-permute-start | bytes 23048 | tf_op jit(solution)/shard_map/ppermute | solution.py:15
  34.2 6.0 %collective-permute-start.6 = (f32[3,64,10,1]{1,3,2,0:T(1,128)S(1)}, f32[3,64,10,1]{1,3,2,0:T(1,128)S(1)}, u32[]{:S(2)}, u32[]{:S(2)}) collective-permute-start(f32[3,64,10,1]{1,3,2,0:T(1,128)S(1)} %get-tuple-element.32), channel_id=1, source_target_pairs={{0,1},{1,2},{2,3},{4,5},{5,6},{6,7},{8,9},{9,10},{10,11},{12,13},{... | collective-permute-start | bytes 23048 | tf_op jit(solution)/shard_map/ppermute | solution.py:12
  42.2 17.2 %copy-start = (s32[1,1,256]{2,1,0:T(1,128)S(1)}, s32[1,1,256]{2,1,0:T(1,128)}, u32[]{:S(2)}) copy-start(s32[1,1,256]{2,1,0:T(1,128)} %param.9) | copy-start | bytes 3076
  42.2 5.1 %collective-permute-start.9 = (f32[3,64,1,128]{1,3,2,0:T(8,128)S(1)}, f32[3,64,1,128]{1,3,2,0:T(8,128)S(1)}, u32[]{:S(2)}, u32[]{:S(2)}) collective-permute-start(f32[3,64,1,128]{1,3,2,0:T(8,128)S(1)} %get-tuple-element.37), channel_id=1, source_target_pairs={{4,0},{8,4},{12,8},{16,12},{20,16},{24,20},{28,24},{32,28},{36,32}... | collective-permute-start | bytes 294920 | tf_op jit(solution)/shard_map/ppermute | solution.py:15
  44.2 9.1 %collective-permute-start.8 = (f32[3,64,1,128]{1,3,2,0:T(8,128)S(1)}, f32[3,64,1,128]{1,3,2,0:T(8,128)S(1)}, u32[]{:S(2)}, u32[]{:S(2)}) collective-permute-start(f32[3,64,1,128]{1,3,2,0:T(8,128)S(1)} %get-tuple-element.36), channel_id=1, source_target_pairs={{0,4},{4,8},{8,12},{12,16},{16,20},{20,24},{24,28},{28,32},{32,36}... | collective-permute-start | bytes 294920 | tf_op jit(solution)/shard_map/ppermute | solution.py:12
  53.3 6.2 %collective-permute-start.11 = (f32[3,64,10,1]{1,3,2,0:T(1,128)S(1)}, f32[3,64,10,1]{1,3,2,0:T(1,128)S(1)}, u32[]{:S(2)}, u32[]{:S(2)}) collective-permute-start(f32[3,64,10,1]{1,3,2,0:T(1,128)S(1)} %get-tuple-element.31), channel_id=1, source_target_pairs={{1,0},{2,1},{3,2},{5,4},{6,5},{7,6},{9,8},{10,9},{11,10},{13,12},{... | collective-permute-start | bytes 23048 | tf_op jit(solution)/shard_map/ppermute | solution.py:15
  54.6 6.3 %collective-permute-start.10 = (f32[3,64,10,1]{1,3,2,0:T(1,128)S(1)}, f32[3,64,10,1]{1,3,2,0:T(1,128)S(1)}, u32[]{:S(2)}, u32[]{:S(2)}) collective-permute-start(f32[3,64,10,1]{1,3,2,0:T(1,128)S(1)} %get-tuple-element.30), channel_id=1, source_target_pairs={{0,1},{1,2},{2,3},{4,5},{5,6},{6,7},{8,9},{9,10},{10,11},{12,13},{... | collective-permute-start | bytes 23048 | tf_op jit(solution)/shard_map/ppermute | solution.py:12
  63.3 5.1 %collective-permute-start.13 = (f32[3,64,1,128]{1,3,2,0:T(8,128)S(1)}, f32[3,64,1,128]{1,3,2,0:T(8,128)S(1)}, u32[]{:S(2)}, u32[]{:S(2)}) collective-permute-start(f32[3,64,1,128]{1,3,2,0:T(8,128)S(1)} %get-tuple-element.35), channel_id=1, source_target_pairs={{4,0},{8,4},{12,8},{16,12},{20,16},{24,20},{28,24},{32,28},{36,32}... | collective-permute-start | bytes 294920 | tf_op jit(solution)/shard_map/ppermute | solution.py:15
  65.3 9.1 %collective-permute-start.12 = (f32[3,64,1,128]{1,3,2,0:T(8,128)S(1)}, f32[3,64,1,128]{1,3,2,0:T(8,128)S(1)}, u32[]{:S(2)}, u32[]{:S(2)}) collective-permute-start(f32[3,64,1,128]{1,3,2,0:T(8,128)S(1)} %get-tuple-element.34), channel_id=1, source_target_pairs={{0,4},{4,8},{8,12},{12,16},{16,20},{20,24},{24,28},{28,32},{32,36}... | collective-permute-start | bytes 294920 | tf_op jit(solution)/shard_map/ppermute | solution.py:12
  74.4 6.2 %collective-permute-start.15 = (f32[3,64,10,1]{1,3,2,0:T(1,128)S(1)}, f32[3,64,10,1]{1,3,2,0:T(1,128)S(1)}, u32[]{:S(2)}, u32[]{:S(2)}) collective-permute-start(f32[3,64,10,1]{1,3,2,0:T(1,128)S(1)} %get-tuple-element.29), channel_id=1, source_target_pairs={{1,0},{2,1},{3,2},{5,4},{6,5},{7,6},{9,8},{10,9},{11,10},{13,12},{... | collective-permute-start | bytes 23048 | tf_op jit(solution)/shard_map/ppermute | solution.py:15
  75.7 6.3 %collective-permute-start.14 = (f32[3,64,10,1]{1,3,2,0:T(1,128)S(1)}, f32[3,64,10,1]{1,3,2,0:T(1,128)S(1)}, u32[]{:S(2)}, u32[]{:S(2)}) collective-permute-start(f32[3,64,10,1]{1,3,2,0:T(1,128)S(1)} %get-tuple-element.28), channel_id=1, source_target_pairs={{0,1},{1,2},{2,3},{4,5},{5,6},{6,7},{8,9},{9,10},{10,11},{12,13},{... | collective-permute-start | bytes 23048 | tf_op jit(solution)/shard_map/ppermute | solution.py:12
  85.3 1.0 copy-start.1
  85.3 1.0 copy-start.2
  87.6 1.2 collective-permute-start.16
  88.9 4.2 %collective-permute-start.17 = (f32[64,65]{1,0:T(8,128)S(1)}, f32[64,65]{1,0:T(8,128)S(1)}, u32[]{:S(2)}, u32[]{:S(2)}) collective-permute-start(f32[64,65]{1,0:T(8,128)S(1)} %fusion.87), channel_id=1, source_target_pairs={{0,1},{1,0},{2,3},{3,2},{4,5},{5,4},{6,7},{7,6},{8,9},{9,8},{10,11... | collective-permute-start | bytes 49928 | tf_op jit(solution)/shard_map/ppermute | solution.py:61
  93.1 6.5 %collective-permute-start.18 = (f32[64,65]{1,0:T(8,128)S(1)}, f32[64,65]{1,0:T(8,128)S(1)}, u32[]{:S(2)}, u32[]{:S(2)}) collective-permute-start(f32[64,65]{1,0:T(8,128)S(1)} %add.267), channel_id=1, source_target_pairs={{0,3},{1,2},{2,1},{3,0},{4,7},{5,6},{6,5},{7,4},{8,11},{9,10},{10,... | collective-permute-start | bytes 49928 | tf_op jit(solution)/shard_map/ppermute | solution.py:61
  99.6 3.9 %collective-permute-start.19 = (f32[64,65]{1,0:T(8,128)S(1)}, f32[64,65]{1,0:T(8,128)S(1)}, u32[]{:S(2)}, u32[]{:S(2)}) collective-permute-start(f32[64,65]{1,0:T(8,128)S(1)} %add.268), channel_id=1, source_target_pairs={{0,64},{4,68},{8,72},{12,76},{16,80},{20,84},{24,88},{28,92},{32,9... | collective-permute-start | bytes 49928 | tf_op jit(solution)/shard_map/ppermute | solution.py:61
  103.5 5.1 %collective-permute-start.20 = (f32[64,65]{1,0:T(8,128)S(1)}, f32[64,65]{1,0:T(8,128)S(1)}, u32[]{:S(2)}, u32[]{:S(2)}) collective-permute-start(f32[64,65]{1,0:T(8,128)S(1)} %add.269), channel_id=1, source_target_pairs={{0,192},{4,196},{8,200},{12,204},{16,208},{20,212},{24,216},{28,22... | collective-permute-start | bytes 49928 | tf_op jit(solution)/shard_map/ppermute | solution.py:61
  108.7 4.1 %collective-permute-start.21 = (f32[64,65]{1,0:T(8,128)S(1)}, f32[64,65]{1,0:T(8,128)S(1)}, u32[]{:S(2)}, u32[]{:S(2)}) collective-permute-start(f32[64,65]{1,0:T(8,128)S(1)} %add.270), channel_id=1, source_target_pairs={{0,8},{4,12},{8,0},{12,4},{16,24},{20,28},{24,16},{28,20},{32,40},... | collective-permute-start | bytes 49928 | tf_op jit(solution)/shard_map/ppermute | solution.py:61
  112.8 4.8 %collective-permute-start.22 = (f32[64,65]{1,0:T(8,128)S(1)}, f32[64,65]{1,0:T(8,128)S(1)}, u32[]{:S(2)}, u32[]{:S(2)}) collective-permute-start(f32[64,65]{1,0:T(8,128)S(1)} %add.271), channel_id=1, source_target_pairs={{0,16},{4,20},{8,24},{12,28},{16,0},{20,4},{24,8},{28,12},{32,48},... | collective-permute-start | bytes 49928 | tf_op jit(solution)/shard_map/ppermute | solution.py:61
  117.6 6.0 %collective-permute-start.23 = (f32[64,65]{1,0:T(8,128)S(1)}, f32[64,65]{1,0:T(8,128)S(1)}, u32[]{:S(2)}, u32[]{:S(2)}) collective-permute-start(f32[64,65]{1,0:T(8,128)S(1)} %add.272), channel_id=1, source_target_pairs={{0,48},{4,52},{8,56},{12,60},{16,32},{20,36},{24,40},{28,44},{32,1... | collective-permute-start | bytes 49928 | tf_op jit(solution)/shard_map/ppermute | solution.py:61

commit v2 on v1

v2 whole, which is shorter than its diff:
```python
import jax
import jax.numpy as jnp
import numpy as np
from jax import lax
from jax.experimental import pallas as pl
from jax.experimental.pallas import tpu as pltpu
from jax.sharding import PartitionSpec as P

F32 = jnp.float32
BF16 = jnp.bfloat16
MEMBERS = 64
BLOCKS = 8
ROWS = 8
COLS = 128
HALO = 3
EXT = ROWS + 2 * HALO
WIDE = 9
OBS = 256
FIELDS = 3
EDGE = FIELDS * HALO * MEMBERS


def vmem(count):
    return [pl.BlockSpec(memory_space=pltpu.VMEM)] * count


def lanes():
    return lax.broadcasted_iota(jnp.int32, (8, COLS), 1)


def turn(value, shift):
    shift = shift % COLS
    return value if shift == 0 else pltpu.roll(value, shift, 1)


def spread(row):
    return jnp.broadcast_to(row, (8, COLS))


def arrange(x_ref, depth_ref, land_ref, start_ref, geo_ref, near_ref, far_ref):
    odd = lax.rem(lax.axis_index("gx"), 2)
    land = land_ref[...].astype(F32)
    geo_ref[0] = 0.125 * depth_ref[...].astype(F32) * land
    geo_ref[1] = land
    for f in range(FIELDS):
        for r in range(ROWS):
            value = x_ref[pl.ds(f * MEMBERS * ROWS + r, MEMBERS, stride=ROWS), :]
            start_ref[f, r] = value * land[r : r + 1, :]
    low = (ROWS - HALO) * (1 - odd)
    for target, first in ((near_ref, low), (far_ref, (ROWS - HALO) - low)):
        for f in range(FIELDS):
            for r in range(HALO):
                at = (f * HALO + r) * MEMBERS
                target[at : at + MEMBERS, :] = start_ref[f, first + r]
        for g in range(2):
            for r in range(HALO):
                at = EDGE + g * HALO + r
                target[at : at + 1, :] = geo_ref[g, pl.ds(first + r, 1), :]
        target[EDGE + 6 : EDGE + 8, :] = jnp.zeros((2, COLS), F32)


def strips(start_ref, geo_ref, near_ref, far_ref, halo_ref, wide_ref, left_ref, right_ref, a_ref, b_ref):
    odd_x = lax.rem(lax.axis_index("gx"), 2) == 1
    odd_y = lax.rem(lax.axis_index("gy"), 2) == 1
    lane = lanes()
    shifted = lax.rem(lane + HALO, COLS)
    for f in range(FIELDS):
        for r in range(HALO):
            at = slice((f * HALO + r) * MEMBERS, (f * HALO + r + 1) * MEMBERS)
            near, far = near_ref[at, :], far_ref[at, :]
            halo_ref[f, r] = jnp.where(odd_x, near, far)
            halo_ref[f, HALO + r] = jnp.where(odd_x, far, near)
    near, far = near_ref[EDGE : EDGE + 8, :], far_ref[EDGE : EDGE + 8, :]
    above, below = jnp.where(odd_x, near, far), jnp.where(odd_x, far, near)
    for g in range(2):
        at = slice(g * HALO, (g + 1) * HALO)
        wide_ref[g, :HALO] = above[at]
        wide_ref[g, HALO : HALO + ROWS] = geo_ref[g]
        wide_ref[g, HALO + ROWS :] = below[at]

    def put(packed, own, f, place):
        to_left, to_right = packed
        left, right = own
        left_ref[place] = left
        right_ref[place] = right
        mine = (lax.rem(lane, WIDE) // HALO) == f
        to_left = jnp.where(mine, turn(left, HALO * f - HALO), to_left)
        to_right = jnp.where(mine, turn(right, HALO * f), to_right)
        return to_left, to_right

    def own_columns(row_of):
        left = jnp.zeros((8, COLS), F32)
        right = jnp.zeros((8, COLS), F32)
        for r in range(EXT):
            value = turn(row_of(r), WIDE * r + HALO)
            left = jnp.where((lane // WIDE == r) & (lax.rem(lane, WIDE) >= HALO), value, left)
            right = jnp.where((shifted // WIDE == r) & (lax.rem(shifted, WIDE) < 2 * HALO), value, right)
        return left, right

    def send(place, packed):
        to_left, to_right = packed
        a_ref[place] = jnp.where(odd_y, to_left, to_right)
        b_ref[place] = jnp.where(odd_y, to_right, to_left)

    def block(m, carry):
        at = pl.ds(pl.multiple_of(m * 8, 8), 8)
        packed = (jnp.zeros((8, COLS), F32),) * 2
        for f in range(FIELDS):

            def row_of(r):
                if r < HALO:
                    return halo_ref[f, r, at, :]
                if r < HALO + ROWS:
                    return start_ref[f, r - HALO, at, :]
                return halo_ref[f, r - ROWS, at, :]

            packed = put(packed, own_columns(row_of), f, f * BLOCKS + m)
        send(m, packed)
        return carry

    lax.fori_loop(0, BLOCKS, block, 0)
    packed = (jnp.zeros((8, COLS), F32),) * 2
    for g in range(2):
        packed = put(packed, own_columns(lambda r: spread(wide_ref[g, r : r + 1, :])), g, FIELDS * BLOCKS + g)
    send(BLOCKS, packed)


def section(h, u, v, depth):
    damp = 0.05 * h
    half = 0.5 * h
    east, north = depth * u, depth * v
    us, vs = 0.05 * u, 0.05 * v
    return dict(
        up=(damp - east, us - half, vs),
        down=(damp + east, us + half, vs),
        back=(damp - north, us, vs - half),
        ahead=(damp + north, us, vs + half),
        here=(-0.2 * h, 0.2 * (v - u), -0.2 * (u + v)),
    )


def tendency(up, down, back, ahead, here):
    return [a + b + c + d + e for a, b, c, d, e in zip(up, down, back, ahead, here)]


def combine(stage, first, old, change):
    new = old + change
    if stage == 0:
        return new
    if stage == 1:
        return 0.75 * first + 0.25 * new
    return (1.0 / 3.0) * first + (2.0 / 3.0) * new


def forecast(
    start_ref, halo_ref, wide_ref, left_ref, right_ref, a_ref, b_ref, cells_ref, values_ref, error_ref,
    anomaly_ref, mean_ref, part_ref, geo, s1, s2, total, seen,
):
    odd_y = lax.rem(lax.axis_index("gy"), 2) == 1
    lane = lanes()
    column = lax.rem(lane, WIDE)
    inner = (lane < HALO) | (lane >= COLS - HALO)
    for r in range(EXT):
        geo[0, r] = spread(wide_ref[0, r : r + 1, :])
        geo[1, r] = spread(0.3 * wide_ref[1, r : r + 1, :])

    def sides(place, f, own):
        a, b = a_ref[place], b_ref[place]
        from_left, from_right = jnp.where(odd_y, a, b), jnp.where(odd_y, b, a)
        left = jnp.where(column < HALO, turn(from_left, -HALO * f), left_ref[own])
        right = jnp.where(
            (column >= HALO) & (column < 2 * HALO), turn(from_right, HALO - HALO * f), right_ref[own]
        )
        return left, right

    depth_sides = sides(BLOCKS, 0, FIELDS * BLOCKS)
    land_sides = [0.3 * value for value in sides(BLOCKS, 1, FIELDS * BLOCKS + 1)]
    total[...] = jnp.zeros_like(total)
    cell = jnp.broadcast_to(cells_ref[...], (8, OBS))
    cell_row, cell_col = cell // COLS, lax.rem(cell, COLS)

    def block(m, carry):
        at = pl.ds(pl.multiple_of(m * 8, 8), 8)

        def row_of(f, r):
            if r < HALO:
                return halo_ref[f, r, at, :]
            if r < HALO + ROWS:
                return start_ref[f, r - HALO, at, :]
            return halo_ref[f, r - ROWS, at, :]

        strip = []
        fields = [sides(m, f, f * BLOCKS + m) for f in range(FIELDS)]
        for side in range(2):
            first = [fields[f][side] for f in range(FIELDS)]
            now = first
            for stage in range(3):
                part = section(*now, depth_sides[side])
                change = tendency(
                    [turn(value, -WIDE) for value in part["up"]],
                    [turn(value, WIDE) for value in part["down"]],
                    [turn(value, -1) for value in part["back"]],
                    [turn(value, 1) for value in part["ahead"]],
                    part["here"],
                )
                now = [combine(stage, first[f], now[f], land_sides[side] * change[f]) for f in range(FIELDS)]
            strip.append(now)
        edge = [jnp.where(column >= HALO, strip[0][f], strip[1][f]) for f in range(FIELDS)]

        heights = []
        for stage in range(3):
            read = row_of if stage == 0 else (lambda f, r, ref=(s1, s2)[stage - 1]: ref[f, r])
            known = {}

            def part_of(r):
                if r not in known:
                    known[r] = section(*[read(f, r) for f in range(FIELDS)], geo[0, r])
                return known[r]

            for r in range(stage + 1, EXT - stage - 1):
                mine = part_of(r)
                change = tendency(
                    part_of(r + 1)["up"],
                    part_of(r - 1)["down"],
                    [turn(value, -1) for value in mine["back"]],
                    [turn(value, 1) for value in mine["ahead"]],
                    mine["here"],
                )
                for f in range(FIELDS):
                    new = combine(stage, row_of(f, r), read(f, r), geo[1, r] * change[f])
                    if stage < 2:
                        (s1, s2)[stage][f, r] = new
                    else:
                        new = jnp.where(inner, turn(edge[f], -(WIDE * r + HALO)), new)
                        anomaly_ref[f, r - HALO, at, :] = new
                        total[f * ROWS + r - HALO] += new
                        if f == 0:
                            heights.append(new)
        for part in range(OBS // COLS):
            cut = slice(part * COLS, (part + 1) * COLS)
            got = jnp.zeros((8, COLS), F32)
            for r in range(ROWS):
                picked = jnp.take_along_axis(heights[r], cell_col[:, cut], axis=1)
                got = jnp.where(cell_row[:, cut] == r, picked, got)
            seen[at, cut] = got
        return carry

    lax.fori_loop(0, BLOCKS, block, 0)

    everything = seen[...]
    obs_mean = jnp.sum(everything, axis=0, keepdims=True) * (1.0 / MEMBERS)
    error = error_ref[...]
    scaled = (everything - obs_mean) * (1.0 / (error * np.sqrt(np.float32(MEMBERS - 1))))
    innovation = (values_ref[...] - obs_mean) / error
    product = lambda a: lax.dot_general(
        a, scaled, (((1,), (1,)), ((), ())), precision=lax.Precision.HIGHEST, preferred_element_type=F32
    )
    gram = product(scaled)
    part_ref[:32, :MEMBERS] = gram[:32]
    part_ref[:32, MEMBERS:] = gram[32:]
    part_ref[32:, :MEMBERS] = product(jnp.broadcast_to(innovation, (8, OBS)))
    part_ref[32:, MEMBERS:] = jnp.zeros((8, MEMBERS), F32)

    for k in range(FIELDS * ROWS):
        f, r = divmod(k, ROWS)
        mean = jnp.sum(total[k], axis=0, keepdims=True) * (1.0 / MEMBERS)
        mean_ref[k : k + 1, :] = mean
        anomaly_ref[f, r] = anomaly_ref[f, r] - mean


def analyse(sum_ref, anomaly_ref, mean_ref, out_ref):
    lane = lanes()
    sub = lax.broadcasted_iota(jnp.int32, (8, COLS), 0)
    table = []
    for b in range(BLOCKS):
        if b < 4:
            value = sum_ref[b * 8 : b * 8 + 8, :]
        else:
            value = turn(sum_ref[(b - 4) * 8 : (b - 4) * 8 + 8, :], MEMBERS)
        value = jnp.where(lane < MEMBERS, value, 0.0)
        one = (lane == sub + 8 * b) | (lane == sub + 8 * b + MEMBERS)
        table.append(value + jnp.where(one, 1.0, 0.0))
    pivots = [jnp.ones((8, COLS), F32) for _ in range(BLOCKS)]
    for j in range(MEMBERS):
        b, s = divmod(j, 8)
        row = spread(table[b][s : s + 1, :])
        pivot = jnp.broadcast_to(row[:, j : j + 1], (8, COLS))
        pivots[b] = jnp.where(sub == s, pivot, pivots[b])
        row = row * (1.0 / pivot)
        for i in range(b, BLOCKS):
            factor = jnp.broadcast_to(table[i][:, j : j + 1], (8, COLS))
            if i == b:
                factor = jnp.where(sub > s, factor, 0.0)
            table[i] = table[i] - factor * row
    inverse = [
        jnp.where(lane < MEMBERS, turn(table[b] * lax.rsqrt(pivots[b]), MEMBERS), 0.0) for b in range(BLOCKS)
    ]
    projection = spread(sum_ref[32:33, :])
    weights = jnp.zeros((8, COLS), F32)
    for b in range(BLOCKS):
        weights = weights + inverse[b] * jnp.sum(inverse[b] * projection, axis=1, keepdims=True)
    weights = jnp.sum(weights, axis=0, keepdims=True) / np.sqrt(np.float32(MEMBERS - 1))
    transform = jnp.concatenate(inverse, axis=0)[:, :MEMBERS] + weights[:, :MEMBERS]
    high = transform.astype(BF16)
    low = (transform - high.astype(F32)).astype(BF16)
    taps = jnp.concatenate([high, low, high], axis=1)
    for f in range(FIELDS):
        for r in range(0, ROWS, 2):
            value = jnp.concatenate([anomaly_ref[f, r], anomaly_ref[f, r + 1]], axis=1)
            big = value.astype(BF16)
            small = (value - big.astype(F32)).astype(BF16)
            mixed = jnp.dot(taps, jnp.concatenate([big, big, small], axis=0), preferred_element_type=F32)
            for q in range(2):
                k = f * ROWS + r + q
                out_ref[pl.ds(f * MEMBERS * ROWS + r + q, MEMBERS, stride=ROWS), :] = (
                    mean_ref[k : k + 1, :] + mixed[:, q * COLS : (q + 1) * COLS]
                )


def swap(value, axis, pairs):
    return lax.ppermute(value, axis, [(a, b) for a, b in pairs] + [(b, a) for a, b in pairs])


def pairs_of(count, first):
    return [(i, i + 1) for i in range(first, count - 1, 2)]


def summed(part):
    for axis, flips in (("gx", (1,)), ("gy", (1, 3)), ("gx", (16, 48, 2, 4, 12))):
        count = lax.axis_size(axis)
        for flip in flips:
            part = part + lax.ppermute(part, axis, [(i, i ^ flip) for i in range(count)])
    return part


def shape(*sizes):
    return jax.ShapeDtypeStruct(sizes, F32)


def local(members_state, depth_level, land_mask, obs_cells, obs_values, obs_error):
    x = members_state.reshape(FIELDS * MEMBERS * ROWS, COLS)
    start, geo, near, far = pl.pallas_call(
        arrange,
        out_shape=(shape(FIELDS, ROWS, MEMBERS, COLS), shape(2, ROWS, COLS), shape(EDGE + 8, COLS), shape(EDGE + 8, COLS)),
        in_specs=vmem(3),
        out_specs=tuple(vmem(4)),
        name="arrange",
    )(x, depth_level, land_mask)
    near = swap(near, "gx", pairs_of(64, 0))
    far = swap(far, "gx", pairs_of(64, 1))
    tile = shape(BLOCKS + 1, 8, COLS)
    halo, wide, left, right, a, b = pl.pallas_call(
        strips,
        out_shape=(
            shape(FIELDS, 2 * HALO, MEMBERS, COLS), shape(2, EXT, COLS),
            shape(FIELDS * BLOCKS + 2, 8, COLS), shape(FIELDS * BLOCKS + 2, 8, COLS), tile, tile,
        ),
        in_specs=vmem(4),
        out_specs=tuple(vmem(6)),
        name="strips",
    )(start, geo, near, far)
    a = swap(a, "gy", pairs_of(4, 0))
    b = swap(b, "gy", pairs_of(4, 1))
    anomaly, mean, part = pl.pallas_call(
        forecast,
        out_shape=(shape(FIELDS, ROWS, MEMBERS, COLS), shape(FIELDS * ROWS, COLS), shape(40, COLS)),
        in_specs=vmem(10),
        out_specs=tuple(vmem(3)),
        scratch_shapes=[
            pltpu.VMEM((2, EXT, 8, COLS), F32),
            pltpu.VMEM((FIELDS, EXT, 8, COLS), F32),
            pltpu.VMEM((FIELDS, EXT, 8, COLS), F32),
            pltpu.VMEM((FIELDS * ROWS, 8, COLS), F32),
            pltpu.VMEM((MEMBERS, OBS), F32),
        ],
        name="forecast",
    )(
        start, halo, wide, left, right, a, b,
        obs_cells.reshape(1, OBS), obs_values.reshape(1, OBS), obs_error.reshape(1, OBS),
    )
    out = pl.pallas_call(
        analyse,
        out_shape=shape(FIELDS * MEMBERS * ROWS, COLS),
        in_specs=vmem(3),
        out_specs=vmem(1)[0],
        name="analyse",
    )(summed(part), anomaly, mean)
    return out.reshape(FIELDS, MEMBERS, ROWS, COLS)


def solution(mesh):
    placed = (
        P(None, None, "gx", "gy"),
        P("gx", "gy"),
        P("gx", "gy"),
        P("gx", "gy", None),
        P("gx", "gy", None),
        P("gx", "gy", None),
    )
    return jax.shard_map(
        local, mesh=mesh, in_specs=placed, out_specs=P(None, None, "gx", "gy"), check_vma=False
    )
```

time: 141 us -> 79.3 us (0.56)
  starting transfers between devices: 53.6 us -> 19.2 us
  Pallas kernels: 0 us -> 24.2 us
  waiting for transfers between devices: 55.7 us -> 33 us
  other arithmetic: 21.6 us -> 1.36 us
  matrix products: 3.83 us -> 0 us
  local copies, waits for them, and re-layouts: 4.7 us -> 1.34 us
    ppermute x16 -> x4, starting transfers between devices: 46.2 us -> 10.2 us  [swap(): lax.ppermute(value, axis, [(a, b) for a, b in pairs] + [(b, a) for a, b i...]
    pallas_call x0 -> x4, Pallas kernels: none -> 24.2 us  [the longest x1 10.8 us: local(): pl.pallas_call(analyse, out_shape=shape(FIELDS * MEMBERS * ROWS, COLS), i...]
    ppermute x16 -> x4, waiting for transfers between devices: 27.3 us -> 6.65 us  [swap(): lax.ppermute(value, axis, [(a, b) for a, b in pairs] + [(b, a) for a, b i...]
    another operation x14 -> x0, other arithmetic: 16.4 us -> none  [the longest x3 6.52 us: local(): lower = jnp.linalg.cholesky(eye + gram)]
    dot_general x3 -> x0, matrix products: 3.27 us -> none  [the longest x1 2.11 us: local(): jnp.einsum('km,fkxy->fmxy', transform, sample_deviations, precision=lax.P...]
    ppermute x8, waiting for transfers between devices: 28.5 us -> 26.3 us  [summed(): lax.ppermute(part, axis, [(i, i ^ flip) for i in range(count)])]
    reduce_sum x2 -> x0, other arithmetic: 1.89 us -> none  [the longest x1 1.71 us: local(): sample_average = jnp.mean(prior_model_vector, axis=1, keepdims=True)]
    ppermute x8, starting transfers between devices: 7.44 us -> 9 us  [summed(): lax.ppermute(part, axis, [(i, i ^ flip) for i in range(count)])]
  transfers between devices with their start and end apart: 24 -> 12, of which waited for: 18 -> 10; matrix products, arithmetic and copies ran while one was open for 2% -> 0% of each run, Pallas kernels for 0% -> 0%
where the time goes in v2:
time: 79.3 us; the launch traced here: 79.1 us
  waiting for transfers between devices  33 us (42%)
  Pallas kernels  24.2 us (31%)
  starting transfers between devices  19.2 us (24%)
  other arithmetic  1.36 us (2%)
  local copies, waits for them, and re-layouts  1.34 us (2%)
    ppermute x8, waiting for transfers between devices, summed(): lax.ppermute(part, axis, [(i, i ^ flip) for i in range(count)])  26.3 us
    pallas_call x1, Pallas kernels, local(): pl.pallas_call(analyse, out_shape=shape(FIELDS * MEMBERS * ROWS, COLS), i...  10.8 us
    ppermute x4, starting transfers between devices, swap(): lax.ppermute(value, axis, [(a, b) for a, b in pairs] + [(b, a) for a, b i...  10.2 us
    ppermute x8, starting transfers between devices, summed(): lax.ppermute(part, axis, [(i, i ^ flip) for i in range(count)])  9 us
    pallas_call x1, Pallas kernels, local(): pl.pallas_call(forecast, out_shape=(shape(FIELDS, ROWS, MEMBERS, COLS), s...  7.14 us
    ppermute x4, waiting for transfers between devices, swap(): lax.ppermute(value, axis, [(a, b) for a, b in pairs] + [(b, a) for a, b i...  6.65 us
    pallas_call x1, Pallas kernels, local(): pl.pallas_call(strips, out_shape=(shape(FIELDS, 2 * HALO, MEMBERS, COLS),...  3.83 us
    pallas_call x1, Pallas kernels, local(): pl.pallas_call(arrange, out_shape=(shape(FIELDS, ROWS, MEMBERS, COLS), sh...  2.36 us
  transfers between devices with their start and end apart: 12, of which 10 were waited for; matrix products, arithmetic and copies ran while one was open for 0% of the time, Pallas kernels for 0%

profile of v2, /device:TPU:24, one launch (start us, length us, event | category | flops | bytes accessed | tf_op | source)
XLA Modules:
  0.0 79.1 jit_solution(15942573187546954291)
XLA Ops:
  0.0 2.4 %arrange.1 = (f32[3,8,64,128]{3,2,1,0:T(8,128)}, f32[2,8,128]{2,1,0:T(8,128)}, f32[584,128]{1,0:T(8,128)}, f32[584,128]{1,0:T(8,128)}) custom-call(f32[1536,128]{1,0:T(8,128)} %bitcast.5, s32[8,128]{1,0:T(8,128)} %depth_ref.1, s32[8,128]{1,0:T(8,128)} %land_ref.1), custom_call_target="tpu_custom_call" | custom-call | tf_op jit(solution)/shard_map/arrange/pallas_call | solution.py:342
  2.4 0.0 collective-permute-start
  2.4 8.0 %collective-permute-start.1 = (f32[584,128]{1,0:T(8,128)}, f32[584,128]{1,0:T(8,128)S(1)}, u32[]{:S(2)}, u32[]{:S(2)}) collective-permute-start(f32[584,128]{1,0:T(8,128)} %get-tuple-element.21), channel_id=1, source_target_pairs={{4,8},{12,16},{20,24},{28,32},{36,40},{44,48},{52,56},{60,64},{68,... | collective-permute-start | bytes 897032 | tf_op jit(solution)/shard_map/ppermute | solution.py:321
  10.4 0.0 collective-permute-done.near_ref
  10.4 4.6 %collective-permute-done.1.far_ref = f32[584,128]{1,0:T(8,128)S(1)} collective-permute-done((f32[584,128]{1,0:T(8,128)}, f32[584,128]{1,0:T(8,128)S(1)}, u32[]{:S(2)}, u32[]{:S(2)}) %collective-permute-start.1) | collective-permute-done | bytes 299040 | tf_op jit(solution)/shard_map/ppermute | solution.py:321
  15.1 0.7 copy-done.1
  15.8 3.8 %strips.1 = (f32[3,6,64,128]{3,2,1,0:T(8,128)}, f32[2,14,128]{2,1,0:T(8,128)}, f32[26,8,128]{2,1,0:T(8,128)}, f32[26,8,128]{2,1,0:T(8,128)}, f32[9,8,128]{2,1,0:T(8,128)}, /*index=5*/f32[9,8,128]{2,1,0:T(8,128)}) custom-call(f32[3,8,64,128]{3,2,1,0:T(8,128)} %get-tuple-element.18.start_ref, f32[2,8,128]{2,1,0:T(8,128)} %get-tuple-element.19.geo_ref, ...), custom_call_target="tpu_custom_call" | custom-call | tf_op jit(solution)/shard_map/strips/pallas_call | solution.py:352
  19.6 1.5 %collective-permute-start.2 = (f32[9,8,128]{2,1,0:T(8,128)}, f32[9,8,128]{2,1,0:T(8,128)S(1)}, u32[]{:S(2)}, u32[]{:S(2)}) collective-permute-start(f32[9,8,128]{2,1,0:T(8,128)} %get-tuple-element.26), channel_id=1, source_target_pairs={{0,1},{2,3},{1,0},{3,2},{4,5},{6,7},{5,4},{7,6},{8,9},{10,11},{9,8... | collective-permute-start | bytes 110600 | tf_op jit(solution)/shard_map/ppermute | solution.py:321
  21.1 0.7 collective-permute-start.3
  21.8 2.0 %collective-permute-done.2.a_ref = f32[9,8,128]{2,1,0:T(8,128)S(1)} collective-permute-done((f32[9,8,128]{2,1,0:T(8,128)}, f32[9,8,128]{2,1,0:T(8,128)S(1)}, u32[]{:S(2)}, u32[]{:S(2)}) %collective-permute-start.2) | collective-permute-done | bytes 36896 | tf_op jit(solution)/shard_map/ppermute | solution.py:321
  23.8 0.6 copy-done.2
  24.4 0.0 copy-done.3
  24.4 7.1 %forecast.1 = (f32[3,8,64,128]{3,2,1,0:T(8,128)}, f32[24,128]{1,0:T(8,128)}, f32[40,128]{1,0:T(8,128)}) custom-call(f32[3,8,64,128]{3,2,1,0:T(8,128)} %get-tuple-element.18.start_ref, f32[3,6,64,128]{3,2,1,0:T(8,128)} %get-tuple-element.22.halo_ref, f32[2,14,128]{2,1,0:T(8,128)} %get-tuple-element.23.wide_ref, f32[26,8,128]{2,1,0:T(8,128)} %get-tuple-element.24.left_ref, ...), custom_call_target="tpu_custom_call" | custom-call | tf_op jit(solution)/shard_map/forecast/pallas_call | solution.py:364
  31.5 0.0 collective-permute-start.4
  31.5 1.4 %collective-permute-done.4 = f32[40,128]{1,0:T(8,128)S(1)} collective-permute-done((f32[40,128]{1,0:T(8,128)}, f32[40,128]{1,0:T(8,128)S(1)}, u32[]{:S(2)}, u32[]{:S(2)}) %collective-permute-start.4) | collective-permute-done | bytes 20512 | tf_op jit(solution)/shard_map/ppermute | solution.py:332
  32.9 0.7 add.24
  33.7 4.0 %collective-permute-start.5 = (f32[40,128]{1,0:T(8,128)S(1)}, f32[40,128]{1,0:T(8,128)S(1)}, u32[]{:S(2)}, u32[]{:S(2)}) collective-permute-start(f32[40,128]{1,0:T(8,128)S(1)} %add.24), channel_id=1, source_target_pairs={{0,1},{1,0},{2,3},{3,2},{4,5},{5,4},{6,7},{7,6},{8,9},{9,8},{10,11... | collective-permute-start | bytes 61448 | tf_op jit(solution)/shard_map/ppermute | solution.py:332
  37.7 1.8 %collective-permute-done.5 = f32[40,128]{1,0:T(8,128)S(1)} collective-permute-done((f32[40,128]{1,0:T(8,128)S(1)}, f32[40,128]{1,0:T(8,128)S(1)}, u32[]{:S(2)}, u32[]{:S(2)}) %collective-permute-start.5) | collective-permute-done | bytes 20512 | tf_op jit(solution)/shard_map/ppermute | solution.py:332
  39.5 2.6 %collective-permute-start.6 = (f32[40,128]{1,0:T(8,128)S(1)}, f32[40,128]{1,0:T(8,128)S(1)}, u32[]{:S(2)}, u32[]{:S(2)}) collective-permute-start(f32[40,128]{1,0:T(8,128)S(1)} %add.25), channel_id=1, source_target_pairs={{0,3},{1,2},{2,1},{3,0},{4,7},{5,6},{6,5},{7,4},{8,11},{9,10},{10,... | collective-permute-start | bytes 61448 | tf_op jit(solution)/shard_map/ppermute | solution.py:332
  42.1 2.4 %collective-permute-done.6 = f32[40,128]{1,0:T(8,128)S(1)} collective-permute-done((f32[40,128]{1,0:T(8,128)S(1)}, f32[40,128]{1,0:T(8,128)S(1)}, u32[]{:S(2)}, u32[]{:S(2)}) %collective-permute-start.6) | collective-permute-done | bytes 20512 | tf_op jit(solution)/shard_map/ppermute | solution.py:332
  44.5 0.4 collective-permute-start.7
  44.9 3.3 %collective-permute-done.7 = f32[40,128]{1,0:T(8,128)S(1)} collective-permute-done((f32[40,128]{1,0:T(8,128)S(1)}, f32[40,128]{1,0:T(8,128)S(1)}, u32[]{:S(2)}, u32[]{:S(2)}) %collective-permute-start.7) | collective-permute-done | bytes 20512 | tf_op jit(solution)/shard_map/ppermute | solution.py:332
  48.3 0.0 collective-permute-start.8
  48.3 5.0 %collective-permute-done.8 = f32[40,128]{1,0:T(8,128)S(1)} collective-permute-done((f32[40,128]{1,0:T(8,128)S(1)}, f32[40,128]{1,0:T(8,128)S(1)}, u32[]{:S(2)}, u32[]{:S(2)}) %collective-permute-start.8) | collective-permute-done | bytes 20512 | tf_op jit(solution)/shard_map/ppermute | solution.py:332
  53.3 0.0 collective-permute-start.9
  53.3 3.8 %collective-permute-done.9 = f32[40,128]{1,0:T(8,128)S(1)} collective-permute-done((f32[40,128]{1,0:T(8,128)S(1)}, f32[40,128]{1,0:T(8,128)S(1)}, u32[]{:S(2)}, u32[]{:S(2)}) %collective-permute-start.9) | collective-permute-done | bytes 20512 | tf_op jit(solution)/shard_map/ppermute | solution.py:332
  57.0 0.0 collective-permute-start.10
  57.1 4.7 %collective-permute-done.10 = f32[40,128]{1,0:T(8,128)S(1)} collective-permute-done((f32[40,128]{1,0:T(8,128)S(1)}, f32[40,128]{1,0:T(8,128)S(1)}, u32[]{:S(2)}, u32[]{:S(2)}) %collective-permute-start.10) | collective-permute-done | bytes 20512 | tf_op jit(solution)/shard_map/ppermute | solution.py:332
  61.7 1.9 %collective-permute-start.11 = (f32[40,128]{1,0:T(8,128)S(1)}, f32[40,128]{1,0:T(8,128)S(1)}, u32[]{:S(2)}, u32[]{:S(2)}) collective-permute-start(f32[40,128]{1,0:T(8,128)S(1)} %add.30), channel_id=1, source_target_pairs={{0,48},{4,52},{8,56},{12,60},{16,32},{20,36},{24,40},{28,44},{32,1... | collective-permute-start | bytes 61448 | tf_op jit(solution)/shard_map/ppermute | solution.py:332
  63.6 4.0 %collective-permute-done.11 = f32[40,128]{1,0:T(8,128)S(1)} collective-permute-done((f32[40,128]{1,0:T(8,128)S(1)}, f32[40,128]{1,0:T(8,128)S(1)}, u32[]{:S(2)}, u32[]{:S(2)}) %collective-permute-start.11) | collective-permute-done | bytes 20512 | tf_op jit(solution)/shard_map/ppermute | solution.py:332
  67.6 0.6 add.31.sum_ref
  68.2 10.8 %analyse.1 = f32[1536,128]{1,0:T(8,128)} custom-call(f32[40,128]{1,0:T(8,128)} %add.31.sum_ref, f32[3,8,64,128]{3,2,1,0:T(8,128)} %get-tuple-element.29.anomaly_ref, f32[24,128]{1,0:T(8,128)} %get-tuple-element.30.mean_ref), custom_call_target="tpu_custom_call" | custom-call | tf_op jit(solution)/shard_map/analyse/pallas_call | solution.py:381
  (12 shorter events, 0.0 us)
Async XLA Ops:
  2.4 8.1 %collective-permute-start = (f32[584,128]{1,0:T(8,128)}, f32[584,128]{1,0:T(8,128)S(1)}, u32[]{:S(2)}, u32[]{:S(2)}) collective-permute-start(f32[584,128]{1,0:T(8,128)} %get-tuple-element.20), channel_id=1, source_target_pairs={{0,4},{8,12},{16,20},{24,28},{32,36},{40,44},{48,52},{56,60},{64,6... | collective-permute-start | bytes 897032 | tf_op jit(solution)/shard_map/ppermute | solution.py:321
  2.4 12.7 %collective-permute-start.1 = (f32[584,128]{1,0:T(8,128)}, f32[584,128]{1,0:T(8,128)S(1)}, u32[]{:S(2)}, u32[]{:S(2)}) collective-permute-start(f32[584,128]{1,0:T(8,128)} %get-tuple-element.21), channel_id=1, source_target_pairs={{4,8},{12,16},{20,24},{28,32},{36,40},{44,48},{52,56},{60,64},{68,... | collective-permute-start | bytes 897032 | tf_op jit(solution)/shard_map/ppermute | solution.py:321
  10.4 4.6 %copy-start = (f32[584,128]{1,0:T(8,128)}, f32[584,128]{1,0:T(8,128)S(1)}, u32[]{:S(2)}) copy-start(f32[584,128]{1,0:T(8,128)S(1)} %collective-permute-done.near_ref) | copy-start | bytes 897028
  15.1 0.7 copy-start.1
  19.6 4.2 %collective-permute-start.2 = (f32[9,8,128]{2,1,0:T(8,128)}, f32[9,8,128]{2,1,0:T(8,128)S(1)}, u32[]{:S(2)}, u32[]{:S(2)}) collective-permute-start(f32[9,8,128]{2,1,0:T(8,128)} %get-tuple-element.26), channel_id=1, source_target_pairs={{0,1},{2,3},{1,0},{3,2},{4,5},{6,7},{5,4},{7,6},{8,9},{10,11},{9,8... | collective-permute-start | bytes 110600 | tf_op jit(solution)/shard_map/ppermute | solution.py:321
  21.1 2.7 %collective-permute-start.3 = (f32[9,8,128]{2,1,0:T(8,128)}, f32[9,8,128]{2,1,0:T(8,128)S(1)}, u32[]{:S(2)}, u32[]{:S(2)}) collective-permute-start(f32[9,8,128]{2,1,0:T(8,128)} %get-tuple-element.27), channel_id=1, source_target_pairs={{1,2},{2,1},{5,6},{6,5},{9,10},{10,9},{13,14},{14,13},{17,18},{18,... | collective-permute-start | bytes 110600 | tf_op jit(solution)/shard_map/ppermute | solution.py:321
  23.8 0.6 copy-start.2
  23.8 0.6 copy-start.3
  31.5 1.4 %collective-permute-start.4 = (f32[40,128]{1,0:T(8,128)}, f32[40,128]{1,0:T(8,128)S(1)}, u32[]{:S(2)}, u32[]{:S(2)}) collective-permute-start(f32[40,128]{1,0:T(8,128)} %get-tuple-element.28), channel_id=1, source_target_pairs={{0,4},{4,0},{8,12},{12,8},{16,20},{20,16},{24,28},{28,24},{32,36},... | collective-permute-start | bytes 61448 | tf_op jit(solution)/shard_map/ppermute | solution.py:332
  33.7 5.8 %collective-permute-start.5 = (f32[40,128]{1,0:T(8,128)S(1)}, f32[40,128]{1,0:T(8,128)S(1)}, u32[]{:S(2)}, u32[]{:S(2)}) collective-permute-start(f32[40,128]{1,0:T(8,128)S(1)} %add.24), channel_id=1, source_target_pairs={{0,1},{1,0},{2,3},{3,2},{4,5},{5,4},{6,7},{7,6},{8,9},{9,8},{10,11... | collective-permute-start | bytes 61448 | tf_op jit(solution)/shard_map/ppermute | solution.py:332
  39.5 5.0 %collective-permute-start.6 = (f32[40,128]{1,0:T(8,128)S(1)}, f32[40,128]{1,0:T(8,128)S(1)}, u32[]{:S(2)}, u32[]{:S(2)}) collective-permute-start(f32[40,128]{1,0:T(8,128)S(1)} %add.25), channel_id=1, source_target_pairs={{0,3},{1,2},{2,1},{3,0},{4,7},{5,6},{6,5},{7,4},{8,11},{9,10},{10,... | collective-permute-start | bytes 61448 | tf_op jit(solution)/shard_map/ppermute | solution.py:332
  44.5 3.8 %collective-permute-start.7 = (f32[40,128]{1,0:T(8,128)S(1)}, f32[40,128]{1,0:T(8,128)S(1)}, u32[]{:S(2)}, u32[]{:S(2)}) collective-permute-start(f32[40,128]{1,0:T(8,128)S(1)} %add.26), channel_id=1, source_target_pairs={{0,64},{4,68},{8,72},{12,76},{16,80},{20,84},{24,88},{28,92},{32,9... | collective-permute-start | bytes 61448 | tf_op jit(solution)/shard_map/ppermute | solution.py:332
  48.3 5.0 %collective-permute-start.8 = (f32[40,128]{1,0:T(8,128)S(1)}, f32[40,128]{1,0:T(8,128)S(1)}, u32[]{:S(2)}, u32[]{:S(2)}) collective-permute-start(f32[40,128]{1,0:T(8,128)S(1)} %add.27), channel_id=1, source_target_pairs={{0,192},{4,196},{8,200},{12,204},{16,208},{20,212},{24,216},{28,22... | collective-permute-start | bytes 61448 | tf_op jit(solution)/shard_map/ppermute | solution.py:332
  53.3 3.8 %collective-permute-start.9 = (f32[40,128]{1,0:T(8,128)S(1)}, f32[40,128]{1,0:T(8,128)S(1)}, u32[]{:S(2)}, u32[]{:S(2)}) collective-permute-start(f32[40,128]{1,0:T(8,128)S(1)} %add.28), channel_id=1, source_target_pairs={{0,8},{4,12},{8,0},{12,4},{16,24},{20,28},{24,16},{28,20},{32,40},... | collective-permute-start | bytes 61448 | tf_op jit(solution)/shard_map/ppermute | solution.py:332
  57.0 4.7 %collective-permute-start.10 = (f32[40,128]{1,0:T(8,128)S(1)}, f32[40,128]{1,0:T(8,128)S(1)}, u32[]{:S(2)}, u32[]{:S(2)}) collective-permute-start(f32[40,128]{1,0:T(8,128)S(1)} %add.29), channel_id=1, source_target_pairs={{0,16},{4,20},{8,24},{12,28},{16,0},{20,4},{24,8},{28,12},{32,48},... | collective-permute-start | bytes 61448 | tf_op jit(solution)/shard_map/ppermute | solution.py:332
  61.7 5.9 %collective-permute-start.11 = (f32[40,128]{1,0:T(8,128)S(1)}, f32[40,128]{1,0:T(8,128)S(1)}, u32[]{:S(2)}, u32[]{:S(2)}) collective-permute-start(f32[40,128]{1,0:T(8,128)S(1)} %add.30), channel_id=1, source_target_pairs={{0,48},{4,52},{8,56},{12,60},{16,32},{20,36},{24,40},{28,44},{32,1... | collective-permute-start | bytes 61448 | tf_op jit(solution)/shard_map/ppermute | solution.py:332

commit v3 on v2

v3 whole, which is shorter than its diff:
```python
import jax
import jax.numpy as jnp
import numpy as np
from jax import lax
from jax.experimental import pallas as pl
from jax.experimental.pallas import tpu as pltpu
from jax.sharding import PartitionSpec as P

F32 = jnp.float32
BF16 = jnp.bfloat16
MEMBERS = 64
BLOCKS = 8
ROWS = 8
COLS = 128
HALO = 3
EXT = ROWS + 2 * HALO
WIDE = 9
OBS = 256
FIELDS = 3
EDGE = FIELDS * HALO * MEMBERS


def vmem(count):
    return [pl.BlockSpec(memory_space=pltpu.VMEM)] * count


def lanes():
    return lax.broadcasted_iota(jnp.int32, (8, COLS), 1)


def grid_sub():
    return lax.broadcasted_iota(jnp.int32, (8, COLS), 0)


def turn(value, shift):
    shift = shift % COLS
    return value if shift == 0 else pltpu.roll(value, shift, 1)


def spread(row):
    return jnp.broadcast_to(row, (8, COLS))


def arrange(x_hbm, depth_hbm, land_hbm, start_ref, geo_ref, near_ref, far_ref, x_ref, depth_ref, land_ref, sems):
    size = MEMBERS * ROWS
    loads = [
        pltpu.make_async_copy(land_hbm, land_ref, sems.at[0]),
        pltpu.make_async_copy(depth_hbm, depth_ref, sems.at[1]),
    ]
    for f in range(FIELDS):
        cut = pl.ds(f * size, size)
        loads.append(pltpu.make_async_copy(x_hbm.at[cut], x_ref.at[cut], sems.at[2 + f]))
    for load in loads:
        load.start()
    odd = lax.rem(lax.axis_index("gx"), 2)
    loads[0].wait()
    loads[1].wait()
    land = land_ref[...].astype(F32)
    geo_ref[0] = 0.125 * depth_ref[...].astype(F32) * land
    geo_ref[1] = land
    low = (ROWS - HALO) * (1 - odd)
    sends = ((near_ref, low), (far_ref, (ROWS - HALO) - low))
    for target, first in sends:
        for g in range(2):
            for r in range(HALO):
                at = EDGE + g * HALO + r
                target[at : at + 1, :] = geo_ref[g, pl.ds(first + r, 1), :]
        target[EDGE + 6 : EDGE + 8, :] = jnp.zeros((2, COLS), F32)
    for f in range(FIELDS):
        loads[2 + f].wait()
        for r in range(ROWS):
            value = x_ref[pl.ds(f * size + r, MEMBERS, stride=ROWS), :]
            start_ref[f, r] = value * land[r : r + 1, :]
        for target, first in sends:
            for r in range(HALO):
                at = (f * HALO + r) * MEMBERS
                target[at : at + MEMBERS, :] = start_ref[f, first + r]


def own_columns(row_of, rows, left, right):
    lane = lanes()
    shifted = lax.rem(lane + HALO, COLS)
    for r in rows:
        value = turn(row_of(r), WIDE * r + HALO)
        left = jnp.where((lane // WIDE == r) & (lax.rem(lane, WIDE) >= HALO), value, left)
        right = jnp.where((shifted // WIDE == r) & (lax.rem(shifted, WIDE) < 2 * HALO), value, right)
    return left, right


def interior(start_ref, geo_ref, left_ref, right_ref, c1_ref, c2_ref, c3_ref, geo):
    for r in range(ROWS):
        geo[0, r] = spread(geo_ref[0, r : r + 1, :])
        geo[1, r] = spread(0.3 * geo_ref[1, r : r + 1, :])
    blank = jnp.zeros((8, COLS), F32)
    inside = range(HALO, HALO + ROWS)

    def block(m, carry):
        at = pl.ds(pl.multiple_of(m * 8, 8), 8)
        for f in range(FIELDS):
            place = f * BLOCKS + m
            left_ref[place], right_ref[place] = own_columns(
                lambda r: start_ref[f, r - HALO, at, :], inside, blank, blank
            )

        def first(f, r):
            return start_ref[f, r, at, :]

        refs = (c1_ref, c2_ref, c3_ref)
        for stage in range(3):
            read = first if stage == 0 else (lambda f, r: refs[stage - 1][f, r - stage, at, :])

            def write(f, r, new):
                refs[stage][f, r - stage - 1, at, :] = new

            advance(stage, range(stage + 1, ROWS - stage - 1), first, read, geo, write)
        return carry

    lax.fori_loop(0, BLOCKS, block, 0)
    for g in range(2):
        place = FIELDS * BLOCKS + g
        left_ref[place], right_ref[place] = own_columns(
            lambda r: spread(geo_ref[g, r - HALO : r - HALO + 1, :]), inside, blank, blank
        )


def strips(near_ref, far_ref, geo_ref, own_left, own_right, halo_ref, wide_ref, left_ref, right_ref, a_ref, b_ref):
    odd_x = lax.rem(lax.axis_index("gx"), 2) == 1
    odd_y = lax.rem(lax.axis_index("gy"), 2) == 1
    field = lax.rem(lanes(), WIDE) // HALO
    outside = tuple(range(HALO)) + tuple(range(HALO + ROWS, EXT))
    near, far = near_ref[EDGE : EDGE + 8, :], far_ref[EDGE : EDGE + 8, :]
    above, below = jnp.where(odd_x, near, far), jnp.where(odd_x, far, near)
    for g in range(2):
        at = slice(g * HALO, (g + 1) * HALO)
        wide_ref[g, :HALO] = above[at]
        wide_ref[g, HALO : HALO + ROWS] = geo_ref[g]
        wide_ref[g, HALO + ROWS :] = below[at]

    def put(packed, row_of, f, place):
        to_left, to_right = packed
        left, right = own_columns(row_of, outside, own_left[place], own_right[place])
        left_ref[place] = left
        right_ref[place] = right
        to_left = jnp.where(field == f, turn(left, HALO * f - HALO), to_left)
        to_right = jnp.where(field == f, turn(right, HALO * f), to_right)
        return to_left, to_right

    def send(place, packed):
        to_left, to_right = packed
        a_ref[place] = jnp.where(odd_y, to_left, to_right)
        b_ref[place] = jnp.where(odd_y, to_right, to_left)

    def block(m, carry):
        at = pl.ds(pl.multiple_of(m * 8, 8), 8)
        packed = (jnp.zeros((8, COLS), F32),) * 2
        for f in range(FIELDS):
            rows = {}
            for r in range(HALO):
                cut = pl.ds(pl.multiple_of((f * HALO + r) * MEMBERS + m * 8, 8), 8)
                near, far = near_ref[cut, :], far_ref[cut, :]
                rows[r] = jnp.where(odd_x, near, far)
                rows[r + ROWS + HALO] = jnp.where(odd_x, far, near)
                halo_ref[f, r, at, :] = rows[r]
                halo_ref[f, r + HALO, at, :] = rows[r + ROWS + HALO]
            packed = put(packed, rows.get, f, f * BLOCKS + m)
        send(m, packed)
        return carry

    lax.fori_loop(0, BLOCKS, block, 0, unroll=2)
    packed = (jnp.zeros((8, COLS), F32),) * 2
    for g in range(2):
        packed = put(packed, lambda r: spread(wide_ref[g, r : r + 1, :]), g, FIELDS * BLOCKS + g)
    send(BLOCKS, packed)


def section(h, u, v, depth):
    damp = 0.05 * h
    half = 0.5 * h
    east, north = depth * u, depth * v
    us, vs = 0.05 * u, 0.05 * v
    return dict(
        up=(damp - east, us - half, vs),
        down=(damp + east, us + half, vs),
        back=(damp - north, us, vs - half),
        ahead=(damp + north, us, vs + half),
        here=(-0.2 * h, 0.2 * (v - u), -0.2 * (u + v)),
    )


def tendency(up, down, back, ahead, here):
    return [a + b + c + d + e for a, b, c, d, e in zip(up, down, back, ahead, here)]


def combine(stage, first, old, change):
    new = old + change
    if stage == 0:
        return new
    if stage == 1:
        return 0.75 * first + 0.25 * new
    return (1.0 / 3.0) * first + (2.0 / 3.0) * new


def advance(stage, rows, first, read, geo, write):
    known = {}

    def part_of(r):
        if r not in known:
            known[r] = section(*[read(f, r) for f in range(FIELDS)], geo[0, r])
        return known[r]

    for r in rows:
        mine = part_of(r)
        change = tendency(
            part_of(r + 1)["up"],
            part_of(r - 1)["down"],
            [turn(value, -1) for value in mine["back"]],
            [turn(value, 1) for value in mine["ahead"]],
            mine["here"],
        )
        for f in range(FIELDS):
            write(f, r, combine(stage, first(f, r), read(f, r), geo[1, r] * change[f]))


OUTER = tuple(range(HALO)) + tuple(range(ROWS - HALO, ROWS))


def outer(start_ref, halo_ref, wide_ref, c1_ref, c2_ref, last_ref, geo, s1, s2):
    for r in range(EXT):
        geo[0, r] = spread(wide_ref[0, r : r + 1, :])
        geo[1, r] = spread(0.3 * wide_ref[1, r : r + 1, :])

    def block(m, carry):
        at = pl.ds(pl.multiple_of(m * 8, 8), 8)

        def first(f, r):
            if r < HALO:
                return halo_ref[f, r, at, :]
            if r < HALO + ROWS:
                return start_ref[f, r - HALO, at, :]
            return halo_ref[f, r - ROWS, at, :]

        for stage in range(3):

            def read(f, r):
                if stage == 0:
                    return first(f, r)
                inside = HALO + stage
                if inside <= r < EXT - inside:
                    return (c1_ref, c2_ref)[stage - 1][f, r - inside, at, :]
                return (s1, s2)[stage - 1][f, r]

            def write(f, r, new):
                if stage < 2:
                    (s1, s2)[stage][f, r] = new
                else:
                    last_ref[f, OUTER.index(r - HALO), at, :] = new

            low, high = stage + 1, stage + 1 + HALO
            advance(stage, range(low, high), first, read, geo, write)
            advance(stage, range(EXT - high, EXT - low), first, read, geo, write)
        return carry

    lax.fori_loop(0, BLOCKS, block, 0)


def final_row(f, r, at, inner_ref, outer_ref):
    return outer_ref[f, OUTER.index(r), at, :] if r in OUTER else inner_ref[f, r - HALO, at, :]


def mended(edge, r, value):
    lane = lanes()
    border = (lane < HALO) | (lane >= COLS - HALO)
    return jnp.where(border, turn(edge, -(WIDE * (r + HALO) + HALO)), value)


def observe(
    wide_ref, left_ref, right_ref, a_ref, b_ref, inner_ref, outer_ref, cells_hbm, values_hbm, error_hbm,
    edge_ref, part_ref, seen, cells_ref, values_ref, error_ref, sems,
):
    loads = [
        pltpu.make_async_copy(source, target, sems.at[i])
        for i, (source, target) in enumerate(
            ((cells_hbm, cells_ref), (values_hbm, values_ref), (error_hbm, error_ref))
        )
    ]
    for load in loads:
        load.start()
    odd_y = lax.rem(lax.axis_index("gy"), 2) == 1
    column = lax.rem(lanes(), WIDE)

    def sides(place, f, own):
        a, b = a_ref[place], b_ref[place]
        from_left, from_right = jnp.where(odd_y, a, b), jnp.where(odd_y, b, a)
        left = jnp.where(column < HALO, turn(from_left, -HALO * f), left_ref[own])
        right = jnp.where(
            (column >= HALO) & (column < 2 * HALO), turn(from_right, HALO - HALO * f), right_ref[own]
        )
        return left, right

    depth_sides = sides(BLOCKS, 0, FIELDS * BLOCKS)
    land_sides = [0.3 * value for value in sides(BLOCKS, 1, FIELDS * BLOCKS + 1)]

    def strip(m, carry):
        fields = [sides(m, f, f * BLOCKS + m) for f in range(FIELDS)]
        done = []
        for side in range(2):
            first = [fields[f][side] for f in range(FIELDS)]
            now = first
            for stage in range(3):
                part = section(*now, depth_sides[side])
                change = tendency(
                    [turn(value, -WIDE) for value in part["up"]],
                    [turn(value, WIDE) for value in part["down"]],
                    [turn(value, -1) for value in part["back"]],
                    [turn(value, 1) for value in part["ahead"]],
                    part["here"],
                )
                now = [combine(stage, first[f], now[f], land_sides[side] * change[f]) for f in range(FIELDS)]
            done.append(now)
        for f in range(FIELDS):
            edge_ref[f, m] = jnp.where(column >= HALO, done[0][f], done[1][f])
        return carry

    lax.fori_loop(0, BLOCKS, strip, 0, unroll=2)
    for load in loads:
        load.wait()
    cell = jnp.broadcast_to(cells_ref[...], (8, OBS))
    cell_row, cell_col = cell // COLS, lax.rem(cell, COLS)

    def look(m, carry):
        at = pl.ds(pl.multiple_of(m * 8, 8), 8)
        edge = edge_ref[0, m]
        heights = [mended(edge, r, final_row(0, r, at, inner_ref, outer_ref)) for r in range(ROWS)]
        for part in range(OBS // COLS):
            cut = slice(part * COLS, (part + 1) * COLS)
            got = jnp.zeros((8, COLS), F32)
            for r in range(ROWS):
                picked = jnp.take_along_axis(heights[r], cell_col[:, cut], axis=1)
                got = jnp.where(cell_row[:, cut] == r, picked, got)
            seen[at, cut] = got
        return carry

    lax.fori_loop(0, BLOCKS, look, 0, unroll=2)
    everything = seen[...]
    obs_mean = jnp.sum(everything, axis=0, keepdims=True) * (1.0 / MEMBERS)
    error = error_ref[...]
    scaled = (everything - obs_mean) * (1.0 / (error * np.sqrt(np.float32(MEMBERS - 1))))
    innovation = (values_ref[...] - obs_mean) / error
    product = lax.dot_general(
        jnp.concatenate([scaled, jnp.broadcast_to(innovation, (8, OBS))], axis=0),
        scaled,
        (((1,), (1,)), ((), ())),
        precision=lax.Precision.HIGHEST,
        preferred_element_type=F32,
    )
    part_ref[:32, :MEMBERS] = product[:32]
    part_ref[:32, MEMBERS:] = product[32:MEMBERS]
    part_ref[32:, :MEMBERS] = product[MEMBERS:]
    part_ref[32:, MEMBERS:] = jnp.zeros((8, MEMBERS), F32)


def deviate(edge_ref, inner_ref, outer_ref, big_ref, small_ref, mean_ref):
    for f in range(FIELDS):
        for r in range(ROWS):
            rows = []
            for m in range(BLOCKS):
                at = slice(m * 8, m * 8 + 8)
                rows.append(mended(edge_ref[f, m], r, final_row(f, r, at, inner_ref, outer_ref)))
            value = jnp.concatenate(rows, axis=0)
            mean = jnp.sum(value, axis=0, keepdims=True) * (1.0 / MEMBERS)
            k = f * ROWS + r
            mean_ref[k : k + 1, :] = mean
            value = value - mean
            big = value.astype(BF16)
            big_ref[f, r] = big
            small_ref[f, r] = (value - big.astype(F32)).astype(BF16)


def column_of(value, j):
    return jnp.broadcast_to(value[:, j : j + 1], (8, COLS))


def inverse_factor(sum_ref):
    lane, sub = lanes(), grid_sub()
    table = []
    for b in range(BLOCKS):
        at = (b % 4) * 8
        value = turn(sum_ref[at : at + 8, :], MEMBERS * (b // 4))
        one = (lane == sub + 8 * b) | (lane == sub + 8 * b + MEMBERS)
        table.append(jnp.where(lane < MEMBERS, value, 0.0) + jnp.where(one, 1.0, 0.0))
    for b in range(BLOCKS):
        rows = [spread(table[b][s : s + 1, :]) for s in range(8)]
        entry = {(s, t): column_of(rows[s], 8 * b + t) for s in range(8) for t in range(s, 8)}
        over = []
        for s in range(8):
            over.append(1.0 / entry[s, s])
            for t in range(s + 1, 8):
                factor = entry[s, t] * over[s]
                for q in range(t, 8):
                    entry[t, q] = entry[t, q] - factor * entry[s, q]
                rows[t] = rows[t] - factor * rows[s]
        for i in range(b + 1, BLOCKS):
            column = [column_of(table[i], 8 * b + s) for s in range(8)]
            for s in range(8):
                column[s] = column[s] * over[s]
                for t in range(s + 1, 8):
                    column[t] = column[t] - column[s] * entry[s, t]
                table[i] = table[i] - column[s] * rows[s]
        for s in range(8):
            table[b] = jnp.where(sub == s, rows[s] * lax.rsqrt(entry[s, s]), table[b])
    return [jnp.where(lane < MEMBERS, turn(value, MEMBERS), 0.0) for value in table]


def analyse(sum_ref, big_ref, small_ref, mean_ref, out_hbm, out_ref, sems):
    inverse = inverse_factor(sum_ref)
    projection = spread(sum_ref[32:33, :])
    weights = jnp.zeros((8, COLS), F32)
    for b in range(BLOCKS):
        weights = weights + inverse[b] * jnp.sum(inverse[b] * projection, axis=1, keepdims=True)
    weights = jnp.sum(weights, axis=0, keepdims=True) / np.sqrt(np.float32(MEMBERS - 1))
    transform = jnp.concatenate(inverse, axis=0)[:, :MEMBERS] + weights[:, :MEMBERS]
    high = transform.astype(BF16)
    low = (transform - high.astype(F32)).astype(BF16)
    taps = jnp.concatenate([high, low, high], axis=1)
    stores = []
    for f in range(FIELDS):
        for r in range(0, ROWS, 2):
            big = jnp.concatenate([big_ref[f, r], big_ref[f, r + 1]], axis=1)
            small = jnp.concatenate([small_ref[f, r], small_ref[f, r + 1]], axis=1)
            mixed = jnp.dot(taps, jnp.concatenate([big, big, small], axis=0), preferred_element_type=F32)
            for q in range(2):
                k = f * ROWS + r + q
                out_ref[pl.ds(f * MEMBERS * ROWS + r + q, MEMBERS, stride=ROWS), :] = (
                    mean_ref[k : k + 1, :] + mixed[:, q * COLS : (q + 1) * COLS]
                )
        cut = pl.ds(f * MEMBERS * ROWS, MEMBERS * ROWS)
        stores.append(pltpu.make_async_copy(out_ref.at[cut], out_hbm.at[cut], sems.at[f]))
        stores[-1].start()
    for store in stores:
        store.wait()


def swap(value, axis, pairs):
    return lax.ppermute(value, axis, [(a, b) for a, b in pairs] + [(b, a) for a, b in pairs])


def pairs_of(count, first):
    return [(i, i + 1) for i in range(first, count - 1, 2)]


def summed(part):
    for axis, flips in (("gx", (1,)), ("gy", (1, 3)), ("gx", (16, 48, 2, 4, 12))):
        count = lax.axis_size(axis)
        for flip in flips:
            part = part + lax.ppermute(part, axis, [(i, i ^ flip) for i in range(count)])
    return part


def shape(*sizes, dtype=F32):
    return jax.ShapeDtypeStruct(sizes, dtype)


def hbm(count):
    return [pl.BlockSpec(memory_space=pltpu.HBM)] * count


def call(body, outs, ins, scratch=(), out_specs=None, moved=2 * 2**20):
    return pl.pallas_call(
        body,
        out_shape=outs,
        in_specs=ins,
        out_specs=out_specs or tuple(vmem(len(outs))),
        scratch_shapes=scratch,
        name=body.__name__,
        compiler_params=pltpu.CompilerParams(vmem_limit_bytes=8 * 2**20),
        cost_estimate=pl.CostEstimate(flops=0, transcendentals=0, bytes_accessed=moved),
    )


def local(members_state, depth_level, land_mask, obs_cells, obs_values, obs_error):
    x = members_state.reshape(FIELDS * MEMBERS * ROWS, COLS)
    dma = pltpu.SemaphoreType.DMA
    payload = shape(EDGE + 8, COLS)
    start, geo, near, far = call(
        arrange,
        (shape(FIELDS, ROWS, MEMBERS, COLS), shape(2, ROWS, COLS), payload, payload),
        hbm(3),
        [
            pltpu.VMEM(x.shape, F32), pltpu.VMEM((ROWS, COLS), jnp.int32), pltpu.VMEM((ROWS, COLS), jnp.int32),
            dma((5,)),
        ],
    )(*[pltpu.with_memory_space_constraint(value, pltpu.HBM) for value in (x, depth_level, land_mask)])
    far = swap(far, "gx", pairs_of(64, 1))
    near = swap(near, "gx", pairs_of(64, 0))
    own = shape(FIELDS * BLOCKS + 2, 8, COLS)
    own_left, own_right, c1, c2, c3 = call(
        interior,
        (own, own) + tuple(shape(FIELDS, count, MEMBERS, COLS) for count in (6, 4, 2)),
        vmem(2),
        [pltpu.VMEM((2, ROWS, 8, COLS), F32)],
        moved=8 * 2**20,
    )(start, geo)
    tile = shape(BLOCKS + 1, 8, COLS)
    outside = shape(FIELDS, 2 * HALO, MEMBERS, COLS)
    halo, wide, left, right, a, b = call(
        strips, (outside, shape(2, EXT, COLS), own, own, tile, tile), vmem(5)
    )(near, far, geo, own_left, own_right)
    b = swap(b, "gy", pairs_of(4, 1))
    a = swap(a, "gy", pairs_of(4, 0))
    rows = pltpu.VMEM((FIELDS, EXT, 8, COLS), F32)
    (last,) = call(
        outer, (outside,), vmem(5), [pltpu.VMEM((2, EXT, 8, COLS), F32), rows, rows], moved=6 * 2**20
    )(start, halo, wide, c1, c2)
    line = pltpu.VMEM((1, OBS), F32)
    edge, part = call(
        observe,
        (shape(FIELDS, BLOCKS, 8, COLS), shape(40, COLS)),
        vmem(7) + hbm(3),
        [pltpu.VMEM((MEMBERS, OBS), F32), pltpu.VMEM((1, OBS), jnp.int32), line, line, dma((3,))],
    )(
        wide, left, right, a, b, c3, last,
        *[
            pltpu.with_memory_space_constraint(value.reshape(1, OBS), pltpu.HBM)
            for value in (obs_cells, obs_values, obs_error)
        ],
    )
    half = shape(FIELDS, ROWS, MEMBERS, COLS, dtype=BF16)
    big, small, mean = call(
        deviate, (half, half, shape(FIELDS * ROWS, COLS)), vmem(3), moved=4 * 2**20
    )(edge, c3, last)
    (out,) = call(
        analyse,
        (shape(*x.shape),),
        vmem(4),
        [pltpu.VMEM(x.shape, F32), dma((FIELDS,))],
        out_specs=tuple(hbm(1)),
    )(summed(part), big, small, mean)
    return out.reshape(FIELDS, MEMBERS, ROWS, COLS)


def solution(mesh):
    placed = (
        P(None, None, "gx", "gy"),
        P("gx", "gy"),
        P("gx", "gy"),
        P("gx", "gy", None),
        P("gx", "gy", None),
        P("gx", "gy", None),
    )
    return jax.shard_map(
        local, mesh=mesh, in_specs=placed, out_specs=P(None, None, "gx", "gy"), check_vma=False
    )
```

time: 79.3 us -> 60.6 us (0.76)
  Pallas kernels: 24.2 us -> 13 us
  waiting for transfers between devices: 33 us -> 28.3 us
  local copies, waits for them, and re-layouts: 1.34 us -> 0 us
  other arithmetic: 1.36 us -> 0.03 us
    pallas_call x4 -> x7, Pallas kernels: 24.2 us -> 13 us  [the longest x1 3.21 us: local(): call(analyse, (shape(*x.shape),), vmem(4), [pltpu.VMEM(x.shape, F32), dma...]
    ppermute x4, waiting for transfers between devices: 6.65 us -> 2.28 us  [swap(): lax.ppermute(value, axis, [(a, b) for a, b in pairs] + [(b, a) for a, b i...]
    unnamed x8 -> x0, local copies, waits for them, and re-layouts: 1.34 us -> none
    add x8, other arithmetic: 1.36 us -> 0.03 us  [summed(): part + lax.ppermute(part, axis, [(i, i ^ flip) for i in range(count)])]
  transfers between devices with their start and end apart: 12 -> 12, of which waited for: 10 -> 9; matrix products, arithmetic and copies ran while one was open for 0% -> 0% of each run, Pallas kernels for 0% -> 8%
where the time goes in v3:
time: 60.6 us; the launch traced here: 60.5 us
  waiting for transfers between devices  28.3 us (47%)
  starting transfers between devices  19 us (31%)
  Pallas kernels  13 us (21%)
    ppermute x8, waiting for transfers between devices, summed(): lax.ppermute(part, axis, [(i, i ^ flip) for i in range(count)])  26 us
    ppermute x4, starting transfers between devices, swap(): lax.ppermute(value, axis, [(a, b) for a, b in pairs] + [(b, a) for a, b i...  10.3 us
    ppermute x8, starting transfers between devices, summed(): lax.ppermute(part, axis, [(i, i ^ flip) for i in range(count)])  8.75 us
    pallas_call x1, Pallas kernels, local(): call(analyse, (shape(*x.shape),), vmem(4), [pltpu.VMEM(x.shape, F32), dma...  3.21 us
    pallas_call x1, Pallas kernels, local(): call(observe, (shape(FIELDS, BLOCKS, 8, COLS), shape(40, COLS)), vmem(7)...  2.93 us
    ppermute x4, waiting for transfers between devices, swap(): lax.ppermute(value, axis, [(a, b) for a, b in pairs] + [(b, a) for a, b i...  2.28 us
    pallas_call x1, Pallas kernels, local(): call(outer, (outside,), vmem(5), [pltpu.VMEM((2, EXT, 8, COLS), F32), row...  2.25 us
    pallas_call x1, Pallas kernels, local(): call(interior, (own, own) + tuple((shape(FIELDS, count, MEMBERS, COLS) fo...  2.14 us
  transfers between devices with their start and end apart: 12, of which 9 were waited for; matrix products, arithmetic and copies ran while one was open for 0% of the time, Pallas kernels for 8%

profile of v3, /device:TPU:24, one launch (start us, length us, event | category | flops | bytes accessed | tf_op | source)
XLA Modules:
  0.0 60.5 jit_solution(9476358192678970537)
XLA Ops:
  0.0 1.2 %arrange.1 = (f32[3,8,64,128]{3,2,1,0:T(8,128)S(1)}, f32[2,8,128]{2,1,0:T(8,128)S(1)}, f32[584,128]{1,0:T(8,128)S(1)}, f32[584,128]{1,0:T(8,128)S(1)}) custom-call(f32[1536,128]{1,0:T(8,128)} %bitcast.5, s32[8,128]{1,0:T(8,128)} %depth_hbm.1, s32[8,128]{1,0:T(8,128)} %land_hbm.1), custom_call_target="tpu_custom_call" | custom-call | bytes 2097152 | tf_op jit(solution)/shard_map/arrange/pallas_call | solution.py:484
  1.3 0.1 collective-permute-start
  1.4 8.0 %collective-permute-start.1 = (f32[584,128]{1,0:T(8,128)S(1)}, f32[584,128]{1,0:T(8,128)S(1)}, u32[]{:S(2)}, u32[]{:S(2)}) collective-permute-start(f32[584,128]{1,0:T(8,128)S(1)} %get-tuple-element.26), channel_id=1, source_target_pairs={{4,8},{12,16},{20,24},{28,32},{36,40},{44,48},{52,56},{60,64},{68,... | collective-permute-start | bytes 897032 | tf_op jit(solution)/shard_map/ppermute | solution.py:444
  9.4 2.1 %interior.1 = (f32[26,8,128]{2,1,0:T(8,128)S(1)}, f32[26,8,128]{2,1,0:T(8,128)S(1)}, f32[3,6,64,128]{3,2,1,0:T(8,128)S(1)}, f32[3,4,64,128]{3,2,1,0:T(8,128)S(1)}, f32[3,2,64,128]{3,2,1,0:T(8,128)S(1)}) custom-call(f32[3,8,64,128]{3,2,1,0:T(8,128)S(1)} %get-tuple-element.28.start_ref, f32[2,8,128]{2,1,0:T(8,128)S(1)} %get-tuple-element.27.geo_ref), custom_call_target="tpu_custom_call" | custom-call | bytes 8388608 | tf_op jit(solution)/shard_map/interior/pallas_call | solution.py:496
  11.5 0.0 collective-permute-done.near_ref
  11.6 2.3 %collective-permute-done.1.far_ref = f32[584,128]{1,0:T(8,128)S(1)} collective-permute-done((f32[584,128]{1,0:T(8,128)S(1)}, f32[584,128]{1,0:T(8,128)S(1)}, u32[]{:S(2)}, u32[]{:S(2)}) %collective-permute-start.1) | collective-permute-done | bytes 299040 | tf_op jit(solution)/shard_map/ppermute | solution.py:444
  13.8 0.9 %strips.1 = (f32[3,6,64,128]{3,2,1,0:T(8,128)S(1)}, f32[2,14,128]{2,1,0:T(8,128)S(1)}, f32[26,8,128]{2,1,0:T(8,128)S(1)}, f32[26,8,128]{2,1,0:T(8,128)S(1)}, f32...) custom-call(f32[584,128]{1,0:T(8,128)S(1)} %collective-permute-done.near_ref, ...), custom_call_target="tpu_custom_call" | custom-call | bytes 2097152 | tf_op jit(solution)/shard_map/strips/pallas_call | solution.py:505
  14.7 1.5 %collective-permute-start.2 = (f32[9,8,128]{2,1,0:T(8,128)S(1)}, f32[9,8,128]{2,1,0:T(8,128)S(1)}, u32[]{:S(2)}, u32[]{:S(2)}) collective-permute-start(f32[9,8,128]{2,1,0:T(8,128)S(1)} %get-tuple-element.34), channel_id=1, source_target_pairs={{0,1},{2,3},{1,0},{3,2},{4,5},{6,7},{5,4},{7,6},{8,9},{10,11},{9,8... | collective-permute-start | bytes 110600 | tf_op jit(solution)/shard_map/ppermute | solution.py:444
  16.2 0.7 %collective-permute-start.3 = (f32[9,8,128]{2,1,0:T(8,128)S(1)}, f32[9,8,128]{2,1,0:T(8,128)S(1)}, u32[]{:S(2)}, u32[]{:S(2)}) collective-permute-start(f32[9,8,128]{2,1,0:T(8,128)S(1)} %get-tuple-element.35), channel_id=1, source_target_pairs={{1,2},{2,1},{5,6},{6,5},{9,10},{10,9},{13,14},{14,13},{17,18},{18,... | collective-permute-start | bytes 110600 | tf_op jit(solution)/shard_map/ppermute | solution.py:444
  16.9 2.3 %outer.1.outer_ref = f32[3,6,64,128]{3,2,1,0:T(8,128)S(1)} custom-call(f32[3,8,64,128]{3,2,1,0:T(8,128)S(1)} %get-tuple-element.28.start_ref, f32[3,6,64,128]{3,2,1,0:T(8,128)S(1)} %get-tuple-element.37.halo_ref, f32[2,14,128]{2,1,0:T(8,128)S(1)} %get-tuple-element.31.wide_ref, f32[3,6,64,128]{3,2,1,0:T(8,128)S(1)} %get-tuple-element.38.c1_ref, ...), custom_call_target="tpu_custom_call" | custom-call | bytes 6291456 | tf_op jit(solution)/shard_map/outer/pallas_call | solution.py:511
  19.1 0.0 collective-permute-done.2.a_ref
  19.2 0.0 collective-permute-done.3.b_ref
  19.2 2.9 %observe.1 = (f32[3,8,8,128]{3,2,1,0:T(8,128)S(1)}, f32[40,128]{1,0:T(8,128)S(1)}) custom-call(f32[2,14,128]{2,1,0:T(8,128)S(1)} %get-tuple-element.31.wide_ref, f32[26,8,128]{2,1,0:T(8,128)S(1)} %get-tuple-element.32.left_ref, f32[26,8,128]{2,1,0:T(8,128)S(1)} %get-tuple-element.33.right_ref, f32[9,8,128]{2,1,0:T(8,128)S(1)} %collective-permute-done.2.a_ref, ...), custom_call_target="tpu_custom_call" | custom-call | bytes 2097152 | tf_op jit(solution)/shard_map/observe/pallas_call | solution.py:515
  22.1 0.1 collective-permute-start.4
  22.2 1.2 %collective-permute-done.4 = f32[40,128]{1,0:T(8,128)S(1)} collective-permute-done((f32[40,128]{1,0:T(8,128)S(1)}, f32[40,128]{1,0:T(8,128)S(1)}, u32[]{:S(2)}, u32[]{:S(2)}) %collective-permute-start.4) | collective-permute-done | bytes 20512 | tf_op jit(solution)/shard_map/ppermute | solution.py:455
  23.4 3.9 %collective-permute-start.5 = (f32[40,128]{1,0:T(8,128)S(1)}, f32[40,128]{1,0:T(8,128)S(1)}, u32[]{:S(2)}, u32[]{:S(2)}) collective-permute-start(f32[40,128]{1,0:T(8,128)S(1)} %add.24), channel_id=1, source_target_pairs={{0,1},{1,0},{2,3},{3,2},{4,5},{5,4},{6,7},{7,6},{8,9},{9,8},{10,11... | collective-permute-start | bytes 61448 | tf_op jit(solution)/shard_map/ppermute | solution.py:455
  27.3 1.8 %collective-permute-done.5 = f32[40,128]{1,0:T(8,128)S(1)} collective-permute-done((f32[40,128]{1,0:T(8,128)S(1)}, f32[40,128]{1,0:T(8,128)S(1)}, u32[]{:S(2)}, u32[]{:S(2)}) %collective-permute-start.5) | collective-permute-done | bytes 20512 | tf_op jit(solution)/shard_map/ppermute | solution.py:455
  29.1 2.3 %collective-permute-start.6 = (f32[40,128]{1,0:T(8,128)S(1)}, f32[40,128]{1,0:T(8,128)S(1)}, u32[]{:S(2)}, u32[]{:S(2)}) collective-permute-start(f32[40,128]{1,0:T(8,128)S(1)} %add.25), channel_id=1, source_target_pairs={{0,3},{1,2},{2,1},{3,0},{4,7},{5,6},{6,5},{7,4},{8,11},{9,10},{10,... | collective-permute-start | bytes 61448 | tf_op jit(solution)/shard_map/ppermute | solution.py:455
  31.3 2.7 %collective-permute-done.6 = f32[40,128]{1,0:T(8,128)S(1)} collective-permute-done((f32[40,128]{1,0:T(8,128)S(1)}, f32[40,128]{1,0:T(8,128)S(1)}, u32[]{:S(2)}, u32[]{:S(2)}) %collective-permute-start.6) | collective-permute-done | bytes 20512 | tf_op jit(solution)/shard_map/ppermute | solution.py:455
  34.1 0.4 collective-permute-start.7
  34.5 3.3 %collective-permute-done.7 = f32[40,128]{1,0:T(8,128)S(1)} collective-permute-done((f32[40,128]{1,0:T(8,128)S(1)}, f32[40,128]{1,0:T(8,128)S(1)}, u32[]{:S(2)}, u32[]{:S(2)}) %collective-permute-start.7) | collective-permute-done | bytes 20512 | tf_op jit(solution)/shard_map/ppermute | solution.py:455
  37.9 0.0 collective-permute-start.8
  37.9 5.0 %collective-permute-done.8 = f32[40,128]{1,0:T(8,128)S(1)} collective-permute-done((f32[40,128]{1,0:T(8,128)S(1)}, f32[40,128]{1,0:T(8,128)S(1)}, u32[]{:S(2)}, u32[]{:S(2)}) %collective-permute-start.8) | collective-permute-done | bytes 20512 | tf_op jit(solution)/shard_map/ppermute | solution.py:455
  42.9 0.0 collective-permute-start.9
  42.9 3.8 %collective-permute-done.9 = f32[40,128]{1,0:T(8,128)S(1)} collective-permute-done((f32[40,128]{1,0:T(8,128)S(1)}, f32[40,128]{1,0:T(8,128)S(1)}, u32[]{:S(2)}, u32[]{:S(2)}) %collective-permute-start.9) | collective-permute-done | bytes 20512 | tf_op jit(solution)/shard_map/ppermute | solution.py:455
  46.7 0.0 collective-permute-start.10
  46.7 4.7 %collective-permute-done.10 = f32[40,128]{1,0:T(8,128)S(1)} collective-permute-done((f32[40,128]{1,0:T(8,128)S(1)}, f32[40,128]{1,0:T(8,128)S(1)}, u32[]{:S(2)}, u32[]{:S(2)}) %collective-permute-start.10) | collective-permute-done | bytes 20512 | tf_op jit(solution)/shard_map/ppermute | solution.py:455
  51.3 2.0 %collective-permute-start.11 = (f32[40,128]{1,0:T(8,128)S(1)}, f32[40,128]{1,0:T(8,128)S(1)}, u32[]{:S(2)}, u32[]{:S(2)}) collective-permute-start(f32[40,128]{1,0:T(8,128)S(1)} %add.30), channel_id=1, source_target_pairs={{0,48},{4,52},{8,56},{12,60},{16,32},{20,36},{24,40},{28,44},{32,1... | collective-permute-start | bytes 61448 | tf_op jit(solution)/shard_map/ppermute | solution.py:455
  53.4 0.3 deviate.1
  53.7 3.6 %collective-permute-done.11 = f32[40,128]{1,0:T(8,128)S(1)} collective-permute-done((f32[40,128]{1,0:T(8,128)S(1)}, f32[40,128]{1,0:T(8,128)S(1)}, u32[]{:S(2)}, u32[]{:S(2)}) %collective-permute-start.11) | collective-permute-done | bytes 20512 | tf_op jit(solution)/shard_map/ppermute | solution.py:455
  57.2 3.2 %analyse.1 = f32[1536,128]{1,0:T(8,128)} custom-call(f32[40,128]{1,0:T(8,128)S(1)} %add.31.sum_ref, bf16[3,8,64,128]{3,2,1,0:T(8,128)(2,1)S(1)} %get-tuple-element.42.big_ref, bf16[3,8,64,128]{3,2,1,0:T(8,128)(2,1)S(1)} %get-tuple-element.43.small_ref, f32[24,128]{1,0:T(8,128)S(1)} %get-tuple-element.44.mean_ref), custom_call_target="tpu_custom_call" | custom-call | bytes 2097152 | tf_op jit(solution)/shard_map/analyse/pallas_call | solution.py:531
  (8 shorter events, 0.0 us)
Async XLA Ops:
  1.3 10.3 %collective-permute-start = (f32[584,128]{1,0:T(8,128)S(1)}, f32[584,128]{1,0:T(8,128)S(1)}, u32[]{:S(2)}, u32[]{:S(2)}) collective-permute-start(f32[584,128]{1,0:T(8,128)S(1)} %get-tuple-element.25), channel_id=1, source_target_pairs={{0,4},{8,12},{16,20},{24,28},{32,36},{40,44},{48,52},{56,60},{64,6... | collective-permute-start | bytes 897032 | tf_op jit(solution)/shard_map/ppermute | solution.py:444
  1.4 12.5 %collective-permute-start.1 = (f32[584,128]{1,0:T(8,128)S(1)}, f32[584,128]{1,0:T(8,128)S(1)}, u32[]{:S(2)}, u32[]{:S(2)}) collective-permute-start(f32[584,128]{1,0:T(8,128)S(1)} %get-tuple-element.26), channel_id=1, source_target_pairs={{4,8},{12,16},{20,24},{28,32},{36,40},{44,48},{52,56},{60,64},{68,... | collective-permute-start | bytes 897032 | tf_op jit(solution)/shard_map/ppermute | solution.py:444
  14.7 4.4 %collective-permute-start.2 = (f32[9,8,128]{2,1,0:T(8,128)S(1)}, f32[9,8,128]{2,1,0:T(8,128)S(1)}, u32[]{:S(2)}, u32[]{:S(2)}) collective-permute-start(f32[9,8,128]{2,1,0:T(8,128)S(1)} %get-tuple-element.34), channel_id=1, source_target_pairs={{0,1},{2,3},{1,0},{3,2},{4,5},{6,7},{5,4},{7,6},{8,9},{10,11},{9,8... | collective-permute-start | bytes 110600 | tf_op jit(solution)/shard_map/ppermute | solution.py:444
  16.2 2.9 %collective-permute-start.3 = (f32[9,8,128]{2,1,0:T(8,128)S(1)}, f32[9,8,128]{2,1,0:T(8,128)S(1)}, u32[]{:S(2)}, u32[]{:S(2)}) collective-permute-start(f32[9,8,128]{2,1,0:T(8,128)S(1)} %get-tuple-element.35), channel_id=1, source_target_pairs={{1,2},{2,1},{5,6},{6,5},{9,10},{10,9},{13,14},{14,13},{17,18},{18,... | collective-permute-start | bytes 110600 | tf_op jit(solution)/shard_map/ppermute | solution.py:444
  22.1 1.3 %collective-permute-start.4 = (f32[40,128]{1,0:T(8,128)S(1)}, f32[40,128]{1,0:T(8,128)S(1)}, u32[]{:S(2)}, u32[]{:S(2)}) collective-permute-start(f32[40,128]{1,0:T(8,128)S(1)} %get-tuple-element.40), channel_id=1, source_target_pairs={{0,4},{4,0},{8,12},{12,8},{16,20},{20,16},{24,28},{28,24},{32,36},... | collective-permute-start | bytes 61448 | tf_op jit(solution)/shard_map/ppermute | solution.py:455
  23.4 5.7 %collective-permute-start.5 = (f32[40,128]{1,0:T(8,128)S(1)}, f32[40,128]{1,0:T(8,128)S(1)}, u32[]{:S(2)}, u32[]{:S(2)}) collective-permute-start(f32[40,128]{1,0:T(8,128)S(1)} %add.24), channel_id=1, source_target_pairs={{0,1},{1,0},{2,3},{3,2},{4,5},{5,4},{6,7},{7,6},{8,9},{9,8},{10,11... | collective-permute-start | bytes 61448 | tf_op jit(solution)/shard_map/ppermute | solution.py:455
  29.1 5.0 %collective-permute-start.6 = (f32[40,128]{1,0:T(8,128)S(1)}, f32[40,128]{1,0:T(8,128)S(1)}, u32[]{:S(2)}, u32[]{:S(2)}) collective-permute-start(f32[40,128]{1,0:T(8,128)S(1)} %add.25), channel_id=1, source_target_pairs={{0,3},{1,2},{2,1},{3,0},{4,7},{5,6},{6,5},{7,4},{8,11},{9,10},{10,... | collective-permute-start | bytes 61448 | tf_op jit(solution)/shard_map/ppermute | solution.py:455
  34.1 3.8 %collective-permute-start.7 = (f32[40,128]{1,0:T(8,128)S(1)}, f32[40,128]{1,0:T(8,128)S(1)}, u32[]{:S(2)}, u32[]{:S(2)}) collective-permute-start(f32[40,128]{1,0:T(8,128)S(1)} %add.26), channel_id=1, source_target_pairs={{0,64},{4,68},{8,72},{12,76},{16,80},{20,84},{24,88},{28,92},{32,9... | collective-permute-start | bytes 61448 | tf_op jit(solution)/shard_map/ppermute | solution.py:455
  37.9 5.0 %collective-permute-start.8 = (f32[40,128]{1,0:T(8,128)S(1)}, f32[40,128]{1,0:T(8,128)S(1)}, u32[]{:S(2)}, u32[]{:S(2)}) collective-permute-start(f32[40,128]{1,0:T(8,128)S(1)} %add.27), channel_id=1, source_target_pairs={{0,192},{4,196},{8,200},{12,204},{16,208},{20,212},{24,216},{28,22... | collective-permute-start | bytes 61448 | tf_op jit(solution)/shard_map/ppermute | solution.py:455
  42.9 3.8 %collective-permute-start.9 = (f32[40,128]{1,0:T(8,128)S(1)}, f32[40,128]{1,0:T(8,128)S(1)}, u32[]{:S(2)}, u32[]{:S(2)}) collective-permute-start(f32[40,128]{1,0:T(8,128)S(1)} %add.28), channel_id=1, source_target_pairs={{0,8},{4,12},{8,0},{12,4},{16,24},{20,28},{24,16},{28,20},{32,40},... | collective-permute-start | bytes 61448 | tf_op jit(solution)/shard_map/ppermute | solution.py:455
  46.7 4.7 %collective-permute-start.10 = (f32[40,128]{1,0:T(8,128)S(1)}, f32[40,128]{1,0:T(8,128)S(1)}, u32[]{:S(2)}, u32[]{:S(2)}) collective-permute-start(f32[40,128]{1,0:T(8,128)S(1)} %add.29), channel_id=1, source_target_pairs={{0,16},{4,20},{8,24},{12,28},{16,0},{20,4},{24,8},{28,12},{32,48},... | collective-permute-start | bytes 61448 | tf_op jit(solution)/shard_map/ppermute | solution.py:455
  51.3 5.9 %collective-permute-start.11 = (f32[40,128]{1,0:T(8,128)S(1)}, f32[40,128]{1,0:T(8,128)S(1)}, u32[]{:S(2)}, u32[]{:S(2)}) collective-permute-start(f32[40,128]{1,0:T(8,128)S(1)} %add.30), channel_id=1, source_target_pairs={{0,48},{4,52},{8,56},{12,60},{16,32},{20,36},{24,40},{28,44},{32,1... | collective-permute-start | bytes 61448 | tf_op jit(solution)/shard_map/ppermute | solution.py:455

commit v4 on v3

--- a/solution.py
+++ b/solution.py
@@ -128,8 +128,14 @@
     odd_y = lax.rem(lax.axis_index("gy"), 2) == 1
     field = lax.rem(lanes(), WIDE) // HALO
     outside = tuple(range(HALO)) + tuple(range(HALO + ROWS, EXT))
-    near, far = near_ref[EDGE : EDGE + 8, :], far_ref[EDGE : EDGE + 8, :]
-    above, below = jnp.where(odd_x, near, far), jnp.where(odd_x, far, near)
+    place_x = lax.axis_index("gx")
+    inside = (place_x > 0) & (place_x < lax.axis_size("gx") - 1)
+
+    def halves(cut):
+        near, far = near_ref[cut, :], jnp.where(inside, far_ref[cut, :], 0.0)
+        return jnp.where(odd_x, near, far), jnp.where(odd_x, far, near)
+
+    above, below = halves(slice(EDGE, EDGE + 8))
     for g in range(2):
         at = slice(g * HALO, (g + 1) * HALO)
         wide_ref[g, :HALO] = above[at]
@@ -157,9 +163,7 @@
             rows = {}
             for r in range(HALO):
                 cut = pl.ds(pl.multiple_of((f * HALO + r) * MEMBERS + m * 8, 8), 8)
-                near, far = near_ref[cut, :], far_ref[cut, :]
-                rows[r] = jnp.where(odd_x, near, far)
-                rows[r + ROWS + HALO] = jnp.where(odd_x, far, near)
+                rows[r], rows[r + ROWS + HALO] = halves(cut)
                 halo_ref[f, r, at, :] = rows[r]
                 halo_ref[f, r + HALO, at, :] = rows[r + ROWS + HALO]
             packed = put(packed, rows.get, f, f * BLOCKS + m)
@@ -285,11 +289,13 @@
     ]
     for load in loads:
         load.start()
-    odd_y = lax.rem(lax.axis_index("gy"), 2) == 1
+    place_y = lax.axis_index("gy")
+    odd_y = lax.rem(place_y, 2) == 1
+    inside = (place_y > 0) & (place_y < lax.axis_size("gy") - 1)
     column = lax.rem(lanes(), WIDE)
 
     def sides(place, f, own):
-        a, b = a_ref[place], b_ref[place]
+        a, b = a_ref[place], jnp.where(inside, b_ref[place], 0.0)
         from_left, from_right = jnp.where(odd_y, a, b), jnp.where(odd_y, b, a)
         left = jnp.where(column < HALO, turn(from_left, -HALO * f), left_ref[own])
         right = jnp.where(
@@ -321,7 +327,7 @@
             edge_ref[f, m] = jnp.where(column >= HALO, done[0][f], done[1][f])
         return carry
 
-    lax.fori_loop(0, BLOCKS, strip, 0, unroll=2)
+    lax.fori_loop(0, BLOCKS, strip, 0, unroll=4)
     for load in loads:
         load.wait()
     cell = jnp.broadcast_to(cells_ref[...], (8, OBS))
@@ -340,7 +346,7 @@
             seen[at, cut] = got
         return carry
 
-    lax.fori_loop(0, BLOCKS, look, 0, unroll=2)
+    lax.fori_loop(0, BLOCKS, look, 0, unroll=4)
     everything = seen[...]
     obs_mean = jnp.sum(everything, axis=0, keepdims=True) * (1.0 / MEMBERS)
     error = error_ref[...]
@@ -353,10 +359,20 @@
         precision=lax.Precision.HIGHEST,
         preferred_element_type=F32,
     )
-    part_ref[:32, :MEMBERS] = product[:32]
-    part_ref[:32, MEMBERS:] = product[32:MEMBERS]
-    part_ref[32:, :MEMBERS] = product[MEMBERS:]
-    part_ref[32:, MEMBERS:] = jnp.zeros((8, MEMBERS), F32)
+    half = MEMBERS // 2
+    whole = jnp.concatenate([product, jnp.zeros((MEMBERS + 8, COLS - MEMBERS), F32)], axis=1)
+    lane, sub = lanes(), grid_sub()
+    folded = []
+    diagonal = jnp.zeros((8, COLS), F32)
+    for k in range(half // 8):
+        upper = whole[k * 8 : k * 8 + 8]
+        lower = turn(whole[half + k * 8 : half + k * 8 + 8], -half)
+        folded.append(jnp.where((lane >= half) | (lane >= sub + 8 * k), upper, lower))
+        diagonal = diagonal + jnp.where(lane == sub + 8 * k, lower, 0.0)
+    for k in range(2):
+        part_ref[k * 8 : k * 8 + 8, :] = jnp.where(lane < MEMBERS, folded[k], turn(folded[k + 2], MEMBERS))
+    diagonal = turn(spread(jnp.sum(diagonal, axis=0, keepdims=True)), MEMBERS)
+    part_ref[16:, :] = jnp.where(lane < MEMBERS, whole[MEMBERS:], diagonal)
 
 
 def deviate(edge_ref, inner_ref, outer_ref, big_ref, small_ref, mean_ref):
@@ -380,12 +396,22 @@
     return jnp.broadcast_to(value[:, j : j + 1], (8, COLS))
 
 
-def inverse_factor(sum_ref):
+def inverse_factor(sum_ref, flip_ref):
     lane, sub = lanes(), grid_sub()
+    half = MEMBERS // 2
+    folded = [turn(sum_ref[(k % 2) * 8 : (k % 2) * 8 + 8, :], MEMBERS * (k // 2)) for k in range(4)]
+    flip_ref[:, :half] = jnp.transpose(jnp.concatenate(folded, axis=0))
+    diagonal = turn(spread(sum_ref[16:17, :]), MEMBERS)
     table = []
     for b in range(BLOCKS):
-        at = (b % 4) * 8
-        value = turn(sum_ref[at : at + 8, :], MEMBERS * (b // 4))
+        k = b % 4
+        flipped = flip_ref[k * 8 : k * 8 + 8, :]
+        at = sub + 8 * k
+        if b < 4:
+            value = jnp.where((lane >= at), folded[k], flipped)
+        else:
+            value = jnp.where(lane < at, folded[k], jnp.where(lane > at, flipped, diagonal))
+            value = jnp.where(lane < half, flip_ref[b * 8 : b * 8 + 8, :], turn(value, half))
         one = (lane == sub + 8 * b) | (lane == sub + 8 * b + MEMBERS)
         table.append(jnp.where(lane < MEMBERS, value, 0.0) + jnp.where(one, 1.0, 0.0))
     for b in range(BLOCKS):
@@ -411,9 +437,9 @@
     return [jnp.where(lane < MEMBERS, turn(value, MEMBERS), 0.0) for value in table]
 
 
-def analyse(sum_ref, big_ref, small_ref, mean_ref, out_hbm, out_ref, sems):
-    inverse = inverse_factor(sum_ref)
-    projection = spread(sum_ref[32:33, :])
+def analyse(sum_ref, big_ref, small_ref, mean_ref, out_hbm, out_ref, flip_ref, sems):
+    inverse = inverse_factor(sum_ref, flip_ref)
+    projection = spread(sum_ref[16:17, :])
     weights = jnp.zeros((8, COLS), F32)
     for b in range(BLOCKS):
         weights = weights + inverse[b] * jnp.sum(inverse[b] * projection, axis=1, keepdims=True)
@@ -445,14 +471,14 @@
 
 
 def pairs_of(count, first):
-    return [(i, i + 1) for i in range(first, count - 1, 2)]
+    return [(i, (i + 1) % count) for i in range(first, count, 2)]
 
 
 def summed(part):
-    for axis, flips in (("gx", (1,)), ("gy", (1, 3)), ("gx", (16, 48, 2, 4, 12))):
-        count = lax.axis_size(axis)
-        for flip in flips:
-            part = part + lax.ppermute(part, axis, [(i, i ^ flip) for i in range(count)])
+    gx, gy = lax.axis_size("gx"), lax.axis_size("gy")
+    for flip_x, flip_y in ((1, 0), (1, 1), (1, 3), (17, 0), (49, 0), (3, 0), (5, 0), (13, 0)):
+        pairs = [(i * gy + j, (i ^ flip_x) * gy + (j ^ flip_y)) for i in range(gx) for j in range(gy)]
+        part = part + lax.ppermute(part, ("gx", "gy"), pairs)
     return part
 
 
@@ -471,7 +497,6 @@
         in_specs=ins,
         out_specs=out_specs or tuple(vmem(len(outs))),
         scratch_shapes=scratch,
-        name=body.__name__,
         compiler_params=pltpu.CompilerParams(vmem_limit_bytes=8 * 2**20),
         cost_estimate=pl.CostEstimate(flops=0, transcendentals=0, bytes_accessed=moved),
     )
@@ -514,7 +539,7 @@
     line = pltpu.VMEM((1, OBS), F32)
     edge, part = call(
         observe,
-        (shape(FIELDS, BLOCKS, 8, COLS), shape(40, COLS)),
+        (shape(FIELDS, BLOCKS, 8, COLS), shape(24, COLS)),
         vmem(7) + hbm(3),
         [pltpu.VMEM((MEMBERS, OBS), F32), pltpu.VMEM((1, OBS), jnp.int32), line, line, dma((3,))],
     )(
@@ -532,7 +557,7 @@
         analyse,
         (shape(*x.shape),),
         vmem(4),
-        [pltpu.VMEM(x.shape, F32), dma((FIELDS,))],
+        [pltpu.VMEM(x.shape, F32), pltpu.VMEM((COLS, COLS), F32), dma((FIELDS,))],
         out_specs=tuple(hbm(1)),
     )(summed(part), big, small, mean)
     return out.reshape(FIELDS, MEMBERS, ROWS, COLS)
@@ -547,6 +572,5 @@
         P("gx", "gy", None),
         P("gx", "gy", None),
     )
-    return jax.shard_map(
-        local, mesh=mesh, in_specs=placed, out_specs=P(None, None, "gx", "gy"), check_vma=False
-    )
+
+    return jax.shard_map(local, mesh=mesh, in_specs=placed, out_specs=P(None, None, "gx", "gy"), check_vma=False)

time: 60.6 us -> 57.5 us (0.949)
  the two profiles are of different devices: /device:TPU:24 before, /device:TPU:1 now
where the time goes in v4:
time: 57.5 us; the launch traced here: 57.4 us
  waiting for transfers between devices  29 us (50%)
  starting transfers between devices  15.7 us (27%)
  Pallas kernels  12.6 us (22%)
    ppermute x8, waiting for transfers between devices, summed(): part = part + lax.ppermute(part, ('gx', 'gy'), pairs)  24.4 us
    ppermute x8, starting transfers between devices, summed(): part = part + lax.ppermute(part, ('gx', 'gy'), pairs)  11.1 us
    ppermute x4, starting transfers between devices, swap(): lax.ppermute(value, axis, [(a, b) for a, b in pairs] + [(b, a) for a, b i...  4.62 us
    ppermute x4, waiting for transfers between devices, swap(): lax.ppermute(value, axis, [(a, b) for a, b in pairs] + [(b, a) for a, b i...  4.57 us
    pallas_call x1, Pallas kernels, local(): call(analyse, (shape(*x.shape),), vmem(4), [pltpu.VMEM(x.shape, F32), plt...  3.4 us
    pallas_call x1, Pallas kernels, local(): call(observe, (shape(FIELDS, BLOCKS, 8, COLS), shape(24, COLS)), vmem(7)...  2.4 us
    pallas_call x1, Pallas kernels, local(): call(outer, (outside,), vmem(5), [pltpu.VMEM((2, EXT, 8, COLS), F32), row...  2.25 us
    pallas_call x1, Pallas kernels, local(): call(interior, (own, own) + tuple((shape(FIELDS, count, MEMBERS, COLS) fo...  2.14 us
  transfers between devices with their start and end apart: 12, of which 10 were waited for; matrix products, arithmetic and copies ran while one was open for 0% of the time, Pallas kernels for 8%

profile of v4, /device:TPU:1, one launch (start us, length us, event | category | flops | bytes accessed | tf_op | source)
XLA Modules:
  0.0 57.4 jit_solution(2110904280661929224)
XLA Ops:
  0.0 1.2 %shard_map.64 = (f32[3,8,64,128]{3,2,1,0:T(8,128)S(1)}, f32[2,8,128]{2,1,0:T(8,128)S(1)}, f32[584,128]{1,0:T(8,128)S(1)}, f32[584,128]{1,0:T(8,128)S(1)}) custom-call(f32[1536,128]{1,0:T(8,128)} %bitcast.5, s32[8,128]{1,0:T(8,128)} %depth_hbm.1, s32[8,128]{1,0:T(8,128)} %land_hbm.1), custom_call_target="tpu_custom_call" | custom-call | bytes 2097152 | tf_op jit(solution)/shard_map/pallas_call | solution.py:509
  1.3 3.3 %collective-permute-start = (f32[584,128]{1,0:T(8,128)S(1)}, f32[584,128]{1,0:T(8,128)S(1)}, u32[]{:S(2)}, u32[]{:S(2)}) collective-permute-start(f32[584,128]{1,0:T(8,128)S(1)} %get-tuple-element.25), channel_id=1, source_target_pairs={{0,4},{8,12},{16,20},{24,28},{32,36},{40,44},{48,52},{56,60},{64,6... | collective-permute-start | bytes 897032 | tf_op jit(solution)/shard_map/ppermute | solution.py:470
  4.5 0.0 collective-permute-start.1
  4.5 2.1 %shard_map.65 = (f32[26,8,128]{2,1,0:T(8,128)S(1)}, f32[26,8,128]{2,1,0:T(8,128)S(1)}, f32[3,6,64,128]{3,2,1,0:T(8,128)S(1)}, f32[3,4,64,128]{3,2,1,0:T(8,128)S(1)}, f32[3,2,64,128]{3,2,1,0:T(8,128)S(1)}) custom-call(f32[3,8,64,128]{3,2,1,0:T(8,128)S(1)} %get-tuple-element.28.start_ref, f32[2,8,128]{2,1,0:T(8,128)S(1)} %get-tuple-element.27.geo_ref), custom_call_target="tpu_custom_call" | custom-call | bytes 8388608 | tf_op jit(solution)/shard_map/pallas_call | solution.py:521
  6.7 0.0 collective-permute-done.near_ref
  6.7 4.0 %collective-permute-done.1.far_ref = f32[584,128]{1,0:T(8,128)S(1)} collective-permute-done((f32[584,128]{1,0:T(8,128)S(1)}, f32[584,128]{1,0:T(8,128)S(1)}, u32[]{:S(2)}, u32[]{:S(2)}) %collective-permute-start.1) | collective-permute-done | bytes 299040 | tf_op jit(solution)/shard_map/ppermute | solution.py:470
  10.7 0.9 %shard_map.66 = (f32[3,6,64,128]{3,2,1,0:T(8,128)S(1)}, f32[2,14,128]{2,1,0:T(8,128)S(1)}, f32[26,8,128]{2,1,0:T(8,128)S(1)}, f32[26,8,128]{2,1,0:T(8,128)S(1)},...) custom-call(f32[584,128]{1,0:T(8,128)S(1)} %collective-permute-done.near_ref, ...), custom_call_target="tpu_custom_call" | custom-call | bytes 2097152 | tf_op jit(solution)/shard_map/pallas_call | solution.py:530
  11.6 0.0 collective-permute-start.2
  11.6 1.3 %collective-permute-start.3 = (f32[9,8,128]{2,1,0:T(8,128)S(1)}, f32[9,8,128]{2,1,0:T(8,128)S(1)}, u32[]{:S(2)}, u32[]{:S(2)}) collective-permute-start(f32[9,8,128]{2,1,0:T(8,128)S(1)} %get-tuple-element.35), channel_id=1, source_target_pairs={{1,2},{3,0},{2,1},{0,3},{5,6},{7,4},{6,5},{4,7},{9,10},{11,8},{10,... | collective-permute-start | bytes 110600 | tf_op jit(solution)/shard_map/ppermute | solution.py:470
  12.9 2.2 %shard_map.67.outer_ref = f32[3,6,64,128]{3,2,1,0:T(8,128)S(1)} custom-call(f32[3,8,64,128]{3,2,1,0:T(8,128)S(1)} %get-tuple-element.28.start_ref, f32[3,6,64,128]{3,2,1,0:T(8,128)S(1)} %get-tuple-element.37.halo_ref, f32[2,14,128]{2,1,0:T(8,128)S(1)} %get-tuple-element.31.wide_ref, f32[3,6,64,128]{3,2,1,0:T(8,128)S(1)} %get-tuple-element.38.c1_ref, ...), custom_call_target="tpu_custom_call" | custom-call | bytes 6291456 | tf_op jit(solution)/shard_map/pallas_call | solution.py:536
  15.2 0.0 collective-permute-done.2.a_ref
  15.2 0.5 collective-permute-done.3.b_ref
  15.7 2.4 %shard_map.68 = (f32[3,8,8,128]{3,2,1,0:T(8,128)S(1)}, f32[24,128]{1,0:T(8,128)S(1)}) custom-call(f32[2,14,128]{2,1,0:T(8,128)S(1)} %get-tuple-element.31.wide_ref, f32[26,8,128]{2,1,0:T(8,128)S(1)} %get-tuple-element.32.left_ref, f32[26,8,128]{2,1,0:T(8,128)S(1)} %get-tuple-element.33.right_ref, f32[9,8,128]{2,1,0:T(8,128)S(1)} %collective-permute-done.2.a_ref, ...), custom_call_target="tpu_custom_call" | custom-call | bytes 2097152 | tf_op jit(solution)/shard_map/pallas_call | solution.py:540
  18.2 7.6 %collective-permute-start.4 = (f32[24,128]{1,0:T(8,128)S(1)}, f32[24,128]{1,0:T(8,128)S(1)}, u32[]{:S(2)}, u32[]{:S(2)}) collective-permute-start(f32[24,128]{1,0:T(8,128)S(1)} %get-tuple-element.40), channel_id=1, source_target_pairs={{0,4},{1,5},{2,6},{3,7},{4,0},{5,1},{6,2},{7,3},{8,12},{9,13},{10,... | collective-permute-start | bytes 36872 | tf_op jit(solution)/shard_map/ppermute | solution.py:481
  25.8 0.8 %collective-permute-done.4 = f32[24,128]{1,0:T(8,128)S(1)} collective-permute-done((f32[24,128]{1,0:T(8,128)S(1)}, f32[24,128]{1,0:T(8,128)S(1)}, u32[]{:S(2)}, u32[]{:S(2)}) %collective-permute-start.4) | collective-permute-done | bytes 12320 | tf_op jit(solution)/shard_map/ppermute | solution.py:481
  26.6 0.0 collective-permute-start.5
  26.6 3.1 %collective-permute-done.5 = f32[24,128]{1,0:T(8,128)S(1)} collective-permute-done((f32[24,128]{1,0:T(8,128)S(1)}, f32[24,128]{1,0:T(8,128)S(1)}, u32[]{:S(2)}, u32[]{:S(2)}) %collective-permute-start.5) | collective-permute-done | bytes 12320 | tf_op jit(solution)/shard_map/ppermute | solution.py:481
  29.7 2.0 %collective-permute-start.6 = (f32[24,128]{1,0:T(8,128)S(1)}, f32[24,128]{1,0:T(8,128)S(1)}, u32[]{:S(2)}, u32[]{:S(2)}) collective-permute-start(f32[24,128]{1,0:T(8,128)S(1)} %add.25), channel_id=1, source_target_pairs={{0,7},{1,6},{2,5},{3,4},{4,3},{5,2},{6,1},{7,0},{8,15},{9,14},{10,... | collective-permute-start | bytes 36872 | tf_op jit(solution)/shard_map/ppermute | solution.py:481
  31.8 2.3 %collective-permute-done.6 = f32[24,128]{1,0:T(8,128)S(1)} collective-permute-done((f32[24,128]{1,0:T(8,128)S(1)}, f32[24,128]{1,0:T(8,128)S(1)}, u32[]{:S(2)}, u32[]{:S(2)}) %collective-permute-start.6) | collective-permute-done | bytes 12320 | tf_op jit(solution)/shard_map/ppermute | solution.py:481
  34.1 0.0 collective-permute-start.7
  34.1 3.1 %collective-permute-done.7 = f32[24,128]{1,0:T(8,128)S(1)} collective-permute-done((f32[24,128]{1,0:T(8,128)S(1)}, f32[24,128]{1,0:T(8,128)S(1)}, u32[]{:S(2)}, u32[]{:S(2)}) %collective-permute-start.7) | collective-permute-done | bytes 12320 | tf_op jit(solution)/shard_map/ppermute | solution.py:481
  37.2 0.7 %collective-permute-start.8 = (f32[24,128]{1,0:T(8,128)S(1)}, f32[24,128]{1,0:T(8,128)S(1)}, u32[]{:S(2)}, u32[]{:S(2)}) collective-permute-start(f32[24,128]{1,0:T(8,128)S(1)} %add.27), channel_id=1, source_target_pairs={{0,196},{1,197},{2,198},{3,199},{4,192},{5,193},{6,194},{7,195},{8... | collective-permute-start | bytes 36872 | tf_op jit(solution)/shard_map/ppermute | solution.py:481
  37.9 3.6 %collective-permute-done.8 = f32[24,128]{1,0:T(8,128)S(1)} collective-permute-done((f32[24,128]{1,0:T(8,128)S(1)}, f32[24,128]{1,0:T(8,128)S(1)}, u32[]{:S(2)}, u32[]{:S(2)}) %collective-permute-start.8) | collective-permute-done | bytes 12320 | tf_op jit(solution)/shard_map/ppermute | solution.py:481
  41.5 0.0 collective-permute-start.9
  41.5 3.1 %collective-permute-done.9 = f32[24,128]{1,0:T(8,128)S(1)} collective-permute-done((f32[24,128]{1,0:T(8,128)S(1)}, f32[24,128]{1,0:T(8,128)S(1)}, u32[]{:S(2)}, u32[]{:S(2)}) %collective-permute-start.9) | collective-permute-done | bytes 12320 | tf_op jit(solution)/shard_map/ppermute | solution.py:481
  44.6 0.0 collective-permute-start.10
  44.6 4.1 %collective-permute-done.10 = f32[24,128]{1,0:T(8,128)S(1)} collective-permute-done((f32[24,128]{1,0:T(8,128)S(1)}, f32[24,128]{1,0:T(8,128)S(1)}, u32[]{:S(2)}, u32[]{:S(2)}) %collective-permute-start.10) | collective-permute-done | bytes 12320 | tf_op jit(solution)/shard_map/ppermute | solution.py:481
  48.8 0.7 %collective-permute-start.11 = (f32[24,128]{1,0:T(8,128)S(1)}, f32[24,128]{1,0:T(8,128)S(1)}, u32[]{:S(2)}, u32[]{:S(2)}) collective-permute-start(f32[24,128]{1,0:T(8,128)S(1)} %add.30), channel_id=1, source_target_pairs={{0,52},{1,53},{2,54},{3,55},{4,48},{5,49},{6,50},{7,51},{8,60},{9,... | collective-permute-start | bytes 36872 | tf_op jit(solution)/shard_map/ppermute | solution.py:481
  49.5 0.3 shard_map.69
  49.8 4.2 %collective-permute-done.11 = f32[24,128]{1,0:T(8,128)S(1)} collective-permute-done((f32[24,128]{1,0:T(8,128)S(1)}, f32[24,128]{1,0:T(8,128)S(1)}, u32[]{:S(2)}, u32[]{:S(2)}) %collective-permute-start.11) | collective-permute-done | bytes 12320 | tf_op jit(solution)/shard_map/ppermute | solution.py:481
  54.0 3.4 %shard_map.70 = f32[1536,128]{1,0:T(8,128)} custom-call(f32[24,128]{1,0:T(8,128)S(1)} %add.31.sum_ref, bf16[3,8,64,128]{3,2,1,0:T(8,128)(2,1)S(1)} %get-tuple-element.42.big_ref, bf16[3,8,64,128]{3,2,1,0:T(8,128)(2,1)S(1)} %get-tuple-element.43.small_ref, f32[24,128]{1,0:T(8,128)S(1)} %get-tuple-element.44.mean_ref), custom_call_target="tpu_custom_call" | custom-call | bytes 2097152 | tf_op jit(solution)/shard_map/pallas_call | solution.py:556
  (8 shorter events, 0.0 us)
Async XLA Ops:
  1.3 5.4 %collective-permute-start = (f32[584,128]{1,0:T(8,128)S(1)}, f32[584,128]{1,0:T(8,128)S(1)}, u32[]{:S(2)}, u32[]{:S(2)}) collective-permute-start(f32[584,128]{1,0:T(8,128)S(1)} %get-tuple-element.25), channel_id=1, source_target_pairs={{0,4},{8,12},{16,20},{24,28},{32,36},{40,44},{48,52},{56,60},{64,6... | collective-permute-start | bytes 897032 | tf_op jit(solution)/shard_map/ppermute | solution.py:470
  4.5 6.2 %collective-permute-start.1 = (f32[584,128]{1,0:T(8,128)S(1)}, f32[584,128]{1,0:T(8,128)S(1)}, u32[]{:S(2)}, u32[]{:S(2)}) collective-permute-start(f32[584,128]{1,0:T(8,128)S(1)} %get-tuple-element.26), channel_id=1, source_target_pairs={{4,8},{12,16},{20,24},{28,32},{36,40},{44,48},{52,56},{60,64},{68,... | collective-permute-start | bytes 897032 | tf_op jit(solution)/shard_map/ppermute | solution.py:470
  11.6 3.6 %collective-permute-start.2 = (f32[9,8,128]{2,1,0:T(8,128)S(1)}, f32[9,8,128]{2,1,0:T(8,128)S(1)}, u32[]{:S(2)}, u32[]{:S(2)}) collective-permute-start(f32[9,8,128]{2,1,0:T(8,128)S(1)} %get-tuple-element.34), channel_id=1, source_target_pairs={{0,1},{2,3},{1,0},{3,2},{4,5},{6,7},{5,4},{7,6},{8,9},{10,11},{9,8... | collective-permute-start | bytes 110600 | tf_op jit(solution)/shard_map/ppermute | solution.py:470
  11.6 4.1 %collective-permute-start.3 = (f32[9,8,128]{2,1,0:T(8,128)S(1)}, f32[9,8,128]{2,1,0:T(8,128)S(1)}, u32[]{:S(2)}, u32[]{:S(2)}) collective-permute-start(f32[9,8,128]{2,1,0:T(8,128)S(1)} %get-tuple-element.35), channel_id=1, source_target_pairs={{1,2},{3,0},{2,1},{0,3},{5,6},{7,4},{6,5},{4,7},{9,10},{11,8},{10,... | collective-permute-start | bytes 110600 | tf_op jit(solution)/shard_map/ppermute | solution.py:470
  18.2 8.4 %collective-permute-start.4 = (f32[24,128]{1,0:T(8,128)S(1)}, f32[24,128]{1,0:T(8,128)S(1)}, u32[]{:S(2)}, u32[]{:S(2)}) collective-permute-start(f32[24,128]{1,0:T(8,128)S(1)} %get-tuple-element.40), channel_id=1, source_target_pairs={{0,4},{1,5},{2,6},{3,7},{4,0},{5,1},{6,2},{7,3},{8,12},{9,13},{10,... | collective-permute-start | bytes 36872 | tf_op jit(solution)/shard_map/ppermute | solution.py:481
  26.6 3.1 %collective-permute-start.5 = (f32[24,128]{1,0:T(8,128)S(1)}, f32[24,128]{1,0:T(8,128)S(1)}, u32[]{:S(2)}, u32[]{:S(2)}) collective-permute-start(f32[24,128]{1,0:T(8,128)S(1)} %add.24), channel_id=1, source_target_pairs={{0,5},{1,4},{2,7},{3,6},{4,1},{5,0},{6,3},{7,2},{8,13},{9,12},{10,... | collective-permute-start | bytes 36872 | tf_op jit(solution)/shard_map/ppermute | solution.py:481
  29.7 4.3 %collective-permute-start.6 = (f32[24,128]{1,0:T(8,128)S(1)}, f32[24,128]{1,0:T(8,128)S(1)}, u32[]{:S(2)}, u32[]{:S(2)}) collective-permute-start(f32[24,128]{1,0:T(8,128)S(1)} %add.25), channel_id=1, source_target_pairs={{0,7},{1,6},{2,5},{3,4},{4,3},{5,2},{6,1},{7,0},{8,15},{9,14},{10,... | collective-permute-start | bytes 36872 | tf_op jit(solution)/shard_map/ppermute | solution.py:481
  34.1 3.1 %collective-permute-start.7 = (f32[24,128]{1,0:T(8,128)S(1)}, f32[24,128]{1,0:T(8,128)S(1)}, u32[]{:S(2)}, u32[]{:S(2)}) collective-permute-start(f32[24,128]{1,0:T(8,128)S(1)} %add.26), channel_id=1, source_target_pairs={{0,68},{1,69},{2,70},{3,71},{4,64},{5,65},{6,66},{7,67},{8,76},{9,... | collective-permute-start | bytes 36872 | tf_op jit(solution)/shard_map/ppermute | solution.py:481
  37.2 4.3 %collective-permute-start.8 = (f32[24,128]{1,0:T(8,128)S(1)}, f32[24,128]{1,0:T(8,128)S(1)}, u32[]{:S(2)}, u32[]{:S(2)}) collective-permute-start(f32[24,128]{1,0:T(8,128)S(1)} %add.27), channel_id=1, source_target_pairs={{0,196},{1,197},{2,198},{3,199},{4,192},{5,193},{6,194},{7,195},{8... | collective-permute-start | bytes 36872 | tf_op jit(solution)/shard_map/ppermute | solution.py:481
  41.5 3.1 %collective-permute-start.9 = (f32[24,128]{1,0:T(8,128)S(1)}, f32[24,128]{1,0:T(8,128)S(1)}, u32[]{:S(2)}, u32[]{:S(2)}) collective-permute-start(f32[24,128]{1,0:T(8,128)S(1)} %add.28), channel_id=1, source_target_pairs={{0,12},{1,13},{2,14},{3,15},{4,8},{5,9},{6,10},{7,11},{8,4},{9,5},... | collective-permute-start | bytes 36872 | tf_op jit(solution)/shard_map/ppermute | solution.py:481
  44.6 4.1 %collective-permute-start.10 = (f32[24,128]{1,0:T(8,128)S(1)}, f32[24,128]{1,0:T(8,128)S(1)}, u32[]{:S(2)}, u32[]{:S(2)}) collective-permute-start(f32[24,128]{1,0:T(8,128)S(1)} %add.29), channel_id=1, source_target_pairs={{0,20},{1,21},{2,22},{3,23},{4,16},{5,17},{6,18},{7,19},{8,28},{9,... | collective-permute-start | bytes 36872 | tf_op jit(solution)/shard_map/ppermute | solution.py:481
  48.8 5.2 %collective-permute-start.11 = (f32[24,128]{1,0:T(8,128)S(1)}, f32[24,128]{1,0:T(8,128)S(1)}, u32[]{:S(2)}, u32[]{:S(2)}) collective-permute-start(f32[24,128]{1,0:T(8,128)S(1)} %add.30), channel_id=1, source_target_pairs={{0,52},{1,53},{2,54},{3,55},{4,48},{5,49},{6,50},{7,51},{8,60},{9,... | collective-permute-start | bytes 36872 | tf_op jit(solution)/shard_map/ppermute | solution.py:481

commit v5 on v4

--- a/solution.py
+++ b/solution.py
@@ -128,11 +128,9 @@
     odd_y = lax.rem(lax.axis_index("gy"), 2) == 1
     field = lax.rem(lanes(), WIDE) // HALO
     outside = tuple(range(HALO)) + tuple(range(HALO + ROWS, EXT))
-    place_x = lax.axis_index("gx")
-    inside = (place_x > 0) & (place_x < lax.axis_size("gx") - 1)
 
     def halves(cut):
-        near, far = near_ref[cut, :], jnp.where(inside, far_ref[cut, :], 0.0)
+        near, far = near_ref[cut, :], far_ref[cut, :]
         return jnp.where(odd_x, near, far), jnp.where(odd_x, far, near)
 
     above, below = halves(slice(EDGE, EDGE + 8))
@@ -228,58 +226,9 @@
 OUTER = tuple(range(HALO)) + tuple(range(ROWS - HALO, ROWS))
 
 
-def outer(start_ref, halo_ref, wide_ref, c1_ref, c2_ref, last_ref, geo, s1, s2):
-    for r in range(EXT):
-        geo[0, r] = spread(wide_ref[0, r : r + 1, :])
-        geo[1, r] = spread(0.3 * wide_ref[1, r : r + 1, :])
-
-    def block(m, carry):
-        at = pl.ds(pl.multiple_of(m * 8, 8), 8)
-
-        def first(f, r):
-            if r < HALO:
-                return halo_ref[f, r, at, :]
-            if r < HALO + ROWS:
-                return start_ref[f, r - HALO, at, :]
-            return halo_ref[f, r - ROWS, at, :]
-
-        for stage in range(3):
-
-            def read(f, r):
-                if stage == 0:
-                    return first(f, r)
-                inside = HALO + stage
-                if inside <= r < EXT - inside:
-                    return (c1_ref, c2_ref)[stage - 1][f, r - inside, at, :]
-                return (s1, s2)[stage - 1][f, r]
-
-            def write(f, r, new):
-                if stage < 2:
-                    (s1, s2)[stage][f, r] = new
-                else:
-                    last_ref[f, OUTER.index(r - HALO), at, :] = new
-
-            low, high = stage + 1, stage + 1 + HALO
-            advance(stage, range(low, high), first, read, geo, write)
-            advance(stage, range(EXT - high, EXT - low), first, read, geo, write)
-        return carry
-
-    lax.fori_loop(0, BLOCKS, block, 0)
-
-
-def final_row(f, r, at, inner_ref, outer_ref):
-    return outer_ref[f, OUTER.index(r), at, :] if r in OUTER else inner_ref[f, r - HALO, at, :]
-
-
-def mended(edge, r, value):
-    lane = lanes()
-    border = (lane < HALO) | (lane >= COLS - HALO)
-    return jnp.where(border, turn(edge, -(WIDE * (r + HALO) + HALO)), value)
-
-
-def observe(
-    wide_ref, left_ref, right_ref, a_ref, b_ref, inner_ref, outer_ref, cells_hbm, values_hbm, error_hbm,
-    edge_ref, part_ref, seen, cells_ref, values_ref, error_ref, sems,
+def outer(
+    start_ref, halo_ref, wide_ref, c1_ref, c2_ref, cells_hbm, values_hbm, error_hbm,
+    last_ref, cell_ref, weight_ref, geo, s1, s2, cells_ref, values_ref, error_ref, sems,
 ):
     loads = [
         pltpu.make_async_copy(source, target, sems.at[i])
@@ -289,6 +238,66 @@
     ]
     for load in loads:
         load.start()
+    for r in range(EXT):
+        geo[0, r] = spread(wide_ref[0, r : r + 1, :])
+        geo[1, r] = spread(0.3 * wide_ref[1, r : r + 1, :])
+
+    def block(m, carry):
+        at = pl.ds(pl.multiple_of(m * 8, 8), 8)
+
+        def first(f, r):
+            if r < HALO:
+                return halo_ref[f, r, at, :]
+            if r < HALO + ROWS:
+                return start_ref[f, r - HALO, at, :]
+            return halo_ref[f, r - ROWS, at, :]
+
+        for stage in range(3):
+
+            def read(f, r):
+                if stage == 0:
+                    return first(f, r)
+                inside = HALO + stage
+                if inside <= r < EXT - inside:
+                    return (c1_ref, c2_ref)[stage - 1][f, r - inside, at, :]
+                return (s1, s2)[stage - 1][f, r]
+
+            def write(f, r, new):
+                if stage < 2:
+                    (s1, s2)[stage][f, r] = new
+                else:
+                    last_ref[f, OUTER.index(r - HALO), at, :] = new
+
+            low, high = stage + 1, stage + 1 + HALO
+            advance(stage, range(low, high), first, read, geo, write)
+            advance(stage, range(EXT - high, EXT - low), first, read, geo, write)
+        return carry
+
+    lax.fori_loop(0, BLOCKS, block, 0)
+    for load in loads:
+        load.wait()
+    cell = jnp.broadcast_to(cells_ref[...], (8, OBS))
+    cell_ref[0] = cell // COLS
+    cell_ref[1] = lax.rem(cell, COLS)
+    error = error_ref[...]
+    weight_ref[0:1, :] = 1.0 / (error * np.sqrt(np.float32(MEMBERS - 1)))
+    weight_ref[1:2, :] = 1.0 / error
+    weight_ref[2:3, :] = values_ref[...]
+
+
+def final_row(f, r, at, inner_ref, outer_ref):
+    return outer_ref[f, OUTER.index(r), at, :] if r in OUTER else inner_ref[f, r - HALO, at, :]
+
+
+def mended(edge, r, value):
+    lane = lanes()
+    border = (lane < HALO) | (lane >= COLS - HALO)
+    return jnp.where(border, turn(edge, -(WIDE * (r + HALO) + HALO)), value)
+
+
+def observe(
+    left_ref, right_ref, a_ref, b_ref, inner_ref, outer_ref, cell_ref, weight_ref, edge_ref, part_ref, seen
+):
     place_y = lax.axis_index("gy")
     odd_y = lax.rem(place_y, 2) == 1
     inside = (place_y > 0) & (place_y < lax.axis_size("gy") - 1)
@@ -305,6 +314,8 @@
 
     depth_sides = sides(BLOCKS, 0, FIELDS * BLOCKS)
     land_sides = [0.3 * value for value in sides(BLOCKS, 1, FIELDS * BLOCKS + 1)]
+
+    cell_row, cell_col = cell_ref[0], cell_ref[1]
 
     def strip(m, carry):
         fields = [sides(m, f, f * BLOCKS + m) for f in range(FIELDS)]
@@ -323,20 +334,11 @@
                 )
                 now = [combine(stage, first[f], now[f], land_sides[side] * change[f]) for f in range(FIELDS)]
             done.append(now)
+        edges = [jnp.where(column >= HALO, done[0][f], done[1][f]) for f in range(FIELDS)]
         for f in range(FIELDS):
-            edge_ref[f, m] = jnp.where(column >= HALO, done[0][f], done[1][f])
-        return carry
-
-    lax.fori_loop(0, BLOCKS, strip, 0, unroll=4)
-    for load in loads:
-        load.wait()
-    cell = jnp.broadcast_to(cells_ref[...], (8, OBS))
-    cell_row, cell_col = cell // COLS, lax.rem(cell, COLS)
-
-    def look(m, carry):
+            edge_ref[f, m] = edges[f]
         at = pl.ds(pl.multiple_of(m * 8, 8), 8)
-        edge = edge_ref[0, m]
-        heights = [mended(edge, r, final_row(0, r, at, inner_ref, outer_ref)) for r in range(ROWS)]
+        heights = [mended(edges[0], r, final_row(0, r, at, inner_ref, outer_ref)) for r in range(ROWS)]
         for part in range(OBS // COLS):
             cut = slice(part * COLS, (part + 1) * COLS)
             got = jnp.zeros((8, COLS), F32)
@@ -346,12 +348,11 @@
             seen[at, cut] = got
         return carry
 
-    lax.fori_loop(0, BLOCKS, look, 0, unroll=4)
+    lax.fori_loop(0, BLOCKS, strip, 0, unroll=4)
     everything = seen[...]
     obs_mean = jnp.sum(everything, axis=0, keepdims=True) * (1.0 / MEMBERS)
-    error = error_ref[...]
-    scaled = (everything - obs_mean) * (1.0 / (error * np.sqrt(np.float32(MEMBERS - 1))))
-    innovation = (values_ref[...] - obs_mean) / error
+    scaled = (everything - obs_mean) * weight_ref[0:1, :]
+    innovation = (weight_ref[2:3, :] - obs_mean) * weight_ref[1:2, :]
     product = lax.dot_general(
         jnp.concatenate([scaled, jnp.broadcast_to(innovation, (8, OBS))], axis=0),
         scaled,
@@ -470,8 +471,8 @@
     return lax.ppermute(value, axis, [(a, b) for a, b in pairs] + [(b, a) for a, b in pairs])
 
 
-def pairs_of(count, first):
-    return [(i, (i + 1) % count) for i in range(first, count, 2)]
+def pairs_of(count, first, wrap=False):
+    return [(i, (i + 1) % count) for i in range(first, count if wrap else count - 1, 2)]
 
 
 def summed(part):
@@ -530,25 +531,32 @@
     halo, wide, left, right, a, b = call(
         strips, (outside, shape(2, EXT, COLS), own, own, tile, tile), vmem(5)
     )(near, far, geo, own_left, own_right)
-    b = swap(b, "gy", pairs_of(4, 1))
+    b = swap(b, "gy", pairs_of(4, 1, wrap=True))
     a = swap(a, "gy", pairs_of(4, 0))
     rows = pltpu.VMEM((FIELDS, EXT, 8, COLS), F32)
-    (last,) = call(
-        outer, (outside,), vmem(5), [pltpu.VMEM((2, EXT, 8, COLS), F32), rows, rows], moved=6 * 2**20
-    )(start, halo, wide, c1, c2)
     line = pltpu.VMEM((1, OBS), F32)
-    edge, part = call(
-        observe,
-        (shape(FIELDS, BLOCKS, 8, COLS), shape(24, COLS)),
-        vmem(7) + hbm(3),
-        [pltpu.VMEM((MEMBERS, OBS), F32), pltpu.VMEM((1, OBS), jnp.int32), line, line, dma((3,))],
+    last, cell, weight = call(
+        outer,
+        (outside, jax.ShapeDtypeStruct((2, 8, OBS), jnp.int32), shape(8, OBS)),
+        vmem(5) + hbm(3),
+        [
+            pltpu.VMEM((2, EXT, 8, COLS), F32), rows, rows,
+            pltpu.VMEM((1, OBS), jnp.int32), line, line, dma((3,)),
+        ],
+        moved=6 * 2**20,
     )(
-        wide, left, right, a, b, c3, last,
+        start, halo, wide, c1, c2,
         *[
             pltpu.with_memory_space_constraint(value.reshape(1, OBS), pltpu.HBM)
             for value in (obs_cells, obs_values, obs_error)
         ],
     )
+    edge, part = call(
+        observe,
+        (shape(FIELDS, BLOCKS, 8, COLS), shape(24, COLS)),
+        vmem(8),
+        [pltpu.VMEM((MEMBERS, OBS), F32)],
+    )(left, right, a, b, c3, last, cell, weight)
     half = shape(FIELDS, ROWS, MEMBERS, COLS, dtype=BF16)
     big, small, mean = call(
         deviate, (half, half, shape(FIELDS * ROWS, COLS)), vmem(3), moved=4 * 2**20

time: 57.5 us -> 56.9 us (0.990)
  waiting for transfers between devices: 29 us -> 24.7 us
  starting transfers between devices: 15.7 us -> 19.4 us
    ppermute x8, waiting for transfers between devices: 24.4 us -> 19.9 us  [summed(): part = part + lax.ppermute(part, ('gx', 'gy'), pairs)]
    ppermute x4, starting transfers between devices: 4.62 us -> 6.53 us  [swap(): lax.ppermute(value, axis, [(a, b) for a, b in pairs] + [(b, a) for a, b i...]
    ppermute x8, starting transfers between devices: 11.1 us -> 12.9 us  [summed(): part = part + lax.ppermute(part, ('gx', 'gy'), pairs)]
where the time goes in v5:
time: 56.9 us; the launch traced here: 56.8 us
  waiting for transfers between devices  24.7 us (43%)
  starting transfers between devices  19.4 us (34%)
  Pallas kernels  12.5 us (22%)
    ppermute x8, waiting for transfers between devices, summed(): part = part + lax.ppermute(part, ('gx', 'gy'), pairs)  19.9 us
    ppermute x8, starting transfers between devices, summed(): part = part + lax.ppermute(part, ('gx', 'gy'), pairs)  12.9 us
    ppermute x4, starting transfers between devices, swap(): lax.ppermute(value, axis, [(a, b) for a, b in pairs] + [(b, a) for a, b i...  6.53 us
    ppermute x4, waiting for transfers between devices, swap(): lax.ppermute(value, axis, [(a, b) for a, b in pairs] + [(b, a) for a, b i...  4.78 us
    pallas_call x1, Pallas kernels, local(): call(analyse, (shape(*x.shape),), vmem(4), [pltpu.VMEM(x.shape, F32), plt...  3.4 us
    pallas_call x1, Pallas kernels, local(): call(outer, (outside, jax.ShapeDtypeStruct((2, 8, OBS), jnp.int32), shape...  2.3 us
    pallas_call x1, Pallas kernels, local(): call(observe, (shape(FIELDS, BLOCKS, 8, COLS), shape(24, COLS)), vmem(8),...  2.27 us
    pallas_call x1, Pallas kernels, local(): call(interior, (own, own) + tuple((shape(FIELDS, count, MEMBERS, COLS) fo...  2.14 us
  transfers between devices with their start and end apart: 12, of which 10 were waited for; matrix products, arithmetic and copies ran while one was open for 0% of the time, Pallas kernels for 8%

profile of v5, /device:TPU:1, one launch (start us, length us, event | category | flops | bytes accessed | tf_op | source)
XLA Modules:
  0.0 56.8 jit_solution(10834992740610982891)
XLA Ops:
  0.0 1.2 %shard_map.64 = (f32[3,8,64,128]{3,2,1,0:T(8,128)S(1)}, f32[2,8,128]{2,1,0:T(8,128)S(1)}, f32[584,128]{1,0:T(8,128)S(1)}, f32[584,128]{1,0:T(8,128)S(1)}) custom-call(f32[1536,128]{1,0:T(8,128)} %bitcast.5, s32[8,128]{1,0:T(8,128)} %depth_hbm.1, s32[8,128]{1,0:T(8,128)} %land_hbm.1), custom_call_target="tpu_custom_call" | custom-call | bytes 2097152 | tf_op jit(solution)/shard_map/pallas_call | solution.py:510
  1.3 3.3 %collective-permute-start = (f32[584,128]{1,0:T(8,128)S(1)}, f32[584,128]{1,0:T(8,128)S(1)}, u32[]{:S(2)}, u32[]{:S(2)}) collective-permute-start(f32[584,128]{1,0:T(8,128)S(1)} %get-tuple-element.28), channel_id=1, source_target_pairs={{0,4},{8,12},{16,20},{24,28},{32,36},{40,44},{48,52},{56,60},{64,6... | collective-permute-start | bytes 897032 | tf_op jit(solution)/shard_map/ppermute | solution.py:471
  4.5 1.9 %collective-permute-start.1 = (f32[584,128]{1,0:T(8,128)S(1)}, f32[584,128]{1,0:T(8,128)S(1)}, u32[]{:S(2)}, u32[]{:S(2)}) collective-permute-start(f32[584,128]{1,0:T(8,128)S(1)} %get-tuple-element.29), channel_id=1, source_target_pairs={{4,8},{12,16},{20,24},{28,32},{36,40},{44,48},{52,56},{60,64},{68,... | collective-permute-start | bytes 897032 | tf_op jit(solution)/shard_map/ppermute | solution.py:471
  6.5 2.1 %shard_map.65 = (f32[26,8,128]{2,1,0:T(8,128)S(1)}, f32[26,8,128]{2,1,0:T(8,128)S(1)}, f32[3,6,64,128]{3,2,1,0:T(8,128)S(1)}, f32[3,4,64,128]{3,2,1,0:T(8,128)S(1)}, f32[3,2,64,128]{3,2,1,0:T(8,128)S(1)}) custom-call(f32[3,8,64,128]{3,2,1,0:T(8,128)S(1)} %get-tuple-element.31.start_ref, f32[2,8,128]{2,1,0:T(8,128)S(1)} %get-tuple-element.30.geo_ref), custom_call_target="tpu_custom_call" | custom-call | bytes 8388608 | tf_op jit(solution)/shard_map/pallas_call | solution.py:522
  8.6 0.0 collective-permute-done.near_ref
  8.6 4.3 %collective-permute-done.1.far_ref = f32[584,128]{1,0:T(8,128)S(1)} collective-permute-done((f32[584,128]{1,0:T(8,128)S(1)}, f32[584,128]{1,0:T(8,128)S(1)}, u32[]{:S(2)}, u32[]{:S(2)}) %collective-permute-start.1) | collective-permute-done | bytes 299040 | tf_op jit(solution)/shard_map/ppermute | solution.py:471
  12.9 0.9 %shard_map.66 = (f32[3,6,64,128]{3,2,1,0:T(8,128)S(1)}, f32[2,14,128]{2,1,0:T(8,128)S(1)}, f32[26,8,128]{2,1,0:T(8,128)S(1)}, f32[26,8,128]{2,1,0:T(8,128)S(1)},...) custom-call(f32[584,128]{1,0:T(8,128)S(1)} %collective-permute-done.near_ref, ...), custom_call_target="tpu_custom_call" | custom-call | bytes 2097152 | tf_op jit(solution)/shard_map/pallas_call | solution.py:531
  13.8 0.0 collective-permute-start.2
  13.8 1.3 %collective-permute-start.3 = (f32[9,8,128]{2,1,0:T(8,128)S(1)}, f32[9,8,128]{2,1,0:T(8,128)S(1)}, u32[]{:S(2)}, u32[]{:S(2)}) collective-permute-start(f32[9,8,128]{2,1,0:T(8,128)S(1)} %get-tuple-element.37), channel_id=1, source_target_pairs={{1,2},{3,0},{2,1},{0,3},{5,6},{7,4},{6,5},{4,7},{9,10},{11,8},{10,... | collective-permute-start | bytes 110600 | tf_op jit(solution)/shard_map/ppermute | solution.py:471
  15.1 2.3 %shard_map.67 = (f32[3,6,64,128]{3,2,1,0:T(8,128)S(1)}, s32[2,8,256]{2,1,0:T(8,128)S(1)}, f32[8,256]{1,0:T(8,128)S(1)}) custom-call(f32[3,8,64,128]{3,2,1,0:T(8,128)S(1)} %get-tuple-element.31.start_ref, f32[3,6,64,128]{3,2,1,0:T(8,128)S(1)} %get-tuple-element.39.halo_ref, f32[2,14,128]{2,1,0:T(8,128)S(1)} %get-tuple-element.40.wide_ref, ...), custom_call_target="tpu_custom_call" | custom-call | bytes 6291456 | tf_op jit(solution)/shard_map/pallas_call | solution.py:538
  17.4 0.0 collective-permute-done.2.a_ref
  17.4 0.5 collective-permute-done.3.b_ref
  17.9 2.3 %shard_map.68 = (f32[3,8,8,128]{3,2,1,0:T(8,128)S(1)}, f32[24,128]{1,0:T(8,128)S(1)}) custom-call(f32[26,8,128]{2,1,0:T(8,128)S(1)} %get-tuple-element.34.left_ref, f32[26,8,128]{2,1,0:T(8,128)S(1)} %get-tuple-element.35.right_ref, f32[9,8,128]{2,1,0:T(8,128)S(1)} %collective-permute-done.2.a_ref, f32[9,8,128]{2,1,0:T(8,128)S(1)} %collective-permute-done.3.b_ref, ...), custom_call_target="tpu_custom_call" | custom-call | bytes 2097152 | tf_op jit(solution)/shard_map/pallas_call | solution.py:554
  20.2 0.0 collective-permute-start.4
  20.3 1.2 %collective-permute-done.4 = f32[24,128]{1,0:T(8,128)S(1)} collective-permute-done((f32[24,128]{1,0:T(8,128)S(1)}, f32[24,128]{1,0:T(8,128)S(1)}, u32[]{:S(2)}, u32[]{:S(2)}) %collective-permute-start.4) | collective-permute-done | bytes 12320 | tf_op jit(solution)/shard_map/ppermute | solution.py:482
  21.4 0.2 collective-permute-start.5
  21.6 2.9 %collective-permute-done.5 = f32[24,128]{1,0:T(8,128)S(1)} collective-permute-done((f32[24,128]{1,0:T(8,128)S(1)}, f32[24,128]{1,0:T(8,128)S(1)}, u32[]{:S(2)}, u32[]{:S(2)}) %collective-permute-start.5) | collective-permute-done | bytes 12320 | tf_op jit(solution)/shard_map/ppermute | solution.py:482
  24.5 1.3 %collective-permute-start.6 = (f32[24,128]{1,0:T(8,128)S(1)}, f32[24,128]{1,0:T(8,128)S(1)}, u32[]{:S(2)}, u32[]{:S(2)}) collective-permute-start(f32[24,128]{1,0:T(8,128)S(1)} %add.25), channel_id=1, source_target_pairs={{0,7},{1,6},{2,5},{3,4},{4,3},{5,2},{6,1},{7,0},{8,15},{9,14},{10,... | collective-permute-start | bytes 36872 | tf_op jit(solution)/shard_map/ppermute | solution.py:482
  25.8 3.1 %collective-permute-done.6 = f32[24,128]{1,0:T(8,128)S(1)} collective-permute-done((f32[24,128]{1,0:T(8,128)S(1)}, f32[24,128]{1,0:T(8,128)S(1)}, u32[]{:S(2)}, u32[]{:S(2)}) %collective-permute-start.6) | collective-permute-done | bytes 12320 | tf_op jit(solution)/shard_map/ppermute | solution.py:482
  28.9 5.8 %collective-permute-start.7 = (f32[24,128]{1,0:T(8,128)S(1)}, f32[24,128]{1,0:T(8,128)S(1)}, u32[]{:S(2)}, u32[]{:S(2)}) collective-permute-start(f32[24,128]{1,0:T(8,128)S(1)} %add.26), channel_id=1, source_target_pairs={{0,68},{1,69},{2,70},{3,71},{4,64},{5,65},{6,66},{7,67},{8,76},{9,... | collective-permute-start | bytes 36872 | tf_op jit(solution)/shard_map/ppermute | solution.py:482
  34.7 1.4 %collective-permute-done.7 = f32[24,128]{1,0:T(8,128)S(1)} collective-permute-done((f32[24,128]{1,0:T(8,128)S(1)}, f32[24,128]{1,0:T(8,128)S(1)}, u32[]{:S(2)}, u32[]{:S(2)}) %collective-permute-start.7) | collective-permute-done | bytes 12320 | tf_op jit(solution)/shard_map/ppermute | solution.py:482
  36.1 3.5 %collective-permute-start.8 = (f32[24,128]{1,0:T(8,128)S(1)}, f32[24,128]{1,0:T(8,128)S(1)}, u32[]{:S(2)}, u32[]{:S(2)}) collective-permute-start(f32[24,128]{1,0:T(8,128)S(1)} %add.27), channel_id=1, source_target_pairs={{0,196},{1,197},{2,198},{3,199},{4,192},{5,193},{6,194},{7,195},{8... | collective-permute-start | bytes 36872 | tf_op jit(solution)/shard_map/ppermute | solution.py:482
  39.6 1.4 %collective-permute-done.8 = f32[24,128]{1,0:T(8,128)S(1)} collective-permute-done((f32[24,128]{1,0:T(8,128)S(1)}, f32[24,128]{1,0:T(8,128)S(1)}, u32[]{:S(2)}, u32[]{:S(2)}) %collective-permute-start.8) | collective-permute-done | bytes 12320 | tf_op jit(solution)/shard_map/ppermute | solution.py:482
  41.0 0.0 collective-permute-start.9
  41.0 3.1 %collective-permute-done.9 = f32[24,128]{1,0:T(8,128)S(1)} collective-permute-done((f32[24,128]{1,0:T(8,128)S(1)}, f32[24,128]{1,0:T(8,128)S(1)}, u32[]{:S(2)}, u32[]{:S(2)}) %collective-permute-start.9) | collective-permute-done | bytes 12320 | tf_op jit(solution)/shard_map/ppermute | solution.py:482
  44.1 0.0 collective-permute-start.10
  44.1 4.0 %collective-permute-done.10 = f32[24,128]{1,0:T(8,128)S(1)} collective-permute-done((f32[24,128]{1,0:T(8,128)S(1)}, f32[24,128]{1,0:T(8,128)S(1)}, u32[]{:S(2)}, u32[]{:S(2)}) %collective-permute-start.10) | collective-permute-done | bytes 12320 | tf_op jit(solution)/shard_map/ppermute | solution.py:482
  48.1 2.0 %collective-permute-start.11 = (f32[24,128]{1,0:T(8,128)S(1)}, f32[24,128]{1,0:T(8,128)S(1)}, u32[]{:S(2)}, u32[]{:S(2)}) collective-permute-start(f32[24,128]{1,0:T(8,128)S(1)} %add.30), channel_id=1, source_target_pairs={{0,52},{1,53},{2,54},{3,55},{4,48},{5,49},{6,50},{7,51},{8,60},{9,... | collective-permute-start | bytes 36872 | tf_op jit(solution)/shard_map/ppermute | solution.py:482
  50.2 0.3 shard_map.69
  50.5 2.9 %collective-permute-done.11 = f32[24,128]{1,0:T(8,128)S(1)} collective-permute-done((f32[24,128]{1,0:T(8,128)S(1)}, f32[24,128]{1,0:T(8,128)S(1)}, u32[]{:S(2)}, u32[]{:S(2)}) %collective-permute-start.11) | collective-permute-done | bytes 12320 | tf_op jit(solution)/shard_map/ppermute | solution.py:482
  53.4 3.4 %shard_map.70 = f32[1536,128]{1,0:T(8,128)} custom-call(f32[24,128]{1,0:T(8,128)S(1)} %add.31.sum_ref, bf16[3,8,64,128]{3,2,1,0:T(8,128)(2,1)S(1)} %get-tuple-element.48.big_ref, bf16[3,8,64,128]{3,2,1,0:T(8,128)(2,1)S(1)} %get-tuple-element.49.small_ref, f32[24,128]{1,0:T(8,128)S(1)} %get-tuple-element.50.mean_ref), custom_call_target="tpu_custom_call" | custom-call | bytes 2097152 | tf_op jit(solution)/shard_map/pallas_call | solution.py:564
  (8 shorter events, 0.0 us)
Async XLA Ops:
  1.3 7.4 %collective-permute-start = (f32[584,128]{1,0:T(8,128)S(1)}, f32[584,128]{1,0:T(8,128)S(1)}, u32[]{:S(2)}, u32[]{:S(2)}) collective-permute-start(f32[584,128]{1,0:T(8,128)S(1)} %get-tuple-element.28), channel_id=1, source_target_pairs={{0,4},{8,12},{16,20},{24,28},{32,36},{40,44},{48,52},{56,60},{64,6... | collective-permute-start | bytes 897032 | tf_op jit(solution)/shard_map/ppermute | solution.py:471
  4.5 8.4 %collective-permute-start.1 = (f32[584,128]{1,0:T(8,128)S(1)}, f32[584,128]{1,0:T(8,128)S(1)}, u32[]{:S(2)}, u32[]{:S(2)}) collective-permute-start(f32[584,128]{1,0:T(8,128)S(1)} %get-tuple-element.29), channel_id=1, source_target_pairs={{4,8},{12,16},{20,24},{28,32},{36,40},{44,48},{52,56},{60,64},{68,... | collective-permute-start | bytes 897032 | tf_op jit(solution)/shard_map/ppermute | solution.py:471
  13.8 3.6 %collective-permute-start.2 = (f32[9,8,128]{2,1,0:T(8,128)S(1)}, f32[9,8,128]{2,1,0:T(8,128)S(1)}, u32[]{:S(2)}, u32[]{:S(2)}) collective-permute-start(f32[9,8,128]{2,1,0:T(8,128)S(1)} %get-tuple-element.36), channel_id=1, source_target_pairs={{0,1},{2,3},{1,0},{3,2},{4,5},{6,7},{5,4},{7,6},{8,9},{10,11},{9,8... | collective-permute-start | bytes 110600 | tf_op jit(solution)/shard_map/ppermute | solution.py:471
  13.8 4.1 %collective-permute-start.3 = (f32[9,8,128]{2,1,0:T(8,128)S(1)}, f32[9,8,128]{2,1,0:T(8,128)S(1)}, u32[]{:S(2)}, u32[]{:S(2)}) collective-permute-start(f32[9,8,128]{2,1,0:T(8,128)S(1)} %get-tuple-element.37), channel_id=1, source_target_pairs={{1,2},{3,0},{2,1},{0,3},{5,6},{7,4},{6,5},{4,7},{9,10},{11,8},{10,... | collective-permute-start | bytes 110600 | tf_op jit(solution)/shard_map/ppermute | solution.py:471
  20.2 1.2 %collective-permute-start.4 = (f32[24,128]{1,0:T(8,128)S(1)}, f32[24,128]{1,0:T(8,128)S(1)}, u32[]{:S(2)}, u32[]{:S(2)}) collective-permute-start(f32[24,128]{1,0:T(8,128)S(1)} %get-tuple-element.46), channel_id=1, source_target_pairs={{0,4},{1,5},{2,6},{3,7},{4,0},{5,1},{6,2},{7,3},{8,12},{9,13},{10,... | collective-permute-start | bytes 36872 | tf_op jit(solution)/shard_map/ppermute | solution.py:482
  21.4 3.1 %collective-permute-start.5 = (f32[24,128]{1,0:T(8,128)S(1)}, f32[24,128]{1,0:T(8,128)S(1)}, u32[]{:S(2)}, u32[]{:S(2)}) collective-permute-start(f32[24,128]{1,0:T(8,128)S(1)} %add.24), channel_id=1, source_target_pairs={{0,5},{1,4},{2,7},{3,6},{4,1},{5,0},{6,3},{7,2},{8,13},{9,12},{10,... | collective-permute-start | bytes 36872 | tf_op jit(solution)/shard_map/ppermute | solution.py:482
  24.5 4.3 %collective-permute-start.6 = (f32[24,128]{1,0:T(8,128)S(1)}, f32[24,128]{1,0:T(8,128)S(1)}, u32[]{:S(2)}, u32[]{:S(2)}) collective-permute-start(f32[24,128]{1,0:T(8,128)S(1)} %add.25), channel_id=1, source_target_pairs={{0,7},{1,6},{2,5},{3,4},{4,3},{5,2},{6,1},{7,0},{8,15},{9,14},{10,... | collective-permute-start | bytes 36872 | tf_op jit(solution)/shard_map/ppermute | solution.py:482
  28.9 7.2 %collective-permute-start.7 = (f32[24,128]{1,0:T(8,128)S(1)}, f32[24,128]{1,0:T(8,128)S(1)}, u32[]{:S(2)}, u32[]{:S(2)}) collective-permute-start(f32[24,128]{1,0:T(8,128)S(1)} %add.26), channel_id=1, source_target_pairs={{0,68},{1,69},{2,70},{3,71},{4,64},{5,65},{6,66},{7,67},{8,76},{9,... | collective-permute-start | bytes 36872 | tf_op jit(solution)/shard_map/ppermute | solution.py:482
  36.1 4.9 %collective-permute-start.8 = (f32[24,128]{1,0:T(8,128)S(1)}, f32[24,128]{1,0:T(8,128)S(1)}, u32[]{:S(2)}, u32[]{:S(2)}) collective-permute-start(f32[24,128]{1,0:T(8,128)S(1)} %add.27), channel_id=1, source_target_pairs={{0,196},{1,197},{2,198},{3,199},{4,192},{5,193},{6,194},{7,195},{8... | collective-permute-start | bytes 36872 | tf_op jit(solution)/shard_map/ppermute | solution.py:482
  41.0 3.1 %collective-permute-start.9 = (f32[24,128]{1,0:T(8,128)S(1)}, f32[24,128]{1,0:T(8,128)S(1)}, u32[]{:S(2)}, u32[]{:S(2)}) collective-permute-start(f32[24,128]{1,0:T(8,128)S(1)} %add.28), channel_id=1, source_target_pairs={{0,12},{1,13},{2,14},{3,15},{4,8},{5,9},{6,10},{7,11},{8,4},{9,5},... | collective-permute-start | bytes 36872 | tf_op jit(solution)/shard_map/ppermute | solution.py:482
  44.1 4.0 %collective-permute-start.10 = (f32[24,128]{1,0:T(8,128)S(1)}, f32[24,128]{1,0:T(8,128)S(1)}, u32[]{:S(2)}, u32[]{:S(2)}) collective-permute-start(f32[24,128]{1,0:T(8,128)S(1)} %add.29), channel_id=1, source_target_pairs={{0,20},{1,21},{2,22},{3,23},{4,16},{5,17},{6,18},{7,19},{8,28},{9,... | collective-permute-start | bytes 36872 | tf_op jit(solution)/shard_map/ppermute | solution.py:482
  48.1 5.2 %collective-permute-start.11 = (f32[24,128]{1,0:T(8,128)S(1)}, f32[24,128]{1,0:T(8,128)S(1)}, u32[]{:S(2)}, u32[]{:S(2)}) collective-permute-start(f32[24,128]{1,0:T(8,128)S(1)} %add.30), channel_id=1, source_target_pairs={{0,52},{1,53},{2,54},{3,55},{4,48},{5,49},{6,50},{7,51},{8,60},{9,... | collective-permute-start | bytes 36872 | tf_op jit(solution)/shard_map/ppermute | solution.py:482

commit v6 on v5

--- a/solution.py
+++ b/solution.py
@@ -168,7 +168,7 @@
         send(m, packed)
         return carry
 
-    lax.fori_loop(0, BLOCKS, block, 0, unroll=2)
+    lax.fori_loop(0, BLOCKS, block, 0, unroll=4)
     packed = (jnp.zeros((8, COLS), F32),) * 2
     for g in range(2):
         packed = put(packed, lambda r: spread(wide_ref[g, r : r + 1, :]), g, FIELDS * BLOCKS + g)
@@ -438,7 +438,11 @@
     return [jnp.where(lane < MEMBERS, turn(value, MEMBERS), 0.0) for value in table]
 
 
-def analyse(sum_ref, big_ref, small_ref, mean_ref, out_hbm, out_ref, flip_ref, sems):
+def analyse(parts_ref, big_ref, small_ref, mean_ref, out_hbm, out_ref, flip_ref, sum_ref, sems):
+    sums = [parts_ref[i] for i in range(parts_ref.shape[0])]
+    while len(sums) > 1:
+        sums = [a + b for a, b in zip(sums[::2], sums[1::2])]
+    sum_ref[...] = sums[0]
     inverse = inverse_factor(sum_ref, flip_ref)
     projection = spread(sum_ref[16:17, :])
     weights = jnp.zeros((8, COLS), F32)
@@ -475,12 +479,22 @@
     return [(i, (i + 1) % count) for i in range(first, count if wrap else count - 1, 2)]
 
 
-def summed(part):
+def duplicate(part_ref, other_ref, out_ref):
+    value = part_ref[...] + other_ref[...]
+    for i in range(out_ref.shape[0]):
+        out_ref[i] = value
+
+
+def gathered(part):
     gx, gy = lax.axis_size("gx"), lax.axis_size("gy")
-    for flip_x, flip_y in ((1, 0), (1, 1), (1, 3), (17, 0), (49, 0), (3, 0), (5, 0), (13, 0)):
-        pairs = [(i * gy + j, (i ^ flip_x) * gy + (j ^ flip_y)) for i in range(gx) for j in range(gy)]
-        part = part + lax.ppermute(part, ("gx", "gy"), pairs)
-    return part
+    for flip in (1, 3, 5, 13):
+        pairs = [(i * gy + j, (i ^ flip) * gy + j) for i in range(gx) for j in range(gy)]
+        other = lax.ppermute(part, ("gx", "gy"), pairs)
+        if flip < 13:
+            part = part + other
+    groups = [[(y * 16 + i) * gy + x for y in range(gx // 16) for x in range(gy)] for i in range(16)]
+    (copies,) = call(duplicate, (shape(len(groups[0]), *part.shape),), vmem(2))(part, other)
+    return lax.all_to_all(copies, ("gx", "gy"), 0, 0, axis_index_groups=groups)
 
 
 def shape(*sizes, dtype=F32):
@@ -565,9 +579,9 @@
         analyse,
         (shape(*x.shape),),
         vmem(4),
-        [pltpu.VMEM(x.shape, F32), pltpu.VMEM((COLS, COLS), F32), dma((FIELDS,))],
+        [pltpu.VMEM(x.shape, F32), pltpu.VMEM((COLS, COLS), F32), pltpu.VMEM((24, COLS), F32), dma((FIELDS,))],
         out_specs=tuple(hbm(1)),
-    )(summed(part), big, small, mean)
+    )(gathered(part), big, small, mean)
     return out.reshape(FIELDS, MEMBERS, ROWS, COLS)
 
 

time: 56.9 us -> 55.4 us (0.974)
  waiting for transfers between devices: 24.7 us -> 17.2 us
  starting transfers between devices: 19.4 us -> 24.9 us
    ppermute x8 -> x4, waiting for transfers between devices: 19.9 us -> 5.39 us  [gathered(): other = lax.ppermute(part, ('gx', 'gy'), pairs)]
    all_to_all x0 -> x1, starting transfers between devices: none -> 7.43 us  [gathered(): return lax.all_to_all(copies, ('gx', 'gy'), 0, 0, axis_index_groups=groups)]
    all_to_all x0 -> x1, waiting for transfers between devices: none -> 6.88 us  [gathered(): return lax.all_to_all(copies, ('gx', 'gy'), 0, 0, axis_index_groups=groups)]
    ppermute x8 -> x4, starting transfers between devices: 12.9 us -> 11.1 us  [gathered(): other = lax.ppermute(part, ('gx', 'gy'), pairs)]
    pallas_call x0 -> x1, Pallas kernels: none -> 0.69 us  [gathered(): call(duplicate, (shape(len(groups[0]), *part.shape),), vmem(2))(part, other)]
  transfers between devices with their start and end apart: 12 -> 9, of which waited for: 10 -> 7; matrix products, arithmetic and copies ran while one was open for 0% -> 0% of each run, Pallas kernels for 8% -> 9%
where the time goes in v6:
time: 55.4 us; the launch traced here: 55.2 us
  starting transfers between devices  24.9 us (45%)
  waiting for transfers between devices  17.2 us (31%)
  Pallas kernels  13 us (23%)
    ppermute x4, starting transfers between devices, gathered(): other = lax.ppermute(part, ('gx', 'gy'), pairs)  11.1 us
    all_to_all x1, starting transfers between devices, gathered(): return lax.all_to_all(copies, ('gx', 'gy'), 0, 0, axis_index_groups=groups)  7.43 us
    all_to_all x1, waiting for transfers between devices, gathered(): return lax.all_to_all(copies, ('gx', 'gy'), 0, 0, axis_index_groups=groups)  6.88 us
    ppermute x4, starting transfers between devices, swap(): lax.ppermute(value, axis, [(a, b) for a, b in pairs] + [(b, a) for a, b i...  6.42 us
    ppermute x4, waiting for transfers between devices, gathered(): other = lax.ppermute(part, ('gx', 'gy'), pairs)  5.39 us
    ppermute x4, waiting for transfers between devices, swap(): lax.ppermute(value, axis, [(a, b) for a, b in pairs] + [(b, a) for a, b i...  4.9 us
    pallas_call x1, Pallas kernels, local(): call(analyse, (shape(*x.shape),), vmem(4), [pltpu.VMEM(x.shape, F32), plt...  3.41 us
    pallas_call x1, Pallas kernels, local(): call(outer, (outside, jax.ShapeDtypeStruct((2, 8, OBS), jnp.int32), shape...  2.3 us
  transfers between devices with their start and end apart: 9, of which 7 were waited for; matrix products, arithmetic and copies ran while one was open for 0% of the time, Pallas kernels for 9%

profile of v6, /device:TPU:1, one launch (start us, length us, event | category | flops | bytes accessed | tf_op | source)
XLA Modules:
  0.0 55.2 jit_solution(7834295766820634364)
XLA Ops:
  0.0 1.2 %shard_map.64 = (f32[3,8,64,128]{3,2,1,0:T(8,128)S(1)}, f32[2,8,128]{2,1,0:T(8,128)S(1)}, f32[584,128]{1,0:T(8,128)S(1)}, f32[584,128]{1,0:T(8,128)S(1)}) custom-call(f32[1536,128]{1,0:T(8,128)} %bitcast.5, s32[8,128]{1,0:T(8,128)} %depth_hbm.1, s32[8,128]{1,0:T(8,128)} %land_hbm.1), custom_call_target="tpu_custom_call" | custom-call | bytes 2097152 | tf_op jit(solution)/shard_map/pallas_call | solution.py:524
  1.3 3.3 %collective-permute-start = (f32[584,128]{1,0:T(8,128)S(1)}, f32[584,128]{1,0:T(8,128)S(1)}, u32[]{:S(2)}, u32[]{:S(2)}) collective-permute-start(f32[584,128]{1,0:T(8,128)S(1)} %get-tuple-element.28), channel_id=1, source_target_pairs={{0,4},{8,12},{16,20},{24,28},{32,36},{40,44},{48,52},{56,60},{64,6... | collective-permute-start | bytes 897032 | tf_op jit(solution)/shard_map/ppermute | solution.py:475
  4.5 1.9 %collective-permute-start.1 = (f32[584,128]{1,0:T(8,128)S(1)}, f32[584,128]{1,0:T(8,128)S(1)}, u32[]{:S(2)}, u32[]{:S(2)}) collective-permute-start(f32[584,128]{1,0:T(8,128)S(1)} %get-tuple-element.29), channel_id=1, source_target_pairs={{4,8},{12,16},{20,24},{28,32},{36,40},{44,48},{52,56},{60,64},{68,... | collective-permute-start | bytes 897032 | tf_op jit(solution)/shard_map/ppermute | solution.py:475
  6.5 2.1 %shard_map.65 = (f32[26,8,128]{2,1,0:T(8,128)S(1)}, f32[26,8,128]{2,1,0:T(8,128)S(1)}, f32[3,6,64,128]{3,2,1,0:T(8,128)S(1)}, f32[3,4,64,128]{3,2,1,0:T(8,128)S(1)}, f32[3,2,64,128]{3,2,1,0:T(8,128)S(1)}) custom-call(f32[3,8,64,128]{3,2,1,0:T(8,128)S(1)} %get-tuple-element.31.start_ref, f32[2,8,128]{2,1,0:T(8,128)S(1)} %get-tuple-element.30.geo_ref), custom_call_target="tpu_custom_call" | custom-call | bytes 8388608 | tf_op jit(solution)/shard_map/pallas_call | solution.py:536
  8.6 0.0 collective-permute-done.near_ref
  8.6 4.3 %collective-permute-done.1.far_ref = f32[584,128]{1,0:T(8,128)S(1)} collective-permute-done((f32[584,128]{1,0:T(8,128)S(1)}, f32[584,128]{1,0:T(8,128)S(1)}, u32[]{:S(2)}, u32[]{:S(2)}) %collective-permute-start.1) | collective-permute-done | bytes 299040 | tf_op jit(solution)/shard_map/ppermute | solution.py:475
  12.9 0.6 %shard_map.66 = (f32[3,6,64,128]{3,2,1,0:T(8,128)S(1)}, f32[2,14,128]{2,1,0:T(8,128)S(1)}, f32[26,8,128]{2,1,0:T(8,128)S(1)}, f32[26,8,128]{2,1,0:T(8,128)S(1)},...) custom-call(f32[584,128]{1,0:T(8,128)S(1)} %collective-permute-done.near_ref, ...), custom_call_target="tpu_custom_call" | custom-call | bytes 2097152 | tf_op jit(solution)/shard_map/pallas_call | solution.py:545
  13.5 0.0 collective-permute-start.2
  13.5 1.2 %collective-permute-start.3 = (f32[9,8,128]{2,1,0:T(8,128)S(1)}, f32[9,8,128]{2,1,0:T(8,128)S(1)}, u32[]{:S(2)}, u32[]{:S(2)}) collective-permute-start(f32[9,8,128]{2,1,0:T(8,128)S(1)} %get-tuple-element.37), channel_id=1, source_target_pairs={{1,2},{3,0},{2,1},{0,3},{5,6},{7,4},{6,5},{4,7},{9,10},{11,8},{10,... | collective-permute-start | bytes 110600 | tf_op jit(solution)/shard_map/ppermute | solution.py:475
  14.7 2.3 %shard_map.67 = (f32[3,6,64,128]{3,2,1,0:T(8,128)S(1)}, s32[2,8,256]{2,1,0:T(8,128)S(1)}, f32[8,256]{1,0:T(8,128)S(1)}) custom-call(f32[3,8,64,128]{3,2,1,0:T(8,128)S(1)} %get-tuple-element.31.start_ref, f32[3,6,64,128]{3,2,1,0:T(8,128)S(1)} %get-tuple-element.39.halo_ref, f32[2,14,128]{2,1,0:T(8,128)S(1)} %get-tuple-element.40.wide_ref, ...), custom_call_target="tpu_custom_call" | custom-call | bytes 6291456 | tf_op jit(solution)/shard_map/pallas_call | solution.py:552
  17.0 0.0 collective-permute-done.2.a_ref
  17.1 0.6 %collective-permute-done.3.b_ref = f32[9,8,128]{2,1,0:T(8,128)S(1)} collective-permute-done((f32[9,8,128]{2,1,0:T(8,128)S(1)}, f32[9,8,128]{2,1,0:T(8,128)S(1)}, u32[]{:S(2)}, u32[]{:S(2)}) %collective-permute-start.3) | collective-permute-done | bytes 36896 | tf_op jit(solution)/shard_map/ppermute | solution.py:475
  17.7 2.3 %shard_map.68 = (f32[3,8,8,128]{3,2,1,0:T(8,128)S(1)}, f32[24,128]{1,0:T(8,128)S(1)}) custom-call(f32[26,8,128]{2,1,0:T(8,128)S(1)} %get-tuple-element.34.left_ref, f32[26,8,128]{2,1,0:T(8,128)S(1)} %get-tuple-element.35.right_ref, f32[9,8,128]{2,1,0:T(8,128)S(1)} %collective-permute-done.2.a_ref, f32[9,8,128]{2,1,0:T(8,128)S(1)} %collective-permute-done.3.b_ref, ...), custom_call_target="tpu_custom_call" | custom-call | bytes 2097152 | tf_op jit(solution)/shard_map/pallas_call | solution.py:568
  19.9 0.0 collective-permute-start.4
  20.0 1.2 %collective-permute-done.4 = f32[24,128]{1,0:T(8,128)S(1)} collective-permute-done((f32[24,128]{1,0:T(8,128)S(1)}, f32[24,128]{1,0:T(8,128)S(1)}, u32[]{:S(2)}, u32[]{:S(2)}) %collective-permute-start.4) | collective-permute-done | bytes 12320 | tf_op jit(solution)/shard_map/ppermute | solution.py:492
  21.1 2.1 %collective-permute-start.5 = (f32[24,128]{1,0:T(8,128)S(1)}, f32[24,128]{1,0:T(8,128)S(1)}, u32[]{:S(2)}, u32[]{:S(2)}) collective-permute-start(f32[24,128]{1,0:T(8,128)S(1)} %add.9), channel_id=1, source_target_pairs={{0,12},{1,13},{2,14},{3,15},{4,8},{5,9},{6,10},{7,11},{8,4},{9,5},... | collective-permute-start | bytes 36872 | tf_op jit(solution)/shard_map/ppermute | solution.py:492
  23.2 1.4 %collective-permute-done.5 = f32[24,128]{1,0:T(8,128)S(1)} collective-permute-done((f32[24,128]{1,0:T(8,128)S(1)}, f32[24,128]{1,0:T(8,128)S(1)}, u32[]{:S(2)}, u32[]{:S(2)}) %collective-permute-start.5) | collective-permute-done | bytes 12320 | tf_op jit(solution)/shard_map/ppermute | solution.py:492
  24.6 3.3 %collective-permute-start.6 = (f32[24,128]{1,0:T(8,128)S(1)}, f32[24,128]{1,0:T(8,128)S(1)}, u32[]{:S(2)}, u32[]{:S(2)}) collective-permute-start(f32[24,128]{1,0:T(8,128)S(1)} %add.10), channel_id=1, source_target_pairs={{0,20},{1,21},{2,22},{3,23},{4,16},{5,17},{6,18},{7,19},{8,28},{9,... | collective-permute-start | bytes 36872 | tf_op jit(solution)/shard_map/ppermute | solution.py:492
  27.9 1.4 %collective-permute-done.6 = f32[24,128]{1,0:T(8,128)S(1)} collective-permute-done((f32[24,128]{1,0:T(8,128)S(1)}, f32[24,128]{1,0:T(8,128)S(1)}, u32[]{:S(2)}, u32[]{:S(2)}) %collective-permute-start.6) | collective-permute-done | bytes 12320 | tf_op jit(solution)/shard_map/ppermute | solution.py:492
  29.3 5.7 %collective-permute-start.7 = (f32[24,128]{1,0:T(8,128)S(1)}, f32[24,128]{1,0:T(8,128)S(1)}, u32[]{:S(2)}, u32[]{:S(2)}) collective-permute-start(f32[24,128]{1,0:T(8,128)S(1)} %add.11.part_ref), channel_id=1, source_target_pairs={{0,52},{1,53},{2,54},{3,55},{4,48},{5,49},{6,50},{7,51},{8,60},{9,... | collective-permute-start | bytes 36872 | tf_op jit(solution)/shard_map/ppermute | solution.py:492
  35.0 1.5 %collective-permute-done.7.other_ref = f32[24,128]{1,0:T(8,128)S(1)} collective-permute-done((f32[24,128]{1,0:T(8,128)S(1)}, f32[24,128]{1,0:T(8,128)S(1)}, u32[]{:S(2)}, u32[]{:S(2)}) %collective-permute-start.7) | collective-permute-done | bytes 12320 | tf_op jit(solution)/shard_map/ppermute | solution.py:492
  36.4 0.7 %shard_map.69 = f32[16,24,128]{2,1,0:T(8,128)} custom-call(f32[24,128]{1,0:T(8,128)S(1)} %add.11.part_ref, f32[24,128]{1,0:T(8,128)S(1)} %collective-permute-done.7.other_ref), custom_call_target="tpu_custom_call" | custom-call | bytes 2097152 | tf_op jit(solution)/shard_map/pallas_call | solution.py:496
  37.1 7.4 %all-to-all-start = ((f32[16,24,128]{2,1,0:T(8,128)}), f32[16,24,128]{2,1,0:T(8,128)S(1)}, u32[]{:S(2)}, u32[]{:S(2)}) async-start(f32[16,24,128]{2,1,0:T(8,128)} %shard_map.69), calls=%async_computation | async-start | bytes 393216 | tf_op jit(solution)/shard_map/all_to_all | solution.py:497
  44.6 0.3 shard_map.70
  44.9 6.9 %all-to-all-done.parts_ref = f32[16,24,128]{2,1,0:T(8,128)S(1)} async-done(((f32[16,24,128]{2,1,0:T(8,128)}), f32[16,24,128]{2,1,0:T(8,128)S(1)}, u32[]{:S(2)}, u32[]{:S(2)}) %all-to-all-start) | async-done | bytes 196640 | tf_op jit(solution)/shard_map/all_to_all | solution.py:497
  51.8 3.4 %shard_map.71 = f32[1536,128]{1,0:T(8,128)} custom-call(f32[16,24,128]{2,1,0:T(8,128)S(1)} %all-to-all-done.parts_ref, bf16[3,8,64,128]{3,2,1,0:T(8,128)(2,1)S(1)} %get-tuple-element.48.big_ref, bf16[3,8,64,128]{3,2,1,0:T(8,128)(2,1)S(1)} %get-tuple-element.49.small_ref, f32[24,128]{1,0:T(8,128)S(1)} %get-tuple-element.50.mean_ref), custom_call_target="tpu_custom_call" | custom-call | bytes 2097152 | tf_op jit(solution)/shard_map/pallas_call | solution.py:578
  (3 shorter events, 0.0 us)
Async XLA Ops:
  1.3 7.4 %collective-permute-start = (f32[584,128]{1,0:T(8,128)S(1)}, f32[584,128]{1,0:T(8,128)S(1)}, u32[]{:S(2)}, u32[]{:S(2)}) collective-permute-start(f32[584,128]{1,0:T(8,128)S(1)} %get-tuple-element.28), channel_id=1, source_target_pairs={{0,4},{8,12},{16,20},{24,28},{32,36},{40,44},{48,52},{56,60},{64,6... | collective-permute-start | bytes 897032 | tf_op jit(solution)/shard_map/ppermute | solution.py:475
  4.5 8.4 %collective-permute-start.1 = (f32[584,128]{1,0:T(8,128)S(1)}, f32[584,128]{1,0:T(8,128)S(1)}, u32[]{:S(2)}, u32[]{:S(2)}) collective-permute-start(f32[584,128]{1,0:T(8,128)S(1)} %get-tuple-element.29), channel_id=1, source_target_pairs={{4,8},{12,16},{20,24},{28,32},{36,40},{44,48},{52,56},{60,64},{68,... | collective-permute-start | bytes 897032 | tf_op jit(solution)/shard_map/ppermute | solution.py:475
  13.5 3.5 %collective-permute-start.2 = (f32[9,8,128]{2,1,0:T(8,128)S(1)}, f32[9,8,128]{2,1,0:T(8,128)S(1)}, u32[]{:S(2)}, u32[]{:S(2)}) collective-permute-start(f32[9,8,128]{2,1,0:T(8,128)S(1)} %get-tuple-element.36), channel_id=1, source_target_pairs={{0,1},{2,3},{1,0},{3,2},{4,5},{6,7},{5,4},{7,6},{8,9},{10,11},{9,8... | collective-permute-start | bytes 110600 | tf_op jit(solution)/shard_map/ppermute | solution.py:475
  13.5 4.1 %collective-permute-start.3 = (f32[9,8,128]{2,1,0:T(8,128)S(1)}, f32[9,8,128]{2,1,0:T(8,128)S(1)}, u32[]{:S(2)}, u32[]{:S(2)}) collective-permute-start(f32[9,8,128]{2,1,0:T(8,128)S(1)} %get-tuple-element.37), channel_id=1, source_target_pairs={{1,2},{3,0},{2,1},{0,3},{5,6},{7,4},{6,5},{4,7},{9,10},{11,8},{10,... | collective-permute-start | bytes 110600 | tf_op jit(solution)/shard_map/ppermute | solution.py:475
  19.9 1.2 %collective-permute-start.4 = (f32[24,128]{1,0:T(8,128)S(1)}, f32[24,128]{1,0:T(8,128)S(1)}, u32[]{:S(2)}, u32[]{:S(2)}) collective-permute-start(f32[24,128]{1,0:T(8,128)S(1)} %get-tuple-element.46), channel_id=1, source_target_pairs={{0,4},{1,5},{2,6},{3,7},{4,0},{5,1},{6,2},{7,3},{8,12},{9,13},{10,... | collective-permute-start | bytes 36872 | tf_op jit(solution)/shard_map/ppermute | solution.py:492
  21.1 3.5 %collective-permute-start.5 = (f32[24,128]{1,0:T(8,128)S(1)}, f32[24,128]{1,0:T(8,128)S(1)}, u32[]{:S(2)}, u32[]{:S(2)}) collective-permute-start(f32[24,128]{1,0:T(8,128)S(1)} %add.9), channel_id=1, source_target_pairs={{0,12},{1,13},{2,14},{3,15},{4,8},{5,9},{6,10},{7,11},{8,4},{9,5},... | collective-permute-start | bytes 36872 | tf_op jit(solution)/shard_map/ppermute | solution.py:492
  24.6 4.7 %collective-permute-start.6 = (f32[24,128]{1,0:T(8,128)S(1)}, f32[24,128]{1,0:T(8,128)S(1)}, u32[]{:S(2)}, u32[]{:S(2)}) collective-permute-start(f32[24,128]{1,0:T(8,128)S(1)} %add.10), channel_id=1, source_target_pairs={{0,20},{1,21},{2,22},{3,23},{4,16},{5,17},{6,18},{7,19},{8,28},{9,... | collective-permute-start | bytes 36872 | tf_op jit(solution)/shard_map/ppermute | solution.py:492
  29.3 7.1 %collective-permute-start.7 = (f32[24,128]{1,0:T(8,128)S(1)}, f32[24,128]{1,0:T(8,128)S(1)}, u32[]{:S(2)}, u32[]{:S(2)}) collective-permute-start(f32[24,128]{1,0:T(8,128)S(1)} %add.11.part_ref), channel_id=1, source_target_pairs={{0,52},{1,53},{2,54},{3,55},{4,48},{5,49},{6,50},{7,51},{8,60},{9,... | collective-permute-start | bytes 36872 | tf_op jit(solution)/shard_map/ppermute | solution.py:492
  37.1 14.6 %all-to-all-start = ((f32[16,24,128]{2,1,0:T(8,128)}), f32[16,24,128]{2,1,0:T(8,128)S(1)}, u32[]{:S(2)}, u32[]{:S(2)}) async-start(f32[16,24,128]{2,1,0:T(8,128)} %shard_map.69), calls=%async_computation | async-start | bytes 393216 | tf_op jit(solution)/shard_map/all_to_all | solution.py:497

commit v7 on v6

--- a/solution.py
+++ b/solution.py
@@ -418,23 +418,31 @@
     for b in range(BLOCKS):
         rows = [spread(table[b][s : s + 1, :]) for s in range(8)]
         entry = {(s, t): column_of(rows[s], 8 * b + t) for s in range(8) for t in range(s, 8)}
-        over = []
-        for s in range(8):
-            over.append(1.0 / entry[s, s])
-            for t in range(s + 1, 8):
-                factor = entry[s, t] * over[s]
-                for q in range(t, 8):
-                    entry[t, q] = entry[t, q] - factor * entry[s, q]
-                rows[t] = rows[t] - factor * rows[s]
+        over = {}
+        for s in range(0, 8, 2):
+            p, q, r = entry[s, s], entry[s, s + 1], entry[s + 1, s + 1]
+            over[s] = 1.0 / (p * r - q * q)
+            for t in range(s + 2, 8):
+                one = (r * entry[s, t] - q * entry[s + 1, t]) * over[s]
+                two = (p * entry[s + 1, t] - q * entry[s, t]) * over[s]
+                for k in range(t, 8):
+                    entry[t, k] = entry[t, k] - (one * entry[s, k] + two * entry[s + 1, k])
+                rows[t] = rows[t] - (one * rows[s] + two * rows[s + 1])
         for i in range(b + 1, BLOCKS):
             column = [column_of(table[i], 8 * b + s) for s in range(8)]
-            for s in range(8):
-                column[s] = column[s] * over[s]
-                for t in range(s + 1, 8):
-                    column[t] = column[t] - column[s] * entry[s, t]
-                table[i] = table[i] - column[s] * rows[s]
-        for s in range(8):
-            table[b] = jnp.where(sub == s, rows[s] * lax.rsqrt(entry[s, s]), table[b])
+            for s in range(0, 8, 2):
+                p, q, r = entry[s, s], entry[s, s + 1], entry[s + 1, s + 1]
+                one = (r * column[s] - q * column[s + 1]) * over[s]
+                two = (p * column[s + 1] - q * column[s]) * over[s]
+                for t in range(s + 2, 8):
+                    column[t] = column[t] - (one * entry[s, t] + two * entry[s + 1, t])
+                table[i] = table[i] - (one * rows[s] + two * rows[s + 1])
+        for s in range(0, 8, 2):
+            p, q, r = entry[s, s], entry[s, s + 1], entry[s + 1, s + 1]
+            inverse = 1.0 / p
+            last = (rows[s + 1] - (q * inverse) * rows[s]) * lax.rsqrt((p * r - q * q) * inverse)
+            table[b] = jnp.where(sub == s, rows[s] * lax.rsqrt(p), table[b])
+            table[b] = jnp.where(sub == s + 1, last, table[b])
     return [jnp.where(lane < MEMBERS, turn(value, MEMBERS), 0.0) for value in table]
 
 
@@ -487,10 +495,10 @@
 
 def gathered(part):
     gx, gy = lax.axis_size("gx"), lax.axis_size("gy")
-    for flip in (1, 3, 5, 13):
+    for flip in (1, 13, 5, 3):
         pairs = [(i * gy + j, (i ^ flip) * gy + j) for i in range(gx) for j in range(gy)]
         other = lax.ppermute(part, ("gx", "gy"), pairs)
-        if flip < 13:
+        if flip != 3:
             part = part + other
     groups = [[(y * 16 + i) * gy + x for y in range(gx // 16) for x in range(gy)] for i in range(16)]
     (copies,) = call(duplicate, (shape(len(groups[0]), *part.shape),), vmem(2))(part, other)

time: 55.4 us -> 55.2 us (level)
  no operation moved by 1% of the time
where the time goes in v7:
time: 55.2 us; the launch traced here: 54.9 us
  starting transfers between devices  24.8 us (45%)
  waiting for transfers between devices  17.3 us (31%)
  Pallas kernels  12.8 us (23%)
    ppermute x4, starting transfers between devices, gathered(): other = lax.ppermute(part, ('gx', 'gy'), pairs)  10.9 us
    all_to_all x1, starting transfers between devices, gathered(): return lax.all_to_all(copies, ('gx', 'gy'), 0, 0, axis_index_groups=groups)  7.44 us
    all_to_all x1, waiting for transfers between devices, gathered(): return lax.all_to_all(copies, ('gx', 'gy'), 0, 0, axis_index_groups=groups)  6.88 us
    ppermute x4, starting transfers between devices, swap(): lax.ppermute(value, axis, [(a, b) for a, b in pairs] + [(b, a) for a, b i...  6.42 us
    ppermute x4, waiting for transfers between devices, gathered(): other = lax.ppermute(part, ('gx', 'gy'), pairs)  5.48 us
    ppermute x4, waiting for transfers between devices, swap(): lax.ppermute(value, axis, [(a, b) for a, b in pairs] + [(b, a) for a, b i...  4.9 us
    pallas_call x1, Pallas kernels, local(): call(analyse, (shape(*x.shape),), vmem(4), [pltpu.VMEM(x.shape, F32), plt...  3.23 us
    pallas_call x1, Pallas kernels, local(): call(outer, (outside, jax.ShapeDtypeStruct((2, 8, OBS), jnp.int32), shape...  2.3 us
  transfers between devices with their start and end apart: 9, of which 7 were waited for; matrix products, arithmetic and copies ran while one was open for 0% of the time, Pallas kernels for 9%

profile of v7, /device:TPU:1, one launch (start us, length us, event | category | flops | bytes accessed | tf_op | source)
XLA Modules:
  0.0 54.9 jit_solution(1832675921529566187)
XLA Ops:
  0.0 1.2 %shard_map.64 = (f32[3,8,64,128]{3,2,1,0:T(8,128)S(1)}, f32[2,8,128]{2,1,0:T(8,128)S(1)}, f32[584,128]{1,0:T(8,128)S(1)}, f32[584,128]{1,0:T(8,128)S(1)}) custom-call(f32[1536,128]{1,0:T(8,128)} %bitcast.5, s32[8,128]{1,0:T(8,128)} %depth_hbm.1, s32[8,128]{1,0:T(8,128)} %land_hbm.1), custom_call_target="tpu_custom_call" | custom-call | bytes 2097152 | tf_op jit(solution)/shard_map/pallas_call | solution.py:532
  1.3 3.3 %collective-permute-start = (f32[584,128]{1,0:T(8,128)S(1)}, f32[584,128]{1,0:T(8,128)S(1)}, u32[]{:S(2)}, u32[]{:S(2)}) collective-permute-start(f32[584,128]{1,0:T(8,128)S(1)} %get-tuple-element.28), channel_id=1, source_target_pairs={{0,4},{8,12},{16,20},{24,28},{32,36},{40,44},{48,52},{56,60},{64,6... | collective-permute-start | bytes 897032 | tf_op jit(solution)/shard_map/ppermute | solution.py:483
  4.5 1.9 %collective-permute-start.1 = (f32[584,128]{1,0:T(8,128)S(1)}, f32[584,128]{1,0:T(8,128)S(1)}, u32[]{:S(2)}, u32[]{:S(2)}) collective-permute-start(f32[584,128]{1,0:T(8,128)S(1)} %get-tuple-element.29), channel_id=1, source_target_pairs={{4,8},{12,16},{20,24},{28,32},{36,40},{44,48},{52,56},{60,64},{68,... | collective-permute-start | bytes 897032 | tf_op jit(solution)/shard_map/ppermute | solution.py:483
  6.5 2.1 %shard_map.65 = (f32[26,8,128]{2,1,0:T(8,128)S(1)}, f32[26,8,128]{2,1,0:T(8,128)S(1)}, f32[3,6,64,128]{3,2,1,0:T(8,128)S(1)}, f32[3,4,64,128]{3,2,1,0:T(8,128)S(1)}, f32[3,2,64,128]{3,2,1,0:T(8,128)S(1)}) custom-call(f32[3,8,64,128]{3,2,1,0:T(8,128)S(1)} %get-tuple-element.31.start_ref, f32[2,8,128]{2,1,0:T(8,128)S(1)} %get-tuple-element.30.geo_ref), custom_call_target="tpu_custom_call" | custom-call | bytes 8388608 | tf_op jit(solution)/shard_map/pallas_call | solution.py:544
  8.6 0.0 collective-permute-done.near_ref
  8.6 4.3 %collective-permute-done.1.far_ref = f32[584,128]{1,0:T(8,128)S(1)} collective-permute-done((f32[584,128]{1,0:T(8,128)S(1)}, f32[584,128]{1,0:T(8,128)S(1)}, u32[]{:S(2)}, u32[]{:S(2)}) %collective-permute-start.1) | collective-permute-done | bytes 299040 | tf_op jit(solution)/shard_map/ppermute | solution.py:483
  12.9 0.6 %shard_map.66 = (f32[3,6,64,128]{3,2,1,0:T(8,128)S(1)}, f32[2,14,128]{2,1,0:T(8,128)S(1)}, f32[26,8,128]{2,1,0:T(8,128)S(1)}, f32[26,8,128]{2,1,0:T(8,128)S(1)},...) custom-call(f32[584,128]{1,0:T(8,128)S(1)} %collective-permute-done.near_ref, ...), custom_call_target="tpu_custom_call" | custom-call | bytes 2097152 | tf_op jit(solution)/shard_map/pallas_call | solution.py:553
  13.5 0.0 collective-permute-start.2
  13.5 1.2 %collective-permute-start.3 = (f32[9,8,128]{2,1,0:T(8,128)S(1)}, f32[9,8,128]{2,1,0:T(8,128)S(1)}, u32[]{:S(2)}, u32[]{:S(2)}) collective-permute-start(f32[9,8,128]{2,1,0:T(8,128)S(1)} %get-tuple-element.37), channel_id=1, source_target_pairs={{1,2},{3,0},{2,1},{0,3},{5,6},{7,4},{6,5},{4,7},{9,10},{11,8},{10,... | collective-permute-start | bytes 110600 | tf_op jit(solution)/shard_map/ppermute | solution.py:483
  14.7 2.3 %shard_map.67 = (f32[3,6,64,128]{3,2,1,0:T(8,128)S(1)}, s32[2,8,256]{2,1,0:T(8,128)S(1)}, f32[8,256]{1,0:T(8,128)S(1)}) custom-call(f32[3,8,64,128]{3,2,1,0:T(8,128)S(1)} %get-tuple-element.31.start_ref, f32[3,6,64,128]{3,2,1,0:T(8,128)S(1)} %get-tuple-element.39.halo_ref, f32[2,14,128]{2,1,0:T(8,128)S(1)} %get-tuple-element.40.wide_ref, ...), custom_call_target="tpu_custom_call" | custom-call | bytes 6291456 | tf_op jit(solution)/shard_map/pallas_call | solution.py:560
  17.0 0.0 collective-permute-done.2.a_ref
  17.1 0.6 %collective-permute-done.3.b_ref = f32[9,8,128]{2,1,0:T(8,128)S(1)} collective-permute-done((f32[9,8,128]{2,1,0:T(8,128)S(1)}, f32[9,8,128]{2,1,0:T(8,128)S(1)}, u32[]{:S(2)}, u32[]{:S(2)}) %collective-permute-start.3) | collective-permute-done | bytes 36896 | tf_op jit(solution)/shard_map/ppermute | solution.py:483
  17.7 2.3 %shard_map.68 = (f32[3,8,8,128]{3,2,1,0:T(8,128)S(1)}, f32[24,128]{1,0:T(8,128)S(1)}) custom-call(f32[26,8,128]{2,1,0:T(8,128)S(1)} %get-tuple-element.34.left_ref, f32[26,8,128]{2,1,0:T(8,128)S(1)} %get-tuple-element.35.right_ref, f32[9,8,128]{2,1,0:T(8,128)S(1)} %collective-permute-done.2.a_ref, f32[9,8,128]{2,1,0:T(8,128)S(1)} %collective-permute-done.3.b_ref, ...), custom_call_target="tpu_custom_call" | custom-call | bytes 2097152 | tf_op jit(solution)/shard_map/pallas_call | solution.py:576
  19.9 0.0 collective-permute-start.4
  20.0 1.2 %collective-permute-done.4 = f32[24,128]{1,0:T(8,128)S(1)} collective-permute-done((f32[24,128]{1,0:T(8,128)S(1)}, f32[24,128]{1,0:T(8,128)S(1)}, u32[]{:S(2)}, u32[]{:S(2)}) %collective-permute-start.4) | collective-permute-done | bytes 12320 | tf_op jit(solution)/shard_map/ppermute | solution.py:500
  21.1 6.5 %collective-permute-start.5 = (f32[24,128]{1,0:T(8,128)S(1)}, f32[24,128]{1,0:T(8,128)S(1)}, u32[]{:S(2)}, u32[]{:S(2)}) collective-permute-start(f32[24,128]{1,0:T(8,128)S(1)} %add.9), channel_id=1, source_target_pairs={{0,52},{1,53},{2,54},{3,55},{4,48},{5,49},{6,50},{7,51},{8,60},{9,... | collective-permute-start | bytes 36872 | tf_op jit(solution)/shard_map/ppermute | solution.py:500
  27.6 1.4 %collective-permute-done.5 = f32[24,128]{1,0:T(8,128)S(1)} collective-permute-done((f32[24,128]{1,0:T(8,128)S(1)}, f32[24,128]{1,0:T(8,128)S(1)}, u32[]{:S(2)}, u32[]{:S(2)}) %collective-permute-start.5) | collective-permute-done | bytes 12320 | tf_op jit(solution)/shard_map/ppermute | solution.py:500
  29.0 2.5 %collective-permute-start.6 = (f32[24,128]{1,0:T(8,128)S(1)}, f32[24,128]{1,0:T(8,128)S(1)}, u32[]{:S(2)}, u32[]{:S(2)}) collective-permute-start(f32[24,128]{1,0:T(8,128)S(1)} %add.10), channel_id=1, source_target_pairs={{0,20},{1,21},{2,22},{3,23},{4,16},{5,17},{6,18},{7,19},{8,28},{9,... | collective-permute-start | bytes 36872 | tf_op jit(solution)/shard_map/ppermute | solution.py:500
  31.5 1.6 %collective-permute-done.6 = f32[24,128]{1,0:T(8,128)S(1)} collective-permute-done((f32[24,128]{1,0:T(8,128)S(1)}, f32[24,128]{1,0:T(8,128)S(1)}, u32[]{:S(2)}, u32[]{:S(2)}) %collective-permute-start.6) | collective-permute-done | bytes 12320 | tf_op jit(solution)/shard_map/ppermute | solution.py:500
  33.0 1.9 %collective-permute-start.7 = (f32[24,128]{1,0:T(8,128)S(1)}, f32[24,128]{1,0:T(8,128)S(1)}, u32[]{:S(2)}, u32[]{:S(2)}) collective-permute-start(f32[24,128]{1,0:T(8,128)S(1)} %add.11.part_ref), channel_id=1, source_target_pairs={{0,12},{1,13},{2,14},{3,15},{4,8},{5,9},{6,10},{7,11},{8,4},{9,5},... | collective-permute-start | bytes 36872 | tf_op jit(solution)/shard_map/ppermute | solution.py:500
  35.0 1.4 %collective-permute-done.7.other_ref = f32[24,128]{1,0:T(8,128)S(1)} collective-permute-done((f32[24,128]{1,0:T(8,128)S(1)}, f32[24,128]{1,0:T(8,128)S(1)}, u32[]{:S(2)}, u32[]{:S(2)}) %collective-permute-start.7) | collective-permute-done | bytes 12320 | tf_op jit(solution)/shard_map/ppermute | solution.py:500
  36.3 0.7 %shard_map.69 = f32[16,24,128]{2,1,0:T(8,128)} custom-call(f32[24,128]{1,0:T(8,128)S(1)} %add.11.part_ref, f32[24,128]{1,0:T(8,128)S(1)} %collective-permute-done.7.other_ref), custom_call_target="tpu_custom_call" | custom-call | bytes 2097152 | tf_op jit(solution)/shard_map/pallas_call | solution.py:504
  37.0 7.4 %all-to-all-start = ((f32[16,24,128]{2,1,0:T(8,128)}), f32[16,24,128]{2,1,0:T(8,128)S(1)}, u32[]{:S(2)}, u32[]{:S(2)}) async-start(f32[16,24,128]{2,1,0:T(8,128)} %shard_map.69), calls=%async_computation | async-start | bytes 393216 | tf_op jit(solution)/shard_map/all_to_all | solution.py:505
  44.5 0.3 shard_map.70
  44.8 6.9 %all-to-all-done.parts_ref = f32[16,24,128]{2,1,0:T(8,128)S(1)} async-done(((f32[16,24,128]{2,1,0:T(8,128)}), f32[16,24,128]{2,1,0:T(8,128)S(1)}, u32[]{:S(2)}, u32[]{:S(2)}) %all-to-all-start) | async-done | bytes 196640 | tf_op jit(solution)/shard_map/all_to_all | solution.py:505
  51.7 3.2 %shard_map.71 = f32[1536,128]{1,0:T(8,128)} custom-call(f32[16,24,128]{2,1,0:T(8,128)S(1)} %all-to-all-done.parts_ref, bf16[3,8,64,128]{3,2,1,0:T(8,128)(2,1)S(1)} %get-tuple-element.48.big_ref, bf16[3,8,64,128]{3,2,1,0:T(8,128)(2,1)S(1)} %get-tuple-element.49.small_ref, f32[24,128]{1,0:T(8,128)S(1)} %get-tuple-element.50.mean_ref), custom_call_target="tpu_custom_call" | custom-call | bytes 2097152 | tf_op jit(solution)/shard_map/pallas_call | solution.py:586
  (3 shorter events, 0.0 us)
Async XLA Ops:
  1.3 7.4 %collective-permute-start = (f32[584,128]{1,0:T(8,128)S(1)}, f32[584,128]{1,0:T(8,128)S(1)}, u32[]{:S(2)}, u32[]{:S(2)}) collective-permute-start(f32[584,128]{1,0:T(8,128)S(1)} %get-tuple-element.28), channel_id=1, source_target_pairs={{0,4},{8,12},{16,20},{24,28},{32,36},{40,44},{48,52},{56,60},{64,6... | collective-permute-start | bytes 897032 | tf_op jit(solution)/shard_map/ppermute | solution.py:483
  4.5 8.4 %collective-permute-start.1 = (f32[584,128]{1,0:T(8,128)S(1)}, f32[584,128]{1,0:T(8,128)S(1)}, u32[]{:S(2)}, u32[]{:S(2)}) collective-permute-start(f32[584,128]{1,0:T(8,128)S(1)} %get-tuple-element.29), channel_id=1, source_target_pairs={{4,8},{12,16},{20,24},{28,32},{36,40},{44,48},{52,56},{60,64},{68,... | collective-permute-start | bytes 897032 | tf_op jit(solution)/shard_map/ppermute | solution.py:483
  13.5 3.5 %collective-permute-start.2 = (f32[9,8,128]{2,1,0:T(8,128)S(1)}, f32[9,8,128]{2,1,0:T(8,128)S(1)}, u32[]{:S(2)}, u32[]{:S(2)}) collective-permute-start(f32[9,8,128]{2,1,0:T(8,128)S(1)} %get-tuple-element.36), channel_id=1, source_target_pairs={{0,1},{2,3},{1,0},{3,2},{4,5},{6,7},{5,4},{7,6},{8,9},{10,11},{9,8... | collective-permute-start | bytes 110600 | tf_op jit(solution)/shard_map/ppermute | solution.py:483
  13.5 4.1 %collective-permute-start.3 = (f32[9,8,128]{2,1,0:T(8,128)S(1)}, f32[9,8,128]{2,1,0:T(8,128)S(1)}, u32[]{:S(2)}, u32[]{:S(2)}) collective-permute-start(f32[9,8,128]{2,1,0:T(8,128)S(1)} %get-tuple-element.37), channel_id=1, source_target_pairs={{1,2},{3,0},{2,1},{0,3},{5,6},{7,4},{6,5},{4,7},{9,10},{11,8},{10,... | collective-permute-start | bytes 110600 | tf_op jit(solution)/shard_map/ppermute | solution.py:483
  19.9 1.2 %collective-permute-start.4 = (f32[24,128]{1,0:T(8,128)S(1)}, f32[24,128]{1,0:T(8,128)S(1)}, u32[]{:S(2)}, u32[]{:S(2)}) collective-permute-start(f32[24,128]{1,0:T(8,128)S(1)} %get-tuple-element.46), channel_id=1, source_target_pairs={{0,4},{1,5},{2,6},{3,7},{4,0},{5,1},{6,2},{7,3},{8,12},{9,13},{10,... | collective-permute-start | bytes 36872 | tf_op jit(solution)/shard_map/ppermute | solution.py:500
  21.1 7.8 %collective-permute-start.5 = (f32[24,128]{1,0:T(8,128)S(1)}, f32[24,128]{1,0:T(8,128)S(1)}, u32[]{:S(2)}, u32[]{:S(2)}) collective-permute-start(f32[24,128]{1,0:T(8,128)S(1)} %add.9), channel_id=1, source_target_pairs={{0,52},{1,53},{2,54},{3,55},{4,48},{5,49},{6,50},{7,51},{8,60},{9,... | collective-permute-start | bytes 36872 | tf_op jit(solution)/shard_map/ppermute | solution.py:500
  29.0 4.0 %collective-permute-start.6 = (f32[24,128]{1,0:T(8,128)S(1)}, f32[24,128]{1,0:T(8,128)S(1)}, u32[]{:S(2)}, u32[]{:S(2)}) collective-permute-start(f32[24,128]{1,0:T(8,128)S(1)} %add.10), channel_id=1, source_target_pairs={{0,20},{1,21},{2,22},{3,23},{4,16},{5,17},{6,18},{7,19},{8,28},{9,... | collective-permute-start | bytes 36872 | tf_op jit(solution)/shard_map/ppermute | solution.py:500
  33.0 3.3 %collective-permute-start.7 = (f32[24,128]{1,0:T(8,128)S(1)}, f32[24,128]{1,0:T(8,128)S(1)}, u32[]{:S(2)}, u32[]{:S(2)}) collective-permute-start(f32[24,128]{1,0:T(8,128)S(1)} %add.11.part_ref), channel_id=1, source_target_pairs={{0,12},{1,13},{2,14},{3,15},{4,8},{5,9},{6,10},{7,11},{8,4},{9,5},... | collective-permute-start | bytes 36872 | tf_op jit(solution)/shard_map/ppermute | solution.py:500
  37.0 14.6 %all-to-all-start = ((f32[16,24,128]{2,1,0:T(8,128)}), f32[16,24,128]{2,1,0:T(8,128)S(1)}, u32[]{:S(2)}, u32[]{:S(2)}) async-start(f32[16,24,128]{2,1,0:T(8,128)} %shard_map.69), calls=%async_computation | async-start | bytes 393216 | tf_op jit(solution)/shard_map/all_to_all | solution.py:505
